TPU v7x, 256 devices: a whole 4x4x8 slice. The times are simulated.
256 devices in a mesh: kv: 8 (over y, x_hi), sp: 32 (over z, x_lo, core).
Axes of the slice: x: 4 (x_hi: 2, x_lo: 2; x = x_hi * 2 + x_lo), y: 4, z: 8, core: 2. Of those that a mesh axis runs over, the one named last changes fastest.
Arguments:
- queries: bfloat16 [4096, 4096], P('sp'), may hold values from -1.1953125 to 1.1953125
- keys: bfloat16 [16384, 4096], P(('kv', 'sp')), may hold values from -1.1953125 to 1.1953125
- values: bfloat16 [16384, 4096], P(('kv', 'sp')), may hold values from -6 to 6
- outputs: bfloat16 [4096, 4096], P('sp'), may hold values from -6 to 6
- out_grad: bfloat16 [4096, 4096], P('sp'), may hold values from -1536 to 1536
- stats: float32 [4096, 32], P('sp'), may hold values from -1 to 1
Outputs:
- query_grad: float32 [4096, 4096], P(('kv', 'sp'))
- key_grad: float32 [16384, 4096], P(('kv', 'sp'))
- value_grad: float32 [16384, 4096], P(('kv', 'sp'))
All inputs are finite; a program needn't handle non-finite values.
Results may differ from a plain program's by a relative error of at most 0.0029.
Values may be sent and summed in bfloat16 or wider, within the bound.
No kernel may reach another device: no remote copies, remote signals or barrier semaphores. Data moves between devices by JAX's collectives and lax.ppermute only.
A program may use at most 64 MiB of HBM per device.

v0:
```python
import functools
import math

import jax
import jax.numpy as jnp
from jax import lax
from jax.experimental import pallas as pl
from jax.experimental.pallas import tpu as pltpu
from jax.sharding import Mesh
from jax.sharding import PartitionSpec as P


H = 32
DH = 128
QLEN = 4096
KLEN = 2048
NY, NX, NZ = 4, 2, 8
NKV = NY * NX
SP = ("z", "xl", "c")
ALL = ("y", "xh", "z", "xl", "c")
NSP = 32
ROWS = QLEN // NSP
SHARE = ROWS // NY
GROUP = DH // SHARE
WIDE = 2 * SHARE + 8
KROWS = KLEN // NSP
QB = QLEN // NKV
QROWS = QB // NSP
LOG2E = math.log2(math.e)
ROOT = 1.0 / math.sqrt(DH)
SCALE = 1.0 / (KLEN * NKV)
F32 = jnp.float32
BF16 = jnp.bfloat16


def dot(a, b, dims):
    return lax.dot_general(a, b, ((dims[0], dims[1]), ((), ())), preferred_element_type=F32)


def cost(flops, size, trans=0):
    return pl.CostEstimate(flops=flops, bytes_accessed=size, transcendentals=trans)


def three(x):
    hi = x.astype(BF16).astype(F32)
    mid = (x - hi).astype(BF16).astype(F32)
    return hi, mid, x - hi - mid


def pack_queries(y_ref, group_ref, q_ref, g_ref, o_ref, s_ref, out_ref):
    cols = []
    for h in range(H):
        c = slice(h * DH, (h + 1) * DH)
        out_ref[h, 0:SHARE, :] = q_ref[:, c]
        out_ref[h, SHARE : 2 * SHARE, :] = g_ref[:, c]
        prod = g_ref[:, c].astype(F32) * o_ref[:, c].astype(F32)
        cols.append(jnp.sum(prod, axis=1, keepdims=True))
    delta = jnp.transpose(jnp.concatenate(cols, axis=1))
    stats = s_ref[:, 0:SHARE]
    for b in range(1, NY):
        stats = jnp.where(y_ref[0] == b, s_ref[:, b * SHARE : (b + 1) * SHARE], stats)
    lane = lax.broadcasted_iota(jnp.int32, (H, DH), 1)
    here = lane // SHARE == group_ref[0]
    row = lax.broadcasted_iota(jnp.int32, (H, 8, DH), 1)
    tile = jnp.zeros((H, 8, DH), F32)
    for r, x in enumerate(three(stats * LOG2E) + three(delta)):
        x = jnp.where(here, jnp.concatenate([x] * GROUP, axis=1), 0.0)
        tile = jnp.where(row == r, x[:, None, :], tile)
    out_ref[:, 2 * SHARE : WIDE, :] = tile.astype(BF16)


def packed_queries(y, group, queries, out_grad, outputs, stats):
    wide = pl.BlockSpec((SHARE, H * DH), lambda i, y, g: (y[0], 0))
    return pl.pallas_call(
        pack_queries,
        grid_spec=pltpu.PrefetchScalarGridSpec(
            num_scalar_prefetch=2,
            grid=(1,),
            in_specs=[wide, wide, wide, pl.BlockSpec((H, ROWS), lambda i, y, g: (0, 0))],
            out_specs=pl.BlockSpec((H, WIDE, DH), lambda i, y, g: (0, 0, 0)),
        ),
        out_shape=jax.ShapeDtypeStruct((H, WIDE, DH), BF16),
        cost_estimate=cost(10**6, 2 * 10**6),
        name="pack_queries",
    )(y, group, queries, out_grad, outputs, jnp.transpose(stats))


def pack_keys(k_ref, v_ref, out_ref):
    for h in range(H):
        c = slice(h * DH, (h + 1) * DH)
        out_ref[h, 0:KROWS, :] = k_ref[:, c]
        out_ref[h, KROWS : 2 * KROWS, :] = v_ref[:, c]


def packed_keys(keys, values):
    return pl.pallas_call(
        pack_keys,
        out_shape=jax.ShapeDtypeStruct((H, 2 * KROWS, DH), BF16),
        cost_estimate=cost(10**6, 2 * 10**6),
        name="pack_keys",
    )(keys, values)


def queries_of(parts):
    q = jnp.concatenate([p[:, 0:SHARE, :].reshape(-1, DH) for p in parts], axis=0)
    g = jnp.concatenate([p[:, SHARE : 2 * SHARE, :].reshape(-1, DH) for p in parts], axis=0)
    st, de = [], []
    for p in parts:
        x = jnp.sum(p[:, 2 * SHARE : WIDE, :].astype(F32), axis=0)
        st.append(x[0:1] + x[1:2] + x[2:3])
        de.append(x[3:4] + x[4:5] + x[5:6])
    return q, g, jnp.concatenate(st, axis=1), jnp.concatenate(de, axis=1)


def block_grads(parts, kv_ref, dk_ref, dv_ref, per):
    q, g, st, de = queries_of(parts)
    bk = per * KROWS
    total = None
    for j in range(NSP // per):
        k = kv_ref[j * per : (j + 1) * per, 0:KROWS, :].reshape(bk, DH)
        v = kv_ref[j * per : (j + 1) * per, KROWS : 2 * KROWS, :].reshape(bk, DH)
        at = slice(j * bk, (j + 1) * bk)
        p = jnp.exp2(dot(k, q, ((1,), (1,))) * (ROOT * LOG2E) - st)
        ds = (p * (dot(v, g, ((1,), (1,))) - de)).astype(BF16)
        dv_ref[at, :] += dot(p.astype(BF16), g, ((1,), (0,)))
        dk_ref[at, :] += dot(ds, q, ((1,), (0,)))
        part = dot(ds, k, ((0,), (0,)))
        total = part if total is None else total + part
    return total.reshape(NY, GROUP, SHARE, DH)


def grads(count, first, last, tab, *refs):
    parts = refs[:NY]
    kv_ref = refs[NY]
    rest = refs[NY + 1 :]
    if not first:
        dk_in, dv_in = rest[:2]
        rest = rest[2:]
    dq_refs = rest[:count]
    dk_ref, dv_ref = rest[-2:]
    step = pl.program_id(0)

    @pl.when(step == 0)
    def _():
        dk_ref[...] = jnp.zeros_like(dk_ref) if first else dk_in[...]
        dv_ref[...] = jnp.zeros_like(dv_ref) if first else dv_in[...]

    total = block_grads(parts, kv_ref, dk_ref, dv_ref, 8)
    for n, dq_ref in enumerate(dq_refs):

        @pl.when(step // NX == n)
        def _(dq_ref=dq_ref):
            for b in range(NY):
                dq_ref[0, :, tab[NX * count + b], :, :] = total[b].astype(dq_ref.dtype)

    if last:
        out_ref = rest[count]

        @pl.when(step == NX * count - 1)
        def _():
            dk = (dk_ref[...] * (ROOT * SCALE)).astype(BF16)
            dv = (dv_ref[...] * SCALE).astype(BF16)
            out_ref[:, 0:KROWS, :] = dk.reshape(NSP, KROWS, DH)
            out_ref[:, KROWS : 2 * KROWS, :] = dv.reshape(NSP, KROWS, DH)


DQ = (GROUP, NY, SHARE, DH)
OUT_ROWS = 2 * KROWS + QROWS


def grads_call(count, first, last, tab, parts, kv, sums=()):
    steps = NX * count
    pairs = steps * QB * KLEN

    def dq_spec(n):
        at = lambda i: jnp.clip(i - NX * n, 0, NX - 1)
        return pl.BlockSpec((1, *DQ), lambda i, t: (at(i), 0, 0, 0, 0))

    whole = pl.BlockSpec((KLEN, DH), lambda i, t: (0, 0))
    part = pl.BlockSpec((GROUP, WIDE, DH), lambda i, t: (t[i], 0, 0))
    in_specs = [part] * NY + [pl.BlockSpec((NSP, 2 * KROWS, DH), lambda i, t: (0, 0, 0))]
    out_specs = [dq_spec(n) for n in range(count)]
    out_shape = [jax.ShapeDtypeStruct((NX, *DQ), F32 if last else BF16)] * count
    scratch = []
    if last:
        out_specs.append(pl.BlockSpec((NSP, OUT_ROWS, DH), lambda i, t: (0, 0, 0)))
        out_shape.append(jax.ShapeDtypeStruct((NSP, OUT_ROWS, DH), BF16))
        scratch = [pltpu.VMEM((KLEN, DH), F32)] * 2
    else:
        out_specs += [whole] * 2
        out_shape += [jax.ShapeDtypeStruct((KLEN, DH), F32)] * 2
    return pl.pallas_call(
        functools.partial(grads, count, first, last),
        grid_spec=pltpu.PrefetchScalarGridSpec(
            num_scalar_prefetch=1,
            grid=(steps,),
            in_specs=in_specs + [whole] * len(sums),
            out_specs=out_specs,
            scratch_shapes=scratch,
        ),
        out_shape=out_shape,
        compiler_params=pltpu.CompilerParams(vmem_limit_bytes=26 << 20),
        cost_estimate=cost(pairs * 10 * DH, 4 << 20, pairs),
        name="grads",
    )(tab, *parts, kv, *sums)


def unpack(x_ref, dq_ref, dk_ref, dv_ref):
    for h in range(H):
        c = slice(h * DH, (h + 1) * DH)
        dk_ref[:, c] = x_ref[h, 0:KROWS, :].astype(F32)
        dv_ref[:, c] = x_ref[h, KROWS : 2 * KROWS, :].astype(F32)
        dq_ref[:, c] = x_ref[h, 2 * KROWS : OUT_ROWS, :].astype(F32)


def unpacked(x):
    return pl.pallas_call(
        unpack,
        out_shape=[
            jax.ShapeDtypeStruct((QROWS, H * DH), F32),
            jax.ShapeDtypeStruct((KROWS, H * DH), F32),
            jax.ShapeDtypeStruct((KROWS, H * DH), F32),
        ],
        cost_estimate=cost(10**6, 3 * 10**6),
        name="unpack",
    )(x)


def shift(x, axis, by):
    n = lax.axis_size(axis)
    return lax.ppermute(x, axis, [(i, (i + by) % n) for i in range(n)])


def regroup(x):
    return lax.all_to_all(x, SP, split_axis=0, concat_axis=0, tiled=True)


def body(queries, keys, values, outputs, out_grad, stats):
    y = lax.axis_index("y")
    xh = lax.axis_index("xh")
    group = lax.axis_index("xl") * 2 + lax.axis_index("c")
    at = (y.reshape(1).astype(jnp.int32), group.reshape(1).astype(jnp.int32))
    own = packed_queries(*at, queries, out_grad, outputs, stats)
    own = regroup(own)
    kv = packed_keys(keys, values)
    kv = regroup(kv)

    half = NSP // 2
    before = shift(own, "y", 1)
    after = shift(own, "y", -1)
    low = shift(before[:half], "y", 1)
    high = shift(after[half:], "y", -1)
    parts = (own, before, after, jnp.concatenate([low, high], axis=0))
    where = (y + jnp.array([0, 3, 1, 2], jnp.int32)) % NY

    def members(*dys):
        return [((y + dy) % NY) * NX + (xh + o) % NX for dy in dys for o in (1, 0)]

    def table(ks):
        return jnp.concatenate([jnp.stack(ks), where]).astype(jnp.int32)

    far, up, *sums = grads_call(2, True, False, table(members(2, 1)), parts, kv)
    far = shift(far, "y", 2)
    up = shift(up, "y", 1)
    down, *sums = grads_call(1, False, False, table(members(-1)), parts, kv, sums)
    down = shift(down, "y", -1)
    mine, packed = grads_call(1, False, True, table(members(0)), parts, kv, sums)
    other = mine[0] + (far[0].astype(F32) + up[0].astype(F32) + down[0].astype(F32))
    other = shift(other.astype(BF16), "xh", 1)
    mine = mine[1] + (far[1].astype(F32) + up[1].astype(F32) + down[1].astype(F32))
    mine = (mine + other.astype(F32)) * (ROOT * SCALE)
    mine = mine.reshape(NSP, QROWS, DH).astype(BF16)
    packed = lax.dynamic_update_slice(packed, mine, (0, 2 * KROWS, 0))
    packed = regroup(packed)
    return unpacked(packed)


def solution(mesh):
    torus = Mesh(mesh.devices.reshape(NY, NX, NZ, 2, 2), ALL)
    return jax.shard_map(
        body,
        mesh=torus,
        in_specs=(P(SP), P(ALL), P(ALL), P(SP), P(SP), P(SP)),
        out_specs=(P(ALL), P(ALL), P(ALL)),
        check_vma=False,
    )
```

profile of v0, /device:TPU:1, one launch (start us, length us, event | category | flops | bytes accessed | tf_op | source)
XLA Modules:
  0.0 150.9 jit_solution(12911097324025509913)
XLA Ops:
  0.6 2.5 %pack_queries.1 = bf16[32,72,128]{2,1,0:T(8,128)(2,1)} custom-call(s32[1]{0:T(128)} %bitcast.2.y_ref, s32[1]{0:T(128)} %bitcast.3.group_ref, bf16[128,4096]{1,0:T(8,128)(2,1)} %q_ref.1, bf16[128,4096]{1,0:T(8,128)(2,1)} %g_ref.1, bf16[128,4096]{1,0:T(8,128)(2,1)} %o_ref.1, f32[32,128]{1,0:T(8,128)} %bitcast.21), custom_call_target="tpu_custom_call" | custom-call | flops 1000000 | bytes 2000000 | tf_op jit(solution)/shard_map/pack_queries/pallas_call | solution.py:74
  3.1 11.0 %all-to-all-start = ((bf16[32,72,128]{2,1,0:T(8,128)(2,1)}), bf16[32,72,128]{2,1,0:T(8,128)(2,1)S(1)}, u32[]{:S(2)}, u32[]{:S(2)}) async-start(bf16[32,72,128]{2,1,0:T(8,128)(2,1)} %pack_queries.1), calls=%async_computation | async-start | bytes 1179648 | tf_op jit(solution)/shard_map/all_to_all | solution.py:235
  14.2 2.4 %pack_keys.1 = bf16[32,128,128]{2,1,0:T(8,128)(2,1)} custom-call(bf16[64,4096]{1,0:T(8,128)(2,1)} %k_ref.1, bf16[64,4096]{1,0:T(8,128)(2,1)} %v_ref.1), custom_call_target="tpu_custom_call" | custom-call | flops 1000000 | bytes 2000000 | tf_op jit(solution)/shard_map/pack_keys/pallas_call | solution.py:96
  16.5 0.0 copy-start
  16.5 15.8 %all-to-all-done.refs_0_ = bf16[32,72,128]{2,1,0:T(8,128)(2,1)S(1)} async-done(((bf16[32,72,128]{2,1,0:T(8,128)(2,1)}), bf16[32,72,128]{2,1,0:T(8,128)(2,1)S(1)}, u32[]{:S(2)}, u32[]{:S(2)}) %all-to-all-start) | async-done | bytes 589856 | tf_op jit(solution)/shard_map/all_to_all | solution.py:235
  32.3 4.7 %all-to-all-start.1 = ((bf16[32,128,128]{2,1,0:T(8,128)(2,1)}), bf16[32,128,128]{2,1,0:T(8,128)(2,1)S(1)}, u32[]{:S(2)}, u32[]{:S(2)}) async-start(bf16[32,128,128]{2,1,0:T(8,128)(2,1)} %pack_keys.1), calls=%async_computation.1 | async-start | bytes 2097152 | tf_op jit(solution)/shard_map/all_to_all | solution.py:235
  37.0 2.8 %collective-permute-start.1 = (bf16[32,72,128]{2,1,0:T(8,128)(2,1)S(1)}, bf16[32,72,128]{2,1,0:T(8,128)(2,1)S(1)}, u32[]{:S(2)}, u32[]{:S(2)}) collective-permute-start(bf16[32,72,128]{2,1,0:T(8,128)(2,1)S(1)} %all-to-all-done.refs_0_), channel_id=1, source_target_pairs={{0,192},{64,0},{128,64},{192,128},{1,193},{65,1},{129,65},{193,129... | collective-permute-start | bytes 1769480 | tf_op jit(solution)/shard_map/ppermute | solution.py:231
  39.9 0.0 collective-permute-start
  39.9 12.3 %collective-permute-done.1.refs_2_ = bf16[32,72,128]{2,1,0:T(8,128)(2,1)S(1)} collective-permute-done((bf16[32,72,128]{2,1,0:T(8,128)(2,1)S(1)}, bf16[32,72,128]{2,1,0:T(8,128)(2,1)S(1)}, u32[]{:S(2)}, u32[]{:S(2)}) %collective-permute-start.1) | collective-permute-done | bytes 589856 | tf_op jit(solution)/shard_map/ppermute | solution.py:231
  52.2 0.7 slice.41
  52.9 3.4 %collective-permute-start.3 = (bf16[16,72,128]{2,1,0:T(8,128)(2,1)}, bf16[16,72,128]{2,1,0:T(8,128)(2,1)}, u32[]{:S(2)}, u32[]{:S(2)}) collective-permute-start(bf16[16,72,128]{2,1,0:T(8,128)(2,1)} %slice.41), channel_id=1, source_target_pairs={{0,192},{64,0},{128,64},{192,128},{1,193},{65,1},{129,65},{193,129... | collective-permute-start | bytes 884744 | tf_op jit(solution)/shard_map/ppermute | solution.py:231
  56.3 0.0 collective-permute-done.refs_1_
  56.4 0.1 collective-permute-start.2
  56.5 0.0 copy-done
  56.6 0.1 concatenate.15.tab
  56.6 0.1 add_add_fusion.1
  56.7 8.1 %collective-permute-done.2 = bf16[16,72,128]{2,1,0:T(8,128)(2,1)} collective-permute-done((bf16[16,72,128]{2,1,0:T(8,128)(2,1)S(1)}, bf16[16,72,128]{2,1,0:T(8,128)(2,1)}, u32[]{:S(2)}, u32[]{:S(2)}) %collective-permute-start.2) | collective-permute-done | bytes 294944 | tf_op jit(solution)/shard_map/ppermute | solution.py:231
  64.8 1.0 constant_dynamic-update-slice_fusion.1
  65.8 0.0 collective-permute-done.3
  65.8 1.0 constant_dynamic-update-slice_fusion.refs_3_
  66.8 0.0 all-to-all-done.1.refs_4_
  66.9 12.6 %grads.3 = (bf16[2,4,4,32,128]{4,3,2,1,0:T(8,128)(2,1)S(1)}, bf16[2,4,4,32,128]{4,3,2,1,0:T(8,128)(2,1)S(1)}, f32[2048,128]{1,0:T(8,128)S(1)}, f32[2048,128]{1,0:T(8,128)S(1)}) custom-call(s32[8]{0:T(128)S(1)} %concatenate.15.tab, bf16[32,72,128]{2,1,0:T(8,128)(2,1)S(1)} %all-to-all-done.refs_0_, bf16[32,72,128]{2,1,0:T(8,128)(2,1)S(1)} %collective-permute-done.refs_1_, ...), custom_call_target="tpu_custom_call" | custom-call | flops 5368709120 | bytes 4194304 | tf_op jit(solution)/shard_map/grads/pallas_call | solution.py:192
  79.4 6.6 %grads.4 = (bf16[2,4,4,32,128]{4,3,2,1,0:T(8,128)(2,1)S(1)}, f32[2048,128]{1,0:T(8,128)S(1)}, f32[2048,128]{1,0:T(8,128)S(1)}) custom-call(s32[6]{0:T(128)S(1)} %get-tuple-element.21.tab, bf16[32,72,128]{2,1,0:T(8,128)(2,1)S(1)} %all-to-all-done.refs_0_, bf16[32,72,128]{2,1,0:T(8,128)(2,1)S(1)} %collective-permute-done.refs_1_, ...), custom_call_target="tpu_custom_call" | custom-call | flops 2684354560 | bytes 4194304 | tf_op jit(solution)/shard_map/grads/pallas_call | solution.py:192
  86.1 1.0 collective-permute-start.6
  87.0 0.5 collective-permute-start.4
  87.5 0.6 collective-permute-start.5
  88.1 6.7 %grads.5 = (f32[2,4,4,32,128]{4,3,2,1,0:T(8,128)S(1)}, bf16[32,144,128]{2,1,0:T(8,128)(2,1)S(1)}) custom-call(s32[6]{0:T(128)S(1)} %get-tuple-element.22.tab, bf16[32,72,128]{2,1,0:T(8,128)(2,1)S(1)} %all-to-all-done.refs_0_, bf16[32,72,128]{2,1,0:T(8,128)(2,1)S(1)} %collective-permute-done.refs_1_, bf16[32,72,128]{2,1,0:T(8,128)(2,1)S(1)} %collective-permute-done.1.refs_2_, ...), custom_call_target="tpu_custom_call" | custom-call | flops 2684354560 | bytes 4194304 | tf_op jit(solution)/shard_map/grads/pallas_call | solution.py:192
  94.8 0.0 collective-permute-done.6
  94.8 0.0 collective-permute-done.4
  94.9 7.5 %collective-permute-done.5 = bf16[2,4,4,32,128]{4,3,2,1,0:T(8,128)(2,1)S(1)} collective-permute-done((bf16[2,4,4,32,128]{4,3,2,1,0:T(8,128)(2,1)S(1)}, bf16[2,4,4,32,128]{4,3,2,1,0:T(8,128)(2,1)S(1)}, u32[]{:S(2)}, u32[]{:S(2)}) %collective-permute-start.5) | collective-permute-done | bytes 262176 | tf_op jit(solution)/shard_map/ppermute | solution.py:231
  102.4 0.1 fusion.2
  102.5 2.5 %collective-permute-start.7 = (bf16[4,4,32,128]{3,2,1,0:T(8,128)(2,1)S(1)}, bf16[4,4,32,128]{3,2,1,0:T(8,128)(2,1)S(1)}, u32[]{:S(2)}, u32[]{:S(2)}) collective-permute-start(bf16[4,4,32,128]{3,2,1,0:T(8,128)(2,1)S(1)} %fusion.2), channel_id=1, source_target_pairs={{0,32},{32,0},{1,33},{33,1},{2,34},{34,2},{3,35},{35,3},{4,36},{36... | collective-permute-start | bytes 393224 | tf_op jit(solution)/shard_map/ppermute | solution.py:231
  105.0 3.6 %collective-permute-done.7 = bf16[4,4,32,128]{3,2,1,0:T(8,128)(2,1)S(1)} collective-permute-done((bf16[4,4,32,128]{3,2,1,0:T(8,128)(2,1)S(1)}, bf16[4,4,32,128]{3,2,1,0:T(8,128)(2,1)S(1)}, u32[]{:S(2)}, u32[]{:S(2)}) %collective-permute-start.7) | collective-permute-done | bytes 131104 | tf_op jit(solution)/shard_map/ppermute | solution.py:231
  108.6 0.1 fusion.1
  108.7 39.4 %all_to_all.15.x_ref = bf16[32,144,128]{2,1,0:T(8,128)(2,1)} all-to-all(bf16[32,144,128]{2,1,0:T(8,128)(2,1)S(1)} %constant_dynamic-update-slice_fusion.2), channel_id=1, replica_groups=mesh['y'=4,'xh'=2,'z'=8,'xl'=2,'c'=2] {'z','xl','c'}, dimensions={0} | all-to-all | bytes 2359296 | tf_op jit(solution)/shard_map/all_to_all | solution.py:235
  148.2 2.7 %unpack.1 = (f32[16,4096]{1,0:T(8,128)}, f32[64,4096]{1,0:T(8,128)}, f32[64,4096]{1,0:T(8,128)}) custom-call(bf16[32,144,128]{2,1,0:T(8,128)(2,1)} %all_to_all.15.x_ref), custom_call_target="tpu_custom_call" | custom-call | flops 1000000 | bytes 3000000 | tf_op jit(solution)/shard_map/unpack/pallas_call | solution.py:217
  (3 shorter events, 0.1 us)
Async XLA Ops:
  3.1 29.2 %all-to-all-start = ((bf16[32,72,128]{2,1,0:T(8,128)(2,1)}), bf16[32,72,128]{2,1,0:T(8,128)(2,1)S(1)}, u32[]{:S(2)}, u32[]{:S(2)}) async-start(bf16[32,72,128]{2,1,0:T(8,128)(2,1)} %pack_queries.1), calls=%async_computation | async-start | bytes 1179648 | tf_op jit(solution)/shard_map/all_to_all | solution.py:235
  16.5 39.9 %copy-start = (s32[4]{0:T(128)S(1)}, s32[4]{0:T(128)}, u32[]{:S(2)}) copy-start(s32[4]{0:T(128)} %constant.93.clone) | copy-start | bytes 52
  32.3 34.5 %all-to-all-start.1 = ((bf16[32,128,128]{2,1,0:T(8,128)(2,1)}), bf16[32,128,128]{2,1,0:T(8,128)(2,1)S(1)}, u32[]{:S(2)}, u32[]{:S(2)}) async-start(bf16[32,128,128]{2,1,0:T(8,128)(2,1)} %pack_keys.1), calls=%async_computation.1 | async-start | bytes 2097152 | tf_op jit(solution)/shard_map/all_to_all | solution.py:235
  37.0 15.1 %collective-permute-start.1 = (bf16[32,72,128]{2,1,0:T(8,128)(2,1)S(1)}, bf16[32,72,128]{2,1,0:T(8,128)(2,1)S(1)}, u32[]{:S(2)}, u32[]{:S(2)}) collective-permute-start(bf16[32,72,128]{2,1,0:T(8,128)(2,1)S(1)} %all-to-all-done.refs_0_), channel_id=1, source_target_pairs={{0,192},{64,0},{128,64},{192,128},{1,193},{65,1},{129,65},{193,129... | collective-permute-start | bytes 1769480 | tf_op jit(solution)/shard_map/ppermute | solution.py:231
  39.9 16.5 %collective-permute-start = (bf16[32,72,128]{2,1,0:T(8,128)(2,1)S(1)}, bf16[32,72,128]{2,1,0:T(8,128)(2,1)S(1)}, u32[]{:S(2)}, u32[]{:S(2)}) collective-permute-start(bf16[32,72,128]{2,1,0:T(8,128)(2,1)S(1)} %all-to-all-done.refs_0_), channel_id=1, source_target_pairs={{0,64},{64,128},{128,192},{192,0},{1,65},{65,129},{129,193},{193,1... | collective-permute-start | bytes 1769480 | tf_op jit(solution)/shard_map/ppermute | solution.py:231
  52.9 12.9 %collective-permute-start.3 = (bf16[16,72,128]{2,1,0:T(8,128)(2,1)}, bf16[16,72,128]{2,1,0:T(8,128)(2,1)}, u32[]{:S(2)}, u32[]{:S(2)}) collective-permute-start(bf16[16,72,128]{2,1,0:T(8,128)(2,1)} %slice.41), channel_id=1, source_target_pairs={{0,192},{64,0},{128,64},{192,128},{1,193},{65,1},{129,65},{193,129... | collective-permute-start | bytes 884744 | tf_op jit(solution)/shard_map/ppermute | solution.py:231
  56.4 8.5 %collective-permute-start.2 = (bf16[16,72,128]{2,1,0:T(8,128)(2,1)S(1)}, bf16[16,72,128]{2,1,0:T(8,128)(2,1)}, u32[]{:S(2)}, u32[]{:S(2)}) collective-permute-start(bf16[16,72,128]{2,1,0:T(8,128)(2,1)S(1)} %slice.40), channel_id=1, source_target_pairs={{0,64},{64,128},{128,192},{192,0},{1,65},{65,129},{129,193},{193,1... | collective-permute-start | bytes 884744 | tf_op jit(solution)/shard_map/ppermute | solution.py:231
  86.1 8.8 %collective-permute-start.6 = (bf16[2,4,4,32,128]{4,3,2,1,0:T(8,128)(2,1)S(1)}, bf16[2,4,4,32,128]{4,3,2,1,0:T(8,128)(2,1)S(1)}, u32[]{:S(2)}, u32[]{:S(2)}) collective-permute-start(bf16[2,4,4,32,128]{4,3,2,1,0:T(8,128)(2,1)S(1)} %get-tuple-element.20), channel_id=1, source_target_pairs={{0,192},{64,0},{128,64},{192,128},{1,193},{65,1},{129,65},{193,129... | collective-permute-start | bytes 786440 | tf_op jit(solution)/shard_map/ppermute | solution.py:231
  87.0 7.8 %collective-permute-start.4 = (bf16[2,4,4,32,128]{4,3,2,1,0:T(8,128)(2,1)S(1)}, bf16[2,4,4,32,128]{4,3,2,1,0:T(8,128)(2,1)S(1)}, u32[]{:S(2)}, u32[]{:S(2)}) collective-permute-start(bf16[2,4,4,32,128]{4,3,2,1,0:T(8,128)(2,1)S(1)} %get-tuple-element.18), channel_id=1, source_target_pairs={{0,128},{64,192},{128,0},{192,64},{1,129},{65,193},{129,1},{193,65... | collective-permute-start | bytes 786440 | tf_op jit(solution)/shard_map/ppermute | solution.py:231
  87.5 14.9 %collective-permute-start.5 = (bf16[2,4,4,32,128]{4,3,2,1,0:T(8,128)(2,1)S(1)}, bf16[2,4,4,32,128]{4,3,2,1,0:T(8,128)(2,1)S(1)}, u32[]{:S(2)}, u32[]{:S(2)}) collective-permute-start(bf16[2,4,4,32,128]{4,3,2,1,0:T(8,128)(2,1)S(1)} %get-tuple-element.19), channel_id=1, source_target_pairs={{0,64},{64,128},{128,192},{192,0},{1,65},{65,129},{129,193},{193,1... | collective-permute-start | bytes 786440 | tf_op jit(solution)/shard_map/ppermute | solution.py:231
  102.5 6.2 %collective-permute-start.7 = (bf16[4,4,32,128]{3,2,1,0:T(8,128)(2,1)S(1)}, bf16[4,4,32,128]{3,2,1,0:T(8,128)(2,1)S(1)}, u32[]{:S(2)}, u32[]{:S(2)}) collective-permute-start(bf16[4,4,32,128]{3,2,1,0:T(8,128)(2,1)S(1)} %fusion.2), channel_id=1, source_target_pairs={{0,32},{32,0},{1,33},{33,1},{2,34},{34,2},{3,35},{35,3},{4,36},{36... | collective-permute-start | bytes 393224 | tf_op jit(solution)/shard_map/ppermute | solution.py:231
where the time goes:
time: 151 us
  waiting for transfers between devices  47.4 us (31%)
  blocking collectives  39.4 us (26%)
  Pallas kernels  33.5 us (22%)
  starting transfers between devices  26.6 us (18%)
  local copies, waits for them, and re-layouts  2.86 us (2%)
    all_to_all x1, blocking collectives, regroup(): return lax.all_to_all(x, SP, split_axis=0, concat_axis=0, tiled=True)  39.4 us
    ppermute x8, waiting for transfers between devices, shift(): return lax.ppermute(x, axis, [(i, (i + by) % n) for i in range(n)])  31.6 us
    pallas_call x3, Pallas kernels, grads_call(): pl.pallas_call(functools.partial(grads, count, first, last), grid_spec=pl...  25.9 us
    all_to_all x2, waiting for transfers between devices, regroup(): return lax.all_to_all(x, SP, split_axis=0, concat_axis=0, tiled=True)  15.8 us
    all_to_all x2, starting transfers between devices, regroup(): return lax.all_to_all(x, SP, split_axis=0, concat_axis=0, tiled=True)  15.8 us
    ppermute x8, starting transfers between devices, shift(): return lax.ppermute(x, axis, [(i, (i + by) % n) for i in range(n)])  10.9 us
  transfers between devices with their start and end apart: 10, of which 5 were waited for; matrix products, arithmetic and copies ran while one was open for 2% of the time, Pallas kernels for 6%

commit v1 on v0

--- a/solution.py
+++ b/solution.py
@@ -20,8 +20,9 @@
 ALL = ("y", "xh", "z", "xl", "c")
 NSP = 32
 ROWS = QLEN // NSP
-SHARE = ROWS // NY
-GROUP = DH // SHARE
+SHARE = ROWS // NKV
+GROUP = NSP // NKV
+LANES = GROUP * SHARE
 WIDE = 2 * SHARE + 8
 KROWS = KLEN // NSP
 QB = QLEN // NKV
@@ -47,7 +48,7 @@
     return hi, mid, x - hi - mid
 
 
-def pack_queries(y_ref, group_ref, q_ref, g_ref, o_ref, s_ref, out_ref):
+def pack_queries(share_ref, group_ref, q_ref, g_ref, o_ref, s_ref, out_ref):
     cols = []
     for h in range(H):
         c = slice(h * DH, (h + 1) * DH)
@@ -57,19 +58,19 @@
         cols.append(jnp.sum(prod, axis=1, keepdims=True))
     delta = jnp.transpose(jnp.concatenate(cols, axis=1))
     stats = s_ref[:, 0:SHARE]
-    for b in range(1, NY):
-        stats = jnp.where(y_ref[0] == b, s_ref[:, b * SHARE : (b + 1) * SHARE], stats)
+    for b in range(1, NKV):
+        stats = jnp.where(share_ref[0] == b, s_ref[:, b * SHARE : (b + 1) * SHARE], stats)
     lane = lax.broadcasted_iota(jnp.int32, (H, DH), 1)
-    here = lane // SHARE == group_ref[0]
+    here = lane // SHARE % GROUP == group_ref[0]
     row = lax.broadcasted_iota(jnp.int32, (H, 8, DH), 1)
     tile = jnp.zeros((H, 8, DH), F32)
     for r, x in enumerate(three(stats * LOG2E) + three(delta)):
-        x = jnp.where(here, jnp.concatenate([x] * GROUP, axis=1), 0.0)
+        x = jnp.where(here, jnp.concatenate([x] * (DH // SHARE), axis=1), 0.0)
         tile = jnp.where(row == r, x[:, None, :], tile)
     out_ref[:, 2 * SHARE : WIDE, :] = tile.astype(BF16)
 
 
-def packed_queries(y, group, queries, out_grad, outputs, stats):
+def packed_queries(share, group, queries, out_grad, outputs, stats):
     wide = pl.BlockSpec((SHARE, H * DH), lambda i, y, g: (y[0], 0))
     return pl.pallas_call(
         pack_queries,
@@ -82,7 +83,7 @@
         out_shape=jax.ShapeDtypeStruct((H, WIDE, DH), BF16),
         cost_estimate=cost(10**6, 2 * 10**6),
         name="pack_queries",
-    )(y, group, queries, out_grad, outputs, jnp.transpose(stats))
+    )(share, group, queries, out_grad, outputs, jnp.transpose(stats))
 
 
 def pack_keys(k_ref, v_ref, out_ref):
@@ -104,9 +105,12 @@
 def queries_of(parts):
     q = jnp.concatenate([p[:, 0:SHARE, :].reshape(-1, DH) for p in parts], axis=0)
     g = jnp.concatenate([p[:, SHARE : 2 * SHARE, :].reshape(-1, DH) for p in parts], axis=0)
+    low = lax.broadcasted_iota(jnp.int32, (8, DH), 1) < LANES
     st, de = [], []
-    for p in parts:
-        x = jnp.sum(p[:, 2 * SHARE : WIDE, :].astype(F32), axis=0)
+    for one, two in zip(parts[0::2], parts[1::2]):
+        one = jnp.sum(one[:, 2 * SHARE : WIDE, :].astype(F32), axis=0)
+        two = jnp.sum(two[:, 2 * SHARE : WIDE, :].astype(F32), axis=0)
+        x = jnp.where(low, one, two)
         st.append(x[0:1] + x[1:2] + x[2:3])
         de.append(x[3:4] + x[4:5] + x[5:6])
     return q, g, jnp.concatenate(st, axis=1), jnp.concatenate(de, axis=1)
@@ -126,13 +130,13 @@
         dk_ref[at, :] += dot(ds, q, ((1,), (0,)))
         part = dot(ds, k, ((0,), (0,)))
         total = part if total is None else total + part
-    return total.reshape(NY, GROUP, SHARE, DH)
+    return total.reshape(NKV, GROUP, SHARE, DH)
 
 
 def grads(count, first, last, tab, *refs):
-    parts = refs[:NY]
-    kv_ref = refs[NY]
-    rest = refs[NY + 1 :]
+    parts = refs[:NKV]
+    kv_ref = refs[NKV]
+    rest = refs[NKV + 1 :]
     if not first:
         dk_in, dv_in = rest[:2]
         rest = rest[2:]
@@ -150,7 +154,7 @@
 
         @pl.when(step // NX == n)
         def _(dq_ref=dq_ref):
-            for b in range(NY):
+            for b in range(NKV):
                 dq_ref[0, :, tab[NX * count + b], :, :] = total[b].astype(dq_ref.dtype)
 
     if last:
@@ -164,7 +168,7 @@
             out_ref[:, KROWS : 2 * KROWS, :] = dv.reshape(NSP, KROWS, DH)
 
 
-DQ = (GROUP, NY, SHARE, DH)
+DQ = (GROUP, NKV, SHARE, DH)
 OUT_ROWS = 2 * KROWS + QROWS
 
 
@@ -178,7 +182,7 @@
 
     whole = pl.BlockSpec((KLEN, DH), lambda i, t: (0, 0))
     part = pl.BlockSpec((GROUP, WIDE, DH), lambda i, t: (t[i], 0, 0))
-    in_specs = [part] * NY + [pl.BlockSpec((NSP, 2 * KROWS, DH), lambda i, t: (0, 0, 0))]
+    in_specs = [part] * NKV + [pl.BlockSpec((NSP, 2 * KROWS, DH), lambda i, t: (0, 0, 0))]
     out_specs = [dq_spec(n) for n in range(count)]
     out_shape = [jax.ShapeDtypeStruct((NX, *DQ), F32 if last else BF16)] * count
     scratch = []
@@ -206,7 +210,7 @@
 
 
 def unpack(x_ref, dq_ref, dk_ref, dv_ref):
-    for h in range(H):
+    for h in range(x_ref.shape[0]):
         c = slice(h * DH, (h + 1) * DH)
         dk_ref[:, c] = x_ref[h, 0:KROWS, :].astype(F32)
         dv_ref[:, c] = x_ref[h, KROWS : 2 * KROWS, :].astype(F32)
@@ -214,8 +218,16 @@
 
 
 def unpacked(x):
+    steps = 4
+
+    def wide(rows):
+        return pl.BlockSpec((rows, H * DH // steps), lambda i: (0, i))
+
     return pl.pallas_call(
         unpack,
+        grid=(steps,),
+        in_specs=[pl.BlockSpec((H // steps, OUT_ROWS, DH), lambda i: (i, 0, 0))],
+        out_specs=[wide(QROWS), wide(KROWS), wide(KROWS)],
         out_shape=[
             jax.ShapeDtypeStruct((QROWS, H * DH), F32),
             jax.ShapeDtypeStruct((KROWS, H * DH), F32),
@@ -239,19 +251,23 @@
     y = lax.axis_index("y")
     xh = lax.axis_index("xh")
     group = lax.axis_index("xl") * 2 + lax.axis_index("c")
-    at = (y.reshape(1).astype(jnp.int32), group.reshape(1).astype(jnp.int32))
+    share = (y * NX + xh).astype(jnp.int32)
+    at = (share.reshape(1), group.reshape(1).astype(jnp.int32))
     own = packed_queries(*at, queries, out_grad, outputs, stats)
     own = regroup(own)
     kv = packed_keys(keys, values)
     kv = regroup(kv)
 
-    half = NSP // 2
     before = shift(own, "y", 1)
     after = shift(own, "y", -1)
-    low = shift(before[:half], "y", 1)
-    high = shift(after[half:], "y", -1)
-    parts = (own, before, after, jnp.concatenate([low, high], axis=0))
-    where = (y + jnp.array([0, 3, 1, 2], jnp.int32)) % NY
+    own2 = shift(own, "xh", 1)
+    before2 = shift(own2, "y", 1)
+    after2 = shift(own2, "y", -1)
+    across = shift(before, "y", 1)
+    across2 = shift(after2, "y", -1)
+    parts = (own, own2, before, before2, after, after2, across, across2)
+    away = (y + jnp.array([0, 0, 3, 3, 1, 1, 2, 2], jnp.int32)) % NY
+    where = away * NX + (xh + jnp.array([0, 1] * NY, jnp.int32)) % NX
 
     def members(*dys):
         return [((y + dy) % NY) * NX + (xh + o) % NX for dy in dys for o in (1, 0)]

time: 151 us -> 165 us (1.093)
  starting transfers between devices: 26.6 us -> 33.4 us
  blocking collectives: 39.4 us -> 43.5 us
  Pallas kernels: 33.5 us -> 36.9 us
  local copies, waits for them, and re-layouts: 2.86 us -> 0.11 us
  waiting for transfers between devices: 47.4 us -> 49.2 us
    ppermute x8 -> x11, waiting for transfers between devices: 31.6 us -> 38.8 us  [shift(): return lax.ppermute(x, axis, [(i, (i + by) % n) for i in range(n)])]
    ppermute x8 -> x11, starting transfers between devices: 10.9 us -> 17.4 us  [shift(): return lax.ppermute(x, axis, [(i, (i + by) % n) for i in range(n)])]
    all_to_all x2, waiting for transfers between devices: 15.8 us -> 10.3 us  [regroup(): return lax.all_to_all(x, SP, split_axis=0, concat_axis=0, tiled=True)]
    all_to_all x1, blocking collectives: 39.4 us -> 43.5 us  [regroup(): return lax.all_to_all(x, SP, split_axis=0, concat_axis=0, tiled=True)]
    pallas_call x3, Pallas kernels: 25.9 us -> 28.3 us  [grads_call(): pl.pallas_call(functools.partial(grads, count, first, last), grid_spec=pl...]
  transfers between devices with their start and end apart: 10 -> 13, of which waited for: 5 -> 9; matrix products, arithmetic and copies ran while one was open for 2% -> 0% of each run, Pallas kernels for 6% -> 6%
where the time goes in v1:
time: 165 us; the launch traced here: 164 us
  waiting for transfers between devices  49.2 us (30%)
  blocking collectives  43.5 us (26%)
  Pallas kernels  36.9 us (22%)
  starting transfers between devices  33.4 us (20%)
    all_to_all x1, blocking collectives, regroup(): return lax.all_to_all(x, SP, split_axis=0, concat_axis=0, tiled=True)  43.5 us
    ppermute x11, waiting for transfers between devices, shift(): return lax.ppermute(x, axis, [(i, (i + by) % n) for i in range(n)])  38.8 us
    pallas_call x3, Pallas kernels, grads_call(): pl.pallas_call(functools.partial(grads, count, first, last), grid_spec=pl...  28.3 us
    ppermute x11, starting transfers between devices, shift(): return lax.ppermute(x, axis, [(i, (i + by) % n) for i in range(n)])  17.4 us
    all_to_all x2, starting transfers between devices, regroup(): return lax.all_to_all(x, SP, split_axis=0, concat_axis=0, tiled=True)  16 us
    all_to_all x2, waiting for transfers between devices, regroup(): return lax.all_to_all(x, SP, split_axis=0, concat_axis=0, tiled=True)  10.3 us
    pallas_call x1, Pallas kernels, unpacked(): pl.pallas_call(unpack, grid=(steps,), in_specs=[pl.BlockSpec((H // steps,...  3.62 us
  transfers between devices with their start and end apart: 13, of which 9 were waited for; matrix products, arithmetic and copies ran while one was open for 0% of the time, Pallas kernels for 6%

profile of v1, /device:TPU:1, one launch (start us, length us, event | category | flops | bytes accessed | tf_op | source)
XLA Modules:
  0.0 164.0 jit_solution(15217080739844323290)
XLA Ops:
  0.6 2.6 %pack_queries.1 = bf16[32,40,128]{2,1,0:T(8,128)(2,1)} custom-call(s32[1]{0:T(128)} %bitcast.2.share_ref, s32[1]{0:T(128)} %bitcast.3.group_ref, bf16[128,4096]{1,0:T(8,128)(2,1)} %q_ref.1, bf16[128,4096]{1,0:T(8,128)(2,1)} %g_ref.1, bf16[128,4096]{1,0:T(8,128)(2,1)} %o_ref.1, f32[32,128]{1,0:T(8,128)} %bitcast.21), custom_call_target="tpu_custom_call" | custom-call | flops 1000000 | bytes 2000000 | tf_op jit(solution)/shard_map/pack_queries/pallas_call | solution.py:75
  3.2 11.0 %all-to-all-start = ((bf16[32,40,128]{2,1,0:T(8,128)(2,1)}), bf16[32,40,128]{2,1,0:T(8,128)(2,1)S(1)}, u32[]{:S(2)}, u32[]{:S(2)}) async-start(bf16[32,40,128]{2,1,0:T(8,128)(2,1)} %pack_queries.1), calls=%async_computation | async-start | bytes 655360 | tf_op jit(solution)/shard_map/all_to_all | solution.py:247
  14.3 2.4 %pack_keys.1 = bf16[32,128,128]{2,1,0:T(8,128)(2,1)} custom-call(bf16[64,4096]{1,0:T(8,128)(2,1)} %k_ref.1, bf16[64,4096]{1,0:T(8,128)(2,1)} %v_ref.1), custom_call_target="tpu_custom_call" | custom-call | flops 1000000 | bytes 2000000 | tf_op jit(solution)/shard_map/pack_keys/pallas_call | solution.py:97
  16.6 0.0 copy-start
  16.6 0.0 copy-start.1
  16.6 10.3 %all-to-all-done.refs_0_ = bf16[32,40,128]{2,1,0:T(8,128)(2,1)S(1)} async-done(((bf16[32,40,128]{2,1,0:T(8,128)(2,1)}), bf16[32,40,128]{2,1,0:T(8,128)(2,1)S(1)}, u32[]{:S(2)}, u32[]{:S(2)}) %all-to-all-start) | async-done | bytes 327712 | tf_op jit(solution)/shard_map/all_to_all | solution.py:247
  26.9 4.9 %all-to-all-start.1 = ((bf16[32,128,128]{2,1,0:T(8,128)(2,1)}), bf16[32,128,128]{2,1,0:T(8,128)(2,1)S(1)}, u32[]{:S(2)}, u32[]{:S(2)}) async-start(bf16[32,128,128]{2,1,0:T(8,128)(2,1)} %pack_keys.1), calls=%async_computation.1 | async-start | bytes 2097152 | tf_op jit(solution)/shard_map/all_to_all | solution.py:247
  31.9 2.5 %collective-permute-start = (bf16[32,40,128]{2,1,0:T(8,128)(2,1)S(1)}, bf16[32,40,128]{2,1,0:T(8,128)(2,1)S(1)}, u32[]{:S(2)}, u32[]{:S(2)}) collective-permute-start(bf16[32,40,128]{2,1,0:T(8,128)(2,1)S(1)} %all-to-all-done.refs_0_), channel_id=1, source_target_pairs={{0,32},{32,0},{1,33},{33,1},{2,34},{34,2},{3,35},{35,3},{4,36},{36... | collective-permute-start | bytes 983048 | tf_op jit(solution)/shard_map/ppermute | solution.py:243
  34.4 1.3 collective-permute-start.1
  35.7 13.2 %collective-permute-done.refs_1_ = bf16[32,40,128]{2,1,0:T(8,128)(2,1)S(1)} collective-permute-done((bf16[32,40,128]{2,1,0:T(8,128)(2,1)S(1)}, bf16[32,40,128]{2,1,0:T(8,128)(2,1)S(1)}, u32[]{:S(2)}, u32[]{:S(2)}) %collective-permute-start) | collective-permute-done | bytes 327712 | tf_op jit(solution)/shard_map/ppermute | solution.py:243
  48.9 2.7 %collective-permute-start.4 = (bf16[32,40,128]{2,1,0:T(8,128)(2,1)S(1)}, bf16[32,40,128]{2,1,0:T(8,128)(2,1)S(1)}, u32[]{:S(2)}, u32[]{:S(2)}) collective-permute-start(bf16[32,40,128]{2,1,0:T(8,128)(2,1)S(1)} %collective-permute-done.refs_1_), channel_id=1, source_target_pairs={{0,192},{64,0},{128,64},{192,128},{1,193},{65,1},{129,65},{193,129... | collective-permute-start | bytes 983048 | tf_op jit(solution)/shard_map/ppermute | solution.py:243
  51.6 0.5 collective-permute-start.3
  52.1 1.0 collective-permute-start.2
  53.1 0.0 collective-permute-done.1.refs_2_
  53.1 0.0 collective-permute-start.5
  53.1 4.5 %collective-permute-done.4.refs_5_ = bf16[32,40,128]{2,1,0:T(8,128)(2,1)S(1)} collective-permute-done((bf16[32,40,128]{2,1,0:T(8,128)(2,1)S(1)}, bf16[32,40,128]{2,1,0:T(8,128)(2,1)S(1)}, u32[]{:S(2)}, u32[]{:S(2)}) %collective-permute-start.4) | collective-permute-done | bytes 327712 | tf_op jit(solution)/shard_map/ppermute | solution.py:243
  57.6 3.4 %collective-permute-start.6 = (bf16[32,40,128]{2,1,0:T(8,128)(2,1)S(1)}, bf16[32,40,128]{2,1,0:T(8,128)(2,1)}, u32[]{:S(2)}, u32[]{:S(2)}) collective-permute-start(bf16[32,40,128]{2,1,0:T(8,128)(2,1)S(1)} %collective-permute-done.4.refs_5_), channel_id=1, source_target_pairs={{0,192},{64,0},{128,64},{192,128},{1,193},{65,1},{129,65},{193,129... | collective-permute-start | bytes 983048 | tf_op jit(solution)/shard_map/ppermute | solution.py:243
  61.0 0.0 copy-done
  61.0 0.0 copy-done.1
  61.0 0.1 concatenate.11.tab
  61.1 0.1 add_add_fusion.1
  61.2 3.4 %collective-permute-done.3.refs_4_ = bf16[32,40,128]{2,1,0:T(8,128)(2,1)S(1)} collective-permute-done((bf16[32,40,128]{2,1,0:T(8,128)(2,1)S(1)}, bf16[32,40,128]{2,1,0:T(8,128)(2,1)S(1)}, u32[]{:S(2)}, u32[]{:S(2)}) %collective-permute-start.3) | collective-permute-done | bytes 327712 | tf_op jit(solution)/shard_map/ppermute | solution.py:243
  64.6 3.3 %collective-permute-done.5.refs_6_ = bf16[32,40,128]{2,1,0:T(8,128)(2,1)S(1)} collective-permute-done((bf16[32,40,128]{2,1,0:T(8,128)(2,1)S(1)}, bf16[32,40,128]{2,1,0:T(8,128)(2,1)S(1)}, u32[]{:S(2)}, u32[]{:S(2)}) %collective-permute-start.5) | collective-permute-done | bytes 327712 | tf_op jit(solution)/shard_map/ppermute | solution.py:243
  67.9 0.0 collective-permute-done.2.refs_3_
  67.9 3.7 %collective-permute-done.6.refs_7_ = bf16[32,40,128]{2,1,0:T(8,128)(2,1)} collective-permute-done((bf16[32,40,128]{2,1,0:T(8,128)(2,1)S(1)}, bf16[32,40,128]{2,1,0:T(8,128)(2,1)}, u32[]{:S(2)}, u32[]{:S(2)}) %collective-permute-start.6) | collective-permute-done | bytes 327712 | tf_op jit(solution)/shard_map/ppermute | solution.py:243
  71.6 0.0 all-to-all-done.1.refs_8_
  71.6 13.4 %grads.3 = (bf16[2,4,8,16,128]{4,3,2,1,0:T(8,128)(2,1)S(1)}, bf16[2,4,8,16,128]{4,3,2,1,0:T(8,128)(2,1)S(1)}, f32[2048,128]{1,0:T(8,128)S(1)}, f32[2048,128]{1,0:T(8,128)S(1)}) custom-call(s32[12]{0:T(128)S(1)} %concatenate.11.tab, bf16[32,40,128]{2,1,0:T(8,128)(2,1)S(1)} %all-to-all-done.refs_0_, bf16[32,40,128]{2,1,0:T(8,128)(2,1)S(1)} %collective-permute-done.refs_1_, ...), custom_call_target="tpu_custom_call" | custom-call | flops 5368709120 | bytes 4194304 | tf_op jit(solution)/shard_map/grads/pallas_call | solution.py:196
  85.0 7.4 %grads.4 = (bf16[2,4,8,16,128]{4,3,2,1,0:T(8,128)(2,1)S(1)}, f32[2048,128]{1,0:T(8,128)S(1)}, f32[2048,128]{1,0:T(8,128)S(1)}) custom-call(s32[10]{0:T(128)S(1)} %get-tuple-element.21.tab, bf16[32,40,128]{2,1,0:T(8,128)(2,1)S(1)} %all-to-all-done.refs_0_, bf16[32,40,128]{2,1,0:T(8,128)(2,1)S(1)} %collective-permute-done.refs_1_, ...), custom_call_target="tpu_custom_call" | custom-call | flops 2684354560 | bytes 4194304 | tf_op jit(solution)/shard_map/grads/pallas_call | solution.py:196
  92.5 3.6 %collective-permute-start.9 = (bf16[2,4,8,16,128]{4,3,2,1,0:T(8,128)(2,1)S(1)}, bf16[2,4,8,16,128]{4,3,2,1,0:T(8,128)(2,1)S(1)}, u32[]{:S(2)}, u32[]{:S(2)}) collective-permute-start(bf16[2,4,8,16,128]{4,3,2,1,0:T(8,128)(2,1)S(1)} %get-tuple-element.20), channel_id=1, source_target_pairs={{0,192},{64,0},{128,64},{192,128},{1,193},{65,1},{129,65},{193,129... | collective-permute-start | bytes 786440 | tf_op jit(solution)/shard_map/ppermute | solution.py:243
  96.0 0.0 collective-permute-start.7
  96.1 0.7 collective-permute-start.8
  96.7 7.5 %grads.5 = (f32[2,4,8,16,128]{4,3,2,1,0:T(8,128)S(1)}, bf16[32,144,128]{2,1,0:T(8,128)(2,1)S(1)}) custom-call(s32[10]{0:T(128)S(1)} %get-tuple-element.22.tab, bf16[32,40,128]{2,1,0:T(8,128)(2,1)S(1)} %all-to-all-done.refs_0_, bf16[32,40,128]{2,1,0:T(8,128)(2,1)S(1)} %collective-permute-done.refs_1_, ...), custom_call_target="tpu_custom_call" | custom-call | flops 2684354560 | bytes 4194304 | tf_op jit(solution)/shard_map/grads/pallas_call | solution.py:196
  104.3 1.7 %collective-permute-done.9 = bf16[2,4,8,16,128]{4,3,2,1,0:T(8,128)(2,1)S(1)} collective-permute-done((bf16[2,4,8,16,128]{4,3,2,1,0:T(8,128)(2,1)S(1)}, bf16[2,4,8,16,128]{4,3,2,1,0:T(8,128)(2,1)S(1)}, u32[]{:S(2)}, u32[]{:S(2)}) %collective-permute-start.9) | collective-permute-done | bytes 262176 | tf_op jit(solution)/shard_map/ppermute | solution.py:243
  106.0 0.0 collective-permute-done.7
  106.0 4.8 %collective-permute-done.8 = bf16[2,4,8,16,128]{4,3,2,1,0:T(8,128)(2,1)S(1)} collective-permute-done((bf16[2,4,8,16,128]{4,3,2,1,0:T(8,128)(2,1)S(1)}, bf16[2,4,8,16,128]{4,3,2,1,0:T(8,128)(2,1)S(1)}, u32[]{:S(2)}, u32[]{:S(2)}) %collective-permute-start.8) | collective-permute-done | bytes 262176 | tf_op jit(solution)/shard_map/ppermute | solution.py:243
  110.8 0.1 fusion.2
  110.9 1.7 %collective-permute-start.10 = (bf16[4,8,16,128]{3,2,1,0:T(8,128)(2,1)S(1)}, bf16[4,8,16,128]{3,2,1,0:T(8,128)(2,1)S(1)}, u32[]{:S(2)}, u32[]{:S(2)}) collective-permute-start(bf16[4,8,16,128]{3,2,1,0:T(8,128)(2,1)S(1)} %fusion.2), channel_id=1, source_target_pairs={{0,32},{32,0},{1,33},{33,1},{2,34},{34,2},{3,35},{35,3},{4,36},{36... | collective-permute-start | bytes 393224 | tf_op jit(solution)/shard_map/ppermute | solution.py:243
  112.6 4.2 %collective-permute-done.10 = bf16[4,8,16,128]{3,2,1,0:T(8,128)(2,1)S(1)} collective-permute-done((bf16[4,8,16,128]{3,2,1,0:T(8,128)(2,1)S(1)}, bf16[4,8,16,128]{3,2,1,0:T(8,128)(2,1)S(1)}, u32[]{:S(2)}, u32[]{:S(2)}) %collective-permute-start.10) | collective-permute-done | bytes 131104 | tf_op jit(solution)/shard_map/ppermute | solution.py:243
  116.8 0.1 fusion.1
  116.9 43.5 %all_to_all.15.x_ref = bf16[32,144,128]{2,1,0:T(8,128)(2,1)} all-to-all(bf16[32,144,128]{2,1,0:T(8,128)(2,1)S(1)} %constant_dynamic-update-slice_fusion), channel_id=1, replica_groups=mesh['y'=4,'xh'=2,'z'=8,'xl'=2,'c'=2] {'z','xl','c'}, dimensions={0} | all-to-all | bytes 2359296 | tf_op jit(solution)/shard_map/all_to_all | solution.py:247
  160.3 3.6 %unpack.1 = (f32[16,4096]{1,0:T(8,128)}, f32[64,4096]{1,0:T(8,128)}, f32[64,4096]{1,0:T(8,128)}) custom-call(bf16[32,144,128]{2,1,0:T(8,128)(2,1)} %all_to_all.15.x_ref), custom_call_target="tpu_custom_call" | custom-call | flops 1000000 | bytes 3000000 | tf_op jit(solution)/shard_map/unpack/pallas_call | solution.py:226
  (2 shorter events, 0.0 us)
Async XLA Ops:
  3.2 23.7 %all-to-all-start = ((bf16[32,40,128]{2,1,0:T(8,128)(2,1)}), bf16[32,40,128]{2,1,0:T(8,128)(2,1)S(1)}, u32[]{:S(2)}, u32[]{:S(2)}) async-start(bf16[32,40,128]{2,1,0:T(8,128)(2,1)} %pack_queries.1), calls=%async_computation | async-start | bytes 655360 | tf_op jit(solution)/shard_map/all_to_all | solution.py:247
  16.6 44.4 %copy-start = (s32[8]{0:T(128)S(1)}, s32[8]{0:T(128)}, u32[]{:S(2)}) copy-start(s32[8]{0:T(128)} %constant.102.clone) | copy-start | bytes 100
  16.6 44.4 %copy-start.1 = (s32[8]{0:T(128)S(1)}, s32[8]{0:T(128)}, u32[]{:S(2)}) copy-start(s32[8]{0:T(128)} %constant.101.clone) | copy-start | bytes 100
  26.9 44.7 %all-to-all-start.1 = ((bf16[32,128,128]{2,1,0:T(8,128)(2,1)}), bf16[32,128,128]{2,1,0:T(8,128)(2,1)S(1)}, u32[]{:S(2)}, u32[]{:S(2)}) async-start(bf16[32,128,128]{2,1,0:T(8,128)(2,1)} %pack_keys.1), calls=%async_computation.1 | async-start | bytes 2097152 | tf_op jit(solution)/shard_map/all_to_all | solution.py:247
  31.9 17.0 %collective-permute-start = (bf16[32,40,128]{2,1,0:T(8,128)(2,1)S(1)}, bf16[32,40,128]{2,1,0:T(8,128)(2,1)S(1)}, u32[]{:S(2)}, u32[]{:S(2)}) collective-permute-start(bf16[32,40,128]{2,1,0:T(8,128)(2,1)S(1)} %all-to-all-done.refs_0_), channel_id=1, source_target_pairs={{0,32},{32,0},{1,33},{33,1},{2,34},{34,2},{3,35},{35,3},{4,36},{36... | collective-permute-start | bytes 983048 | tf_op jit(solution)/shard_map/ppermute | solution.py:243
  34.4 18.7 %collective-permute-start.1 = (bf16[32,40,128]{2,1,0:T(8,128)(2,1)S(1)}, bf16[32,40,128]{2,1,0:T(8,128)(2,1)S(1)}, u32[]{:S(2)}, u32[]{:S(2)}) collective-permute-start(bf16[32,40,128]{2,1,0:T(8,128)(2,1)S(1)} %all-to-all-done.refs_0_), channel_id=1, source_target_pairs={{0,64},{64,128},{128,192},{192,0},{1,65},{65,129},{129,193},{193,1... | collective-permute-start | bytes 983048 | tf_op jit(solution)/shard_map/ppermute | solution.py:243
  48.9 8.7 %collective-permute-start.4 = (bf16[32,40,128]{2,1,0:T(8,128)(2,1)S(1)}, bf16[32,40,128]{2,1,0:T(8,128)(2,1)S(1)}, u32[]{:S(2)}, u32[]{:S(2)}) collective-permute-start(bf16[32,40,128]{2,1,0:T(8,128)(2,1)S(1)} %collective-permute-done.refs_1_), channel_id=1, source_target_pairs={{0,192},{64,0},{128,64},{192,128},{1,193},{65,1},{129,65},{193,129... | collective-permute-start | bytes 983048 | tf_op jit(solution)/shard_map/ppermute | solution.py:243
  51.6 13.0 %collective-permute-start.3 = (bf16[32,40,128]{2,1,0:T(8,128)(2,1)S(1)}, bf16[32,40,128]{2,1,0:T(8,128)(2,1)S(1)}, u32[]{:S(2)}, u32[]{:S(2)}) collective-permute-start(bf16[32,40,128]{2,1,0:T(8,128)(2,1)S(1)} %all-to-all-done.refs_0_), channel_id=1, source_target_pairs={{0,192},{64,0},{128,64},{192,128},{1,193},{65,1},{129,65},{193,129... | collective-permute-start | bytes 983048 | tf_op jit(solution)/shard_map/ppermute | solution.py:243
  52.1 15.8 %collective-permute-start.2 = (bf16[32,40,128]{2,1,0:T(8,128)(2,1)S(1)}, bf16[32,40,128]{2,1,0:T(8,128)(2,1)S(1)}, u32[]{:S(2)}, u32[]{:S(2)}) collective-permute-start(bf16[32,40,128]{2,1,0:T(8,128)(2,1)S(1)} %collective-permute-done.refs_1_), channel_id=1, source_target_pairs={{0,64},{64,128},{128,192},{192,0},{1,65},{65,129},{129,193},{193,1... | collective-permute-start | bytes 983048 | tf_op jit(solution)/shard_map/ppermute | solution.py:243
  53.1 14.8 %collective-permute-start.5 = (bf16[32,40,128]{2,1,0:T(8,128)(2,1)S(1)}, bf16[32,40,128]{2,1,0:T(8,128)(2,1)S(1)}, u32[]{:S(2)}, u32[]{:S(2)}) collective-permute-start(bf16[32,40,128]{2,1,0:T(8,128)(2,1)S(1)} %collective-permute-done.1.refs_2_), channel_id=1, source_target_pairs={{0,64},{64,128},{128,192},{192,0},{1,65},{65,129},{129,193},{193,1... | collective-permute-start | bytes 983048 | tf_op jit(solution)/shard_map/ppermute | solution.py:243
  57.6 14.0 %collective-permute-start.6 = (bf16[32,40,128]{2,1,0:T(8,128)(2,1)S(1)}, bf16[32,40,128]{2,1,0:T(8,128)(2,1)}, u32[]{:S(2)}, u32[]{:S(2)}) collective-permute-start(bf16[32,40,128]{2,1,0:T(8,128)(2,1)S(1)} %collective-permute-done.4.refs_5_), channel_id=1, source_target_pairs={{0,192},{64,0},{128,64},{192,128},{1,193},{65,1},{129,65},{193,129... | collective-permute-start | bytes 983048 | tf_op jit(solution)/shard_map/ppermute | solution.py:243
  92.5 13.5 %collective-permute-start.9 = (bf16[2,4,8,16,128]{4,3,2,1,0:T(8,128)(2,1)S(1)}, bf16[2,4,8,16,128]{4,3,2,1,0:T(8,128)(2,1)S(1)}, u32[]{:S(2)}, u32[]{:S(2)}) collective-permute-start(bf16[2,4,8,16,128]{4,3,2,1,0:T(8,128)(2,1)S(1)} %get-tuple-element.20), channel_id=1, source_target_pairs={{0,192},{64,0},{128,64},{192,128},{1,193},{65,1},{129,65},{193,129... | collective-permute-start | bytes 786440 | tf_op jit(solution)/shard_map/ppermute | solution.py:243
  96.0 10.0 %collective-permute-start.7 = (bf16[2,4,8,16,128]{4,3,2,1,0:T(8,128)(2,1)S(1)}, bf16[2,4,8,16,128]{4,3,2,1,0:T(8,128)(2,1)S(1)}, u32[]{:S(2)}, u32[]{:S(2)}) collective-permute-start(bf16[2,4,8,16,128]{4,3,2,1,0:T(8,128)(2,1)S(1)} %get-tuple-element.18), channel_id=1, source_target_pairs={{0,128},{64,192},{128,0},{192,64},{1,129},{65,193},{129,1},{193,65... | collective-permute-start | bytes 786440 | tf_op jit(solution)/shard_map/ppermute | solution.py:243
  96.1 14.8 %collective-permute-start.8 = (bf16[2,4,8,16,128]{4,3,2,1,0:T(8,128)(2,1)S(1)}, bf16[2,4,8,16,128]{4,3,2,1,0:T(8,128)(2,1)S(1)}, u32[]{:S(2)}, u32[]{:S(2)}) collective-permute-start(bf16[2,4,8,16,128]{4,3,2,1,0:T(8,128)(2,1)S(1)} %get-tuple-element.19), channel_id=1, source_target_pairs={{0,64},{64,128},{128,192},{192,0},{1,65},{65,129},{129,193},{193,1... | collective-permute-start | bytes 786440 | tf_op jit(solution)/shard_map/ppermute | solution.py:243
  110.9 5.9 %collective-permute-start.10 = (bf16[4,8,16,128]{3,2,1,0:T(8,128)(2,1)S(1)}, bf16[4,8,16,128]{3,2,1,0:T(8,128)(2,1)S(1)}, u32[]{:S(2)}, u32[]{:S(2)}) collective-permute-start(bf16[4,8,16,128]{3,2,1,0:T(8,128)(2,1)S(1)} %fusion.2), channel_id=1, source_target_pairs={{0,32},{32,0},{1,33},{33,1},{2,34},{34,2},{3,35},{35,3},{4,36},{36... | collective-permute-start | bytes 393224 | tf_op jit(solution)/shard_map/ppermute | solution.py:243

commit v2 on v0

--- a/solution.py
+++ b/solution.py
@@ -22,8 +22,9 @@
 ROWS = QLEN // NSP
 SHARE = ROWS // NY
 GROUP = DH // SHARE
-WIDE = 2 * SHARE + 8
+WIDE = 2 * SHARE
 KROWS = KLEN // NSP
+KWIDE = 2 * KROWS + 8
 QB = QLEN // NKV
 QROWS = QB // NSP
 LOG2E = math.log2(math.e)
@@ -47,73 +48,94 @@
     return hi, mid, x - hi - mid
 
 
-def pack_queries(y_ref, group_ref, q_ref, g_ref, o_ref, s_ref, out_ref):
-    cols = []
+def pack_queries(y_ref, q_ref, g_ref, out_ref):
     for h in range(H):
         c = slice(h * DH, (h + 1) * DH)
         out_ref[h, 0:SHARE, :] = q_ref[:, c]
-        out_ref[h, SHARE : 2 * SHARE, :] = g_ref[:, c]
-        prod = g_ref[:, c].astype(F32) * o_ref[:, c].astype(F32)
-        cols.append(jnp.sum(prod, axis=1, keepdims=True))
-    delta = jnp.transpose(jnp.concatenate(cols, axis=1))
-    stats = s_ref[:, 0:SHARE]
-    for b in range(1, NY):
-        stats = jnp.where(y_ref[0] == b, s_ref[:, b * SHARE : (b + 1) * SHARE], stats)
-    lane = lax.broadcasted_iota(jnp.int32, (H, DH), 1)
-    here = lane // SHARE == group_ref[0]
-    row = lax.broadcasted_iota(jnp.int32, (H, 8, DH), 1)
-    tile = jnp.zeros((H, 8, DH), F32)
-    for r, x in enumerate(three(stats * LOG2E) + three(delta)):
-        x = jnp.where(here, jnp.concatenate([x] * GROUP, axis=1), 0.0)
-        tile = jnp.where(row == r, x[:, None, :], tile)
-    out_ref[:, 2 * SHARE : WIDE, :] = tile.astype(BF16)
-
-
-def packed_queries(y, group, queries, out_grad, outputs, stats):
-    wide = pl.BlockSpec((SHARE, H * DH), lambda i, y, g: (y[0], 0))
+        out_ref[h, SHARE:WIDE, :] = g_ref[:, c]
+
+
+def packed_queries(y, queries, out_grad):
+    wide = pl.BlockSpec((SHARE, H * DH), lambda i, y: (y[0], 0))
     return pl.pallas_call(
         pack_queries,
         grid_spec=pltpu.PrefetchScalarGridSpec(
-            num_scalar_prefetch=2,
+            num_scalar_prefetch=1,
             grid=(1,),
-            in_specs=[wide, wide, wide, pl.BlockSpec((H, ROWS), lambda i, y, g: (0, 0))],
-            out_specs=pl.BlockSpec((H, WIDE, DH), lambda i, y, g: (0, 0, 0)),
+            in_specs=[wide, wide],
+            out_specs=pl.BlockSpec((H, WIDE, DH), lambda i, y: (0, 0, 0)),
         ),
         out_shape=jax.ShapeDtypeStruct((H, WIDE, DH), BF16),
-        cost_estimate=cost(10**6, 2 * 10**6),
+        cost_estimate=cost(10**6, 10**6),
         name="pack_queries",
-    )(y, group, queries, out_grad, outputs, jnp.transpose(stats))
-
-
-def pack_keys(k_ref, v_ref, out_ref):
+    )(y, queries, out_grad)
+
+
+def pack_keys(y_ref, k_ref, v_ref, g_ref, o_ref, s_ref, out_ref):
+    cols = []
     for h in range(H):
         c = slice(h * DH, (h + 1) * DH)
         out_ref[h, 0:KROWS, :] = k_ref[:, c]
         out_ref[h, KROWS : 2 * KROWS, :] = v_ref[:, c]
-
-
-def packed_keys(keys, values):
+        prod = g_ref[:, c].astype(F32) * o_ref[:, c].astype(F32)
+        cols.append(jnp.sum(prod, axis=1, keepdims=True))
+    delta = jnp.transpose(jnp.concatenate(cols, axis=1))
+    row = lax.broadcasted_iota(jnp.int32, (H, 8, DH), 1)
+    tile = jnp.zeros((H, 8, DH), F32)
+    for r, x in enumerate(three(s_ref[...] * LOG2E) + three(delta)):
+        turned = x
+        for b in range(1, NY):
+            at = b * SHARE
+            turned = jnp.where(
+                y_ref[0] == b, jnp.concatenate([x[:, at:], x[:, :at]], axis=1), turned
+            )
+        tile = jnp.where(row == r, turned[:, None, :], tile)
+    out_ref[:, 2 * KROWS : KWIDE, :] = tile.astype(BF16)
+
+
+def packed_keys(y, keys, values, out_grad, outputs, stats):
+    def whole(*shape):
+        return pl.BlockSpec(shape, lambda i, y: (0,) * len(shape))
+
     return pl.pallas_call(
         pack_keys,
-        out_shape=jax.ShapeDtypeStruct((H, 2 * KROWS, DH), BF16),
-        cost_estimate=cost(10**6, 2 * 10**6),
+        grid_spec=pltpu.PrefetchScalarGridSpec(
+            num_scalar_prefetch=1,
+            grid=(1,),
+            in_specs=[whole(KROWS, H * DH)] * 2 + [whole(ROWS, H * DH)] * 2 + [whole(H, ROWS)],
+            out_specs=whole(H, KWIDE, DH),
+        ),
+        out_shape=jax.ShapeDtypeStruct((H, KWIDE, DH), BF16),
+        cost_estimate=cost(10**6, 4 * 10**6),
         name="pack_keys",
-    )(keys, values)
-
-
-def queries_of(parts):
+    )(y, keys, values, out_grad, outputs, jnp.transpose(stats))
+
+
+def in_lanes(x):
+    return jnp.concatenate(
+        [
+            x[s : s + 1, b * SHARE : (b + 1) * SHARE]
+            for b in range(NY)
+            for s in range(GROUP)
+        ],
+        axis=1,
+    )
+
+
+def queries_of(member, refs, kv_ref):
+    own, after, low, high, before = refs
+    far = jnp.where(member < NKV // 2, low[...], high[...])
+    parts = (own[...], after[...], far, before[...])
     q = jnp.concatenate([p[:, 0:SHARE, :].reshape(-1, DH) for p in parts], axis=0)
-    g = jnp.concatenate([p[:, SHARE : 2 * SHARE, :].reshape(-1, DH) for p in parts], axis=0)
-    st, de = [], []
-    for p in parts:
-        x = jnp.sum(p[:, 2 * SHARE : WIDE, :].astype(F32), axis=0)
-        st.append(x[0:1] + x[1:2] + x[2:3])
-        de.append(x[3:4] + x[4:5] + x[5:6])
-    return q, g, jnp.concatenate(st, axis=1), jnp.concatenate(de, axis=1)
-
-
-def block_grads(parts, kv_ref, dk_ref, dv_ref, per):
-    q, g, st, de = queries_of(parts)
+    g = jnp.concatenate([p[:, SHARE:WIDE, :].reshape(-1, DH) for p in parts], axis=0)
+    tile = kv_ref[pl.ds(member * GROUP, GROUP), 2 * KROWS : KWIDE, :].astype(F32)
+    st = tile[:, 0, :] + tile[:, 1, :] + tile[:, 2, :]
+    de = tile[:, 3, :] + tile[:, 4, :] + tile[:, 5, :]
+    return q, g, in_lanes(st), in_lanes(de)
+
+
+def block_grads(member, parts, kv_ref, dk_ref, dv_ref, per):
+    q, g, st, de = queries_of(member, parts, kv_ref)
     bk = per * KROWS
     total = None
     for j in range(NSP // per):
@@ -130,9 +152,9 @@
 
 
 def grads(count, first, last, tab, *refs):
-    parts = refs[:NY]
-    kv_ref = refs[NY]
-    rest = refs[NY + 1 :]
+    parts = refs[: NY + 1]
+    kv_ref = refs[NY + 1]
+    rest = refs[NY + 2 :]
     if not first:
         dk_in, dv_in = rest[:2]
         rest = rest[2:]
@@ -145,7 +167,7 @@
         dk_ref[...] = jnp.zeros_like(dk_ref) if first else dk_in[...]
         dv_ref[...] = jnp.zeros_like(dv_ref) if first else dv_in[...]
 
-    total = block_grads(parts, kv_ref, dk_ref, dv_ref, 8)
+    total = block_grads(tab[step], parts, kv_ref, dk_ref, dv_ref, 8)
     for n, dq_ref in enumerate(dq_refs):
 
         @pl.when(step // NX == n)
@@ -178,7 +200,11 @@
 
     whole = pl.BlockSpec((KLEN, DH), lambda i, t: (0, 0))
     part = pl.BlockSpec((GROUP, WIDE, DH), lambda i, t: (t[i], 0, 0))
-    in_specs = [part] * NY + [pl.BlockSpec((NSP, 2 * KROWS, DH), lambda i, t: (0, 0, 0))]
+    half = NKV // 2
+    low = pl.BlockSpec(part.block_shape, lambda i, t: (jnp.minimum(t[i], half - 1), 0, 0))
+    high = pl.BlockSpec(part.block_shape, lambda i, t: (jnp.maximum(t[i] - half, 0), 0, 0))
+    in_specs = [part, part, low, high, part]
+    in_specs.append(pl.BlockSpec((NSP, KWIDE, DH), lambda i, t: (0, 0, 0)))
     out_specs = [dq_spec(n) for n in range(count)]
     out_shape = [jax.ShapeDtypeStruct((NX, *DQ), F32 if last else BF16)] * count
     scratch = []
@@ -205,22 +231,34 @@
     )(tab, *parts, kv, *sums)
 
 
-def unpack(x_ref, dq_ref, dk_ref, dv_ref):
-    for h in range(H):
-        c = slice(h * DH, (h + 1) * DH)
-        dk_ref[:, c] = x_ref[h, 0:KROWS, :].astype(F32)
-        dv_ref[:, c] = x_ref[h, KROWS : 2 * KROWS, :].astype(F32)
-        dq_ref[:, c] = x_ref[h, 2 * KROWS : OUT_ROWS, :].astype(F32)
+def unpack(x_ref, *refs):
+    outs, bufs, sems = refs[:3], refs[3:6], refs[6]
+    copies = []
+    pieces = [(0, 0, QROWS, 2 * KROWS)]
+    for n in (1, 2):
+        for r in range(0, KROWS, KROWS // 2):
+            pieces.append((n, r, KROWS // 2, (n - 1) * KROWS + r))
+    for p, (n, r, rows, at) in enumerate(pieces):
+        for h in range(H):
+            bufs[n][r : r + rows, h * DH : (h + 1) * DH] = x_ref[h, at : at + rows, :].astype(F32)
+        copy = pltpu.make_async_copy(
+            bufs[n].at[r : r + rows], outs[n].at[r : r + rows], sems.at[p]
+        )
+        copy.start()
+        copies.append(copy)
+    for copy in copies:
+        copy.wait()
 
 
 def unpacked(x):
+    shapes = [(QROWS, H * DH), (KROWS, H * DH), (KROWS, H * DH)]
     return pl.pallas_call(
         unpack,
-        out_shape=[
-            jax.ShapeDtypeStruct((QROWS, H * DH), F32),
-            jax.ShapeDtypeStruct((KROWS, H * DH), F32),
-            jax.ShapeDtypeStruct((KROWS, H * DH), F32),
-        ],
+        in_specs=[pl.BlockSpec(memory_space=pltpu.VMEM)],
+        out_specs=[pl.BlockSpec(memory_space=pl.ANY)] * 3,
+        out_shape=[jax.ShapeDtypeStruct(shape, F32) for shape in shapes],
+        scratch_shapes=[pltpu.VMEM(shape, F32) for shape in shapes]
+        + [pltpu.SemaphoreType.DMA((5,))],
         cost_estimate=cost(10**6, 3 * 10**6),
         name="unpack",
     )(x)
@@ -238,11 +276,10 @@
 def body(queries, keys, values, outputs, out_grad, stats):
     y = lax.axis_index("y")
     xh = lax.axis_index("xh")
-    group = lax.axis_index("xl") * 2 + lax.axis_index("c")
-    at = (y.reshape(1).astype(jnp.int32), group.reshape(1).astype(jnp.int32))
-    own = packed_queries(*at, queries, out_grad, outputs, stats)
+    at = y.reshape(1).astype(jnp.int32)
+    own = packed_queries(at, queries, out_grad)
     own = regroup(own)
-    kv = packed_keys(keys, values)
+    kv = packed_keys(at, keys, values, out_grad, outputs, stats)
     kv = regroup(kv)
 
     half = NSP // 2
@@ -250,8 +287,8 @@
     after = shift(own, "y", -1)
     low = shift(before[:half], "y", 1)
     high = shift(after[half:], "y", -1)
-    parts = (own, before, after, jnp.concatenate([low, high], axis=0))
-    where = (y + jnp.array([0, 3, 1, 2], jnp.int32)) % NY
+    parts = (own, after, low, high, before)
+    where = (y + jnp.arange(NY, dtype=jnp.int32)) % NY
 
     def members(*dys):
         return [((y + dy) % NY) * NX + (xh + o) % NX for dy in dys for o in (1, 0)]

time: 151 us -> 148 us (0.980)
  blocking collectives: 39.4 us -> 36.5 us
  local copies, waits for them, and re-layouts: 2.86 us -> 0.84 us
  starting transfers between devices: 26.6 us -> 28.2 us
    ppermute x8, waiting for transfers between devices: 31.6 us -> 27.2 us  [shift(): return lax.ppermute(x, axis, [(i, (i + by) % n) for i in range(n)])]
    all_to_all x2, waiting for transfers between devices: 15.8 us -> 19.5 us  [regroup(): return lax.all_to_all(x, SP, split_axis=0, concat_axis=0, tiled=True)]
    all_to_all x1, blocking collectives: 39.4 us -> 36.5 us  [regroup(): return lax.all_to_all(x, SP, split_axis=0, concat_axis=0, tiled=True)]
  transfers between devices with their start and end apart: 10 -> 10, of which waited for: 5 -> 6; matrix products, arithmetic and copies ran while one was open for 2% -> 1% of each run, Pallas kernels for 6% -> 7%
where the time goes in v2:
time: 148 us
  waiting for transfers between devices  46.7 us (32%)
  blocking collectives  36.5 us (25%)
  Pallas kernels  34.2 us (23%)
  starting transfers between devices  28.2 us (19%)
    all_to_all x1, blocking collectives, regroup(): return lax.all_to_all(x, SP, split_axis=0, concat_axis=0, tiled=True)  36.5 us
    ppermute x8, waiting for transfers between devices, shift(): return lax.ppermute(x, axis, [(i, (i + by) % n) for i in range(n)])  27.2 us
    pallas_call x3, Pallas kernels, grads_call(): pl.pallas_call(functools.partial(grads, count, first, last), grid_spec=pl...  25.7 us
    all_to_all x2, waiting for transfers between devices, regroup(): return lax.all_to_all(x, SP, split_axis=0, concat_axis=0, tiled=True)  19.5 us
    all_to_all x2, starting transfers between devices, regroup(): return lax.all_to_all(x, SP, split_axis=0, concat_axis=0, tiled=True)  16 us
    ppermute x8, starting transfers between devices, shift(): return lax.ppermute(x, axis, [(i, (i + by) % n) for i in range(n)])  12.2 us
    pallas_call x1, Pallas kernels, packed_keys(): pl.pallas_call(pack_keys, grid_spec=pltpu.PrefetchScalarGridSpec(num_scal...  3.83 us
  transfers between devices with their start and end apart: 10, of which 6 were waited for; matrix products, arithmetic and copies ran while one was open for 1% of the time, Pallas kernels for 7%

profile of v2, /device:TPU:1, one launch (start us, length us, event | category | flops | bytes accessed | tf_op | source)
XLA Modules:
  0.0 147.6 jit_solution(417492078964066061)
XLA Ops:
  0.6 1.9 %pack_queries.1 = bf16[32,64,128]{2,1,0:T(8,128)(2,1)} custom-call(s32[1]{0:T(128)} %bitcast.2.y_ref, bf16[128,4096]{1,0:T(8,128)(2,1)} %q_ref.1, bf16[128,4096]{1,0:T(8,128)(2,1)} %g_ref.3), custom_call_target="tpu_custom_call" | custom-call | flops 1000000 | bytes 1000000 | tf_op jit(solution)/shard_map/pack_queries/pallas_call | solution.py:60
  2.6 11.0 %all-to-all-start = ((bf16[32,64,128]{2,1,0:T(8,128)(2,1)}), bf16[32,64,128]{2,1,0:T(8,128)(2,1)S(1)}, u32[]{:S(2)}, u32[]{:S(2)}) async-start(bf16[32,64,128]{2,1,0:T(8,128)(2,1)} %pack_queries.1), calls=%async_computation | async-start | bytes 1048576 | tf_op jit(solution)/shard_map/all_to_all | solution.py:273
  13.6 3.8 %pack_keys.1 = bf16[32,136,128]{2,1,0:T(8,128)(2,1)} custom-call(s32[1]{0:T(128)} %bitcast.2.y_ref, bf16[64,4096]{1,0:T(8,128)(2,1)} %k_ref.1, bf16[64,4096]{1,0:T(8,128)(2,1)} %v_ref.1, bf16[128,4096]{1,0:T(8,128)(2,1)} %g_ref.3, bf16[128,4096]{1,0:T(8,128)(2,1)} %o_ref.1, f32[32,128]{1,0:T(8,128)} %bitcast.20), custom_call_target="tpu_custom_call" | custom-call | flops 1000000 | bytes 4000000 | tf_op jit(solution)/shard_map/pack_keys/pallas_call | solution.py:100
  17.4 12.7 %all-to-all-done.refs_0_ = bf16[32,64,128]{2,1,0:T(8,128)(2,1)S(1)} async-done(((bf16[32,64,128]{2,1,0:T(8,128)(2,1)}), bf16[32,64,128]{2,1,0:T(8,128)(2,1)S(1)}, u32[]{:S(2)}, u32[]{:S(2)}) %all-to-all-start) | async-done | bytes 524320 | tf_op jit(solution)/shard_map/all_to_all | solution.py:273
  30.2 4.9 %all-to-all-start.1 = ((bf16[32,136,128]{2,1,0:T(8,128)(2,1)}), bf16[32,136,128]{2,1,0:T(8,128)(2,1)S(1)}, u32[]{:S(2)}, u32[]{:S(2)}) async-start(bf16[32,136,128]{2,1,0:T(8,128)(2,1)} %pack_keys.1), calls=%async_computation.1 | async-start | bytes 2228224 | tf_op jit(solution)/shard_map/all_to_all | solution.py:273
  35.1 1.4 collective-permute-start.1
  36.5 1.5 %collective-permute-start = (bf16[32,64,128]{2,1,0:T(8,128)(2,1)S(1)}, bf16[32,64,128]{2,1,0:T(8,128)(2,1)S(1)}, u32[]{:S(2)}, u32[]{:S(2)}) collective-permute-start(bf16[32,64,128]{2,1,0:T(8,128)(2,1)S(1)} %all-to-all-done.refs_0_), channel_id=1, source_target_pairs={{0,192},{64,0},{128,64},{192,128},{1,193},{65,1},{129,65},{193,129... | collective-permute-start | bytes 1572872 | tf_op jit(solution)/shard_map/ppermute | solution.py:269
  38.0 11.6 %collective-permute-done.1.refs_4_ = bf16[32,64,128]{2,1,0:T(8,128)(2,1)S(1)} collective-permute-done((bf16[32,64,128]{2,1,0:T(8,128)(2,1)S(1)}, bf16[32,64,128]{2,1,0:T(8,128)(2,1)S(1)}, u32[]{:S(2)}, u32[]{:S(2)}) %collective-permute-start.1) | collective-permute-done | bytes 524320 | tf_op jit(solution)/shard_map/ppermute | solution.py:269
  49.7 0.1 collective-permute-start.2
  49.7 0.0 collective-permute-done.refs_1_
  49.8 0.7 slice.41
  50.5 2.7 %collective-permute-start.3 = (bf16[16,64,128]{2,1,0:T(8,128)(2,1)}, bf16[16,64,128]{2,1,0:T(8,128)(2,1)S(1)}, u32[]{:S(2)}, u32[]{:S(2)}) collective-permute-start(bf16[16,64,128]{2,1,0:T(8,128)(2,1)} %slice.41), channel_id=1, source_target_pairs={{0,192},{64,0},{128,64},{192,128},{1,193},{65,1},{129,65},{193,129... | collective-permute-start | bytes 786440 | tf_op jit(solution)/shard_map/ppermute | solution.py:269
  53.1 0.1 concatenate.11.tab
  53.2 0.1 add_add_fusion.1
  53.3 4.4 %collective-permute-done.2.refs_2_ = bf16[16,64,128]{2,1,0:T(8,128)(2,1)S(1)} collective-permute-done((bf16[16,64,128]{2,1,0:T(8,128)(2,1)S(1)}, bf16[16,64,128]{2,1,0:T(8,128)(2,1)S(1)}, u32[]{:S(2)}, u32[]{:S(2)}) %collective-permute-start.2) | collective-permute-done | bytes 262176 | tf_op jit(solution)/shard_map/ppermute | solution.py:269
  57.7 0.0 collective-permute-done.3.refs_3_
  57.7 6.8 %all-to-all-done.1.refs_5_ = bf16[32,136,128]{2,1,0:T(8,128)(2,1)S(1)} async-done(((bf16[32,136,128]{2,1,0:T(8,128)(2,1)}), bf16[32,136,128]{2,1,0:T(8,128)(2,1)S(1)}, u32[]{:S(2)}, u32[]{:S(2)}) %all-to-all-start.1) | async-done | bytes 1114144 | tf_op jit(solution)/shard_map/all_to_all | solution.py:273
  64.5 12.5 %grads.3 = (bf16[2,4,4,32,128]{4,3,2,1,0:T(8,128)(2,1)S(1)}, bf16[2,4,4,32,128]{4,3,2,1,0:T(8,128)(2,1)S(1)}, f32[2048,128]{1,0:T(8,128)S(1)}, f32[2048,128]{1,0:T(8,128)S(1)}) custom-call(s32[8]{0:T(128)S(1)} %concatenate.11.tab, bf16[32,64,128]{2,1,0:T(8,128)(2,1)S(1)} %all-to-all-done.refs_0_, bf16[32,64,128]{2,1,0:T(8,128)(2,1)S(1)} %collective-permute-done.refs_1_, ...), custom_call_target="tpu_custom_call" | custom-call | flops 5368709120 | bytes 4194304 | tf_op jit(solution)/shard_map/grads/pallas_call | solution.py:218
  77.0 6.6 %grads.4 = (bf16[2,4,4,32,128]{4,3,2,1,0:T(8,128)(2,1)S(1)}, f32[2048,128]{1,0:T(8,128)S(1)}, f32[2048,128]{1,0:T(8,128)S(1)}) custom-call(s32[6]{0:T(128)S(1)} %get-tuple-element.21.tab, bf16[32,64,128]{2,1,0:T(8,128)(2,1)S(1)} %all-to-all-done.refs_0_, bf16[32,64,128]{2,1,0:T(8,128)(2,1)S(1)} %collective-permute-done.refs_1_, ...), custom_call_target="tpu_custom_call" | custom-call | flops 2684354560 | bytes 4194304 | tf_op jit(solution)/shard_map/grads/pallas_call | solution.py:218
  83.5 3.0 %collective-permute-start.6 = (bf16[2,4,4,32,128]{4,3,2,1,0:T(8,128)(2,1)S(1)}, bf16[2,4,4,32,128]{4,3,2,1,0:T(8,128)(2,1)S(1)}, u32[]{:S(2)}, u32[]{:S(2)}) collective-permute-start(bf16[2,4,4,32,128]{4,3,2,1,0:T(8,128)(2,1)S(1)} %get-tuple-element.20), channel_id=1, source_target_pairs={{0,192},{64,0},{128,64},{192,128},{1,193},{65,1},{129,65},{193,129... | collective-permute-start | bytes 786440 | tf_op jit(solution)/shard_map/ppermute | solution.py:269
  86.5 0.3 collective-permute-start.4
  86.9 0.7 collective-permute-start.5
  87.6 6.7 %grads.5 = (f32[2,4,4,32,128]{4,3,2,1,0:T(8,128)S(1)}, bf16[32,144,128]{2,1,0:T(8,128)(2,1)S(1)}) custom-call(s32[6]{0:T(128)S(1)} %get-tuple-element.22.tab, bf16[32,64,128]{2,1,0:T(8,128)(2,1)S(1)} %all-to-all-done.refs_0_, bf16[32,64,128]{2,1,0:T(8,128)(2,1)S(1)} %collective-permute-done.refs_1_, bf16[16,64,128]{2,1,0:T(8,128)(2,1)S(1)} %collective-permute-done.2.refs_2_, ...), custom_call_target="tpu_custom_call" | custom-call | flops 2684354560 | bytes 4194304 | tf_op jit(solution)/shard_map/grads/pallas_call | solution.py:218
  94.3 0.0 collective-permute-done.6
  94.3 0.0 collective-permute-done.4
  94.3 7.6 %collective-permute-done.5 = bf16[2,4,4,32,128]{4,3,2,1,0:T(8,128)(2,1)S(1)} collective-permute-done((bf16[2,4,4,32,128]{4,3,2,1,0:T(8,128)(2,1)S(1)}, bf16[2,4,4,32,128]{4,3,2,1,0:T(8,128)(2,1)S(1)}, u32[]{:S(2)}, u32[]{:S(2)}) %collective-permute-start.5) | collective-permute-done | bytes 262176 | tf_op jit(solution)/shard_map/ppermute | solution.py:269
  101.9 0.1 fusion.2
  102.0 2.5 %collective-permute-start.7 = (bf16[4,4,32,128]{3,2,1,0:T(8,128)(2,1)S(1)}, bf16[4,4,32,128]{3,2,1,0:T(8,128)(2,1)S(1)}, u32[]{:S(2)}, u32[]{:S(2)}) collective-permute-start(bf16[4,4,32,128]{3,2,1,0:T(8,128)(2,1)S(1)} %fusion.2), channel_id=1, source_target_pairs={{0,32},{32,0},{1,33},{33,1},{2,34},{34,2},{3,35},{35,3},{4,36},{36... | collective-permute-start | bytes 393224 | tf_op jit(solution)/shard_map/ppermute | solution.py:269
  104.5 3.6 %collective-permute-done.7 = bf16[4,4,32,128]{3,2,1,0:T(8,128)(2,1)S(1)} collective-permute-done((bf16[4,4,32,128]{3,2,1,0:T(8,128)(2,1)S(1)}, bf16[4,4,32,128]{3,2,1,0:T(8,128)(2,1)S(1)}, u32[]{:S(2)}, u32[]{:S(2)}) %collective-permute-start.7) | collective-permute-done | bytes 131104 | tf_op jit(solution)/shard_map/ppermute | solution.py:269
  108.1 0.1 fusion.1
  108.2 36.5 %all_to_all.15.x_ref = bf16[32,144,128]{2,1,0:T(8,128)(2,1)} all-to-all(bf16[32,144,128]{2,1,0:T(8,128)(2,1)S(1)} %constant_dynamic-update-slice_fusion), channel_id=1, replica_groups=mesh['y'=4,'xh'=2,'z'=8,'xl'=2,'c'=2] {'z','xl','c'}, dimensions={0} | all-to-all | bytes 2359296 | tf_op jit(solution)/shard_map/all_to_all | solution.py:273
  144.8 2.7 %unpack.1 = (f32[16,4096]{1,0:T(8,128)}, f32[64,4096]{1,0:T(8,128)}, f32[64,4096]{1,0:T(8,128)}) custom-call(bf16[32,144,128]{2,1,0:T(8,128)(2,1)} %all_to_all.15.x_ref), custom_call_target="tpu_custom_call" | custom-call | flops 1000000 | bytes 3000000 | tf_op jit(solution)/shard_map/unpack/pallas_call | solution.py:255
  (3 shorter events, 0.0 us)
Async XLA Ops:
  2.6 27.6 %all-to-all-start = ((bf16[32,64,128]{2,1,0:T(8,128)(2,1)}), bf16[32,64,128]{2,1,0:T(8,128)(2,1)S(1)}, u32[]{:S(2)}, u32[]{:S(2)}) async-start(bf16[32,64,128]{2,1,0:T(8,128)(2,1)} %pack_queries.1), calls=%async_computation | async-start | bytes 1048576 | tf_op jit(solution)/shard_map/all_to_all | solution.py:273
  30.2 34.3 %all-to-all-start.1 = ((bf16[32,136,128]{2,1,0:T(8,128)(2,1)}), bf16[32,136,128]{2,1,0:T(8,128)(2,1)S(1)}, u32[]{:S(2)}, u32[]{:S(2)}) async-start(bf16[32,136,128]{2,1,0:T(8,128)(2,1)} %pack_keys.1), calls=%async_computation.1 | async-start | bytes 2228224 | tf_op jit(solution)/shard_map/all_to_all | solution.py:273
  35.1 14.5 %collective-permute-start.1 = (bf16[32,64,128]{2,1,0:T(8,128)(2,1)S(1)}, bf16[32,64,128]{2,1,0:T(8,128)(2,1)S(1)}, u32[]{:S(2)}, u32[]{:S(2)}) collective-permute-start(bf16[32,64,128]{2,1,0:T(8,128)(2,1)S(1)} %all-to-all-done.refs_0_), channel_id=1, source_target_pairs={{0,64},{64,128},{128,192},{192,0},{1,65},{65,129},{129,193},{193,1... | collective-permute-start | bytes 1572872 | tf_op jit(solution)/shard_map/ppermute | solution.py:269
  36.5 13.3 %collective-permute-start = (bf16[32,64,128]{2,1,0:T(8,128)(2,1)S(1)}, bf16[32,64,128]{2,1,0:T(8,128)(2,1)S(1)}, u32[]{:S(2)}, u32[]{:S(2)}) collective-permute-start(bf16[32,64,128]{2,1,0:T(8,128)(2,1)S(1)} %all-to-all-done.refs_0_), channel_id=1, source_target_pairs={{0,192},{64,0},{128,64},{192,128},{1,193},{65,1},{129,65},{193,129... | collective-permute-start | bytes 1572872 | tf_op jit(solution)/shard_map/ppermute | solution.py:269
  49.7 8.0 %collective-permute-start.2 = (bf16[16,64,128]{2,1,0:T(8,128)(2,1)S(1)}, bf16[16,64,128]{2,1,0:T(8,128)(2,1)S(1)}, u32[]{:S(2)}, u32[]{:S(2)}) collective-permute-start(bf16[16,64,128]{2,1,0:T(8,128)(2,1)S(1)} %slice.40), channel_id=1, source_target_pairs={{0,64},{64,128},{128,192},{192,0},{1,65},{65,129},{129,193},{193,1... | collective-permute-start | bytes 786440 | tf_op jit(solution)/shard_map/ppermute | solution.py:269
  50.5 7.2 %collective-permute-start.3 = (bf16[16,64,128]{2,1,0:T(8,128)(2,1)}, bf16[16,64,128]{2,1,0:T(8,128)(2,1)S(1)}, u32[]{:S(2)}, u32[]{:S(2)}) collective-permute-start(bf16[16,64,128]{2,1,0:T(8,128)(2,1)} %slice.41), channel_id=1, source_target_pairs={{0,192},{64,0},{128,64},{192,128},{1,193},{65,1},{129,65},{193,129... | collective-permute-start | bytes 786440 | tf_op jit(solution)/shard_map/ppermute | solution.py:269
  83.5 10.7 %collective-permute-start.6 = (bf16[2,4,4,32,128]{4,3,2,1,0:T(8,128)(2,1)S(1)}, bf16[2,4,4,32,128]{4,3,2,1,0:T(8,128)(2,1)S(1)}, u32[]{:S(2)}, u32[]{:S(2)}) collective-permute-start(bf16[2,4,4,32,128]{4,3,2,1,0:T(8,128)(2,1)S(1)} %get-tuple-element.20), channel_id=1, source_target_pairs={{0,192},{64,0},{128,64},{192,128},{1,193},{65,1},{129,65},{193,129... | collective-permute-start | bytes 786440 | tf_op jit(solution)/shard_map/ppermute | solution.py:269
  86.5 7.8 %collective-permute-start.4 = (bf16[2,4,4,32,128]{4,3,2,1,0:T(8,128)(2,1)S(1)}, bf16[2,4,4,32,128]{4,3,2,1,0:T(8,128)(2,1)S(1)}, u32[]{:S(2)}, u32[]{:S(2)}) collective-permute-start(bf16[2,4,4,32,128]{4,3,2,1,0:T(8,128)(2,1)S(1)} %get-tuple-element.18), channel_id=1, source_target_pairs={{0,128},{64,192},{128,0},{192,64},{1,129},{65,193},{129,1},{193,65... | collective-permute-start | bytes 786440 | tf_op jit(solution)/shard_map/ppermute | solution.py:269
  86.9 15.0 %collective-permute-start.5 = (bf16[2,4,4,32,128]{4,3,2,1,0:T(8,128)(2,1)S(1)}, bf16[2,4,4,32,128]{4,3,2,1,0:T(8,128)(2,1)S(1)}, u32[]{:S(2)}, u32[]{:S(2)}) collective-permute-start(bf16[2,4,4,32,128]{4,3,2,1,0:T(8,128)(2,1)S(1)} %get-tuple-element.19), channel_id=1, source_target_pairs={{0,64},{64,128},{128,192},{192,0},{1,65},{65,129},{129,193},{193,1... | collective-permute-start | bytes 786440 | tf_op jit(solution)/shard_map/ppermute | solution.py:269
  102.0 6.2 %collective-permute-start.7 = (bf16[4,4,32,128]{3,2,1,0:T(8,128)(2,1)S(1)}, bf16[4,4,32,128]{3,2,1,0:T(8,128)(2,1)S(1)}, u32[]{:S(2)}, u32[]{:S(2)}) collective-permute-start(bf16[4,4,32,128]{3,2,1,0:T(8,128)(2,1)S(1)} %fusion.2), channel_id=1, source_target_pairs={{0,32},{32,0},{1,33},{33,1},{2,34},{34,2},{3,35},{35,3},{4,36},{36... | collective-permute-start | bytes 393224 | tf_op jit(solution)/shard_map/ppermute | solution.py:269

commit v3 on v2

--- a/solution.py
+++ b/solution.py
@@ -17,6 +17,7 @@
 NY, NX, NZ = 4, 2, 8
 NKV = NY * NX
 SP = ("z", "xl", "c")
+TURN = ("xl", "c", "z")
 ALL = ("y", "xh", "z", "xl", "c")
 NSP = 32
 ROWS = QLEN // NSP
@@ -124,23 +125,23 @@
 
 def queries_of(member, refs, kv_ref):
     own, after, low, high, before = refs
-    far = jnp.where(member < NKV // 2, low[...], high[...])
+    far = jnp.concatenate([low[...], high[...]], axis=0)
     parts = (own[...], after[...], far, before[...])
-    q = jnp.concatenate([p[:, 0:SHARE, :].reshape(-1, DH) for p in parts], axis=0)
-    g = jnp.concatenate([p[:, SHARE:WIDE, :].reshape(-1, DH) for p in parts], axis=0)
-    tile = kv_ref[pl.ds(member * GROUP, GROUP), 2 * KROWS : KWIDE, :].astype(F32)
+    q = jnp.concatenate([p[:, 0, 0:SHARE, :].reshape(-1, DH) for p in parts], axis=0)
+    g = jnp.concatenate([p[:, 0, SHARE:WIDE, :].reshape(-1, DH) for p in parts], axis=0)
+    tile = kv_ref[:, member, 2 * KROWS : KWIDE, :].astype(F32)
     st = tile[:, 0, :] + tile[:, 1, :] + tile[:, 2, :]
     de = tile[:, 3, :] + tile[:, 4, :] + tile[:, 5, :]
     return q, g, in_lanes(st), in_lanes(de)
 
 
-def block_grads(member, parts, kv_ref, dk_ref, dv_ref, per):
+def block_grads(member, parts, kv_ref, dk_ref, dv_ref):
     q, g, st, de = queries_of(member, parts, kv_ref)
-    bk = per * KROWS
+    bk = NKV * KROWS
     total = None
-    for j in range(NSP // per):
-        k = kv_ref[j * per : (j + 1) * per, 0:KROWS, :].reshape(bk, DH)
-        v = kv_ref[j * per : (j + 1) * per, KROWS : 2 * KROWS, :].reshape(bk, DH)
+    for j in range(GROUP):
+        k = kv_ref[j, :, 0:KROWS, :].reshape(bk, DH)
+        v = kv_ref[j, :, KROWS : 2 * KROWS, :].reshape(bk, DH)
         at = slice(j * bk, (j + 1) * bk)
         p = jnp.exp2(dot(k, q, ((1,), (1,))) * (ROOT * LOG2E) - st)
         ds = (p * (dot(v, g, ((1,), (1,))) - de)).astype(BF16)
@@ -167,7 +168,7 @@
         dk_ref[...] = jnp.zeros_like(dk_ref) if first else dk_in[...]
         dv_ref[...] = jnp.zeros_like(dv_ref) if first else dv_in[...]
 
-    total = block_grads(tab[step], parts, kv_ref, dk_ref, dv_ref, 8)
+    total = block_grads(tab[step], parts, kv_ref, dk_ref, dv_ref)
     for n, dq_ref in enumerate(dq_refs):
 
         @pl.when(step // NX == n)
@@ -199,12 +200,10 @@
         return pl.BlockSpec((1, *DQ), lambda i, t: (at(i), 0, 0, 0, 0))
 
     whole = pl.BlockSpec((KLEN, DH), lambda i, t: (0, 0))
-    part = pl.BlockSpec((GROUP, WIDE, DH), lambda i, t: (t[i], 0, 0))
-    half = NKV // 2
-    low = pl.BlockSpec(part.block_shape, lambda i, t: (jnp.minimum(t[i], half - 1), 0, 0))
-    high = pl.BlockSpec(part.block_shape, lambda i, t: (jnp.maximum(t[i] - half, 0), 0, 0))
-    in_specs = [part, part, low, high, part]
-    in_specs.append(pl.BlockSpec((NSP, KWIDE, DH), lambda i, t: (0, 0, 0)))
+    part = pl.BlockSpec((GROUP, 1, WIDE, DH), lambda i, t: (0, t[i], 0, 0))
+    half = pl.BlockSpec((GROUP // 2, 1, WIDE, DH), lambda i, t: (0, t[i], 0, 0))
+    in_specs = [part, part, half, half, part]
+    in_specs.append(pl.BlockSpec((GROUP, NKV, KWIDE, DH), lambda i, t: (0, 0, 0, 0)))
     out_specs = [dq_spec(n) for n in range(count)]
     out_shape = [jax.ShapeDtypeStruct((NX, *DQ), F32 if last else BF16)] * count
     scratch = []
@@ -259,6 +258,7 @@
         out_shape=[jax.ShapeDtypeStruct(shape, F32) for shape in shapes],
         scratch_shapes=[pltpu.VMEM(shape, F32) for shape in shapes]
         + [pltpu.SemaphoreType.DMA((5,))],
+        compiler_params=pltpu.CompilerParams(vmem_limit_bytes=8 << 20),
         cost_estimate=cost(10**6, 3 * 10**6),
         name="unpack",
     )(x)
@@ -270,7 +270,11 @@
 
 
 def regroup(x):
-    return lax.all_to_all(x, SP, split_axis=0, concat_axis=0, tiled=True)
+    return lax.all_to_all(x, TURN, split_axis=0, concat_axis=0, tiled=True)
+
+
+def by_z(x):
+    return x.reshape(-1, NZ, *x.shape[1:])
 
 
 def body(queries, keys, values, outputs, out_grad, stats):
@@ -287,7 +291,8 @@
     after = shift(own, "y", -1)
     low = shift(before[:half], "y", 1)
     high = shift(after[half:], "y", -1)
-    parts = (own, after, low, high, before)
+    parts = [by_z(x) for x in (own, after, low, high, before)]
+    kv = by_z(kv)
     where = (y + jnp.arange(NY, dtype=jnp.int32)) % NY
 
     def members(*dys):
@@ -306,6 +311,7 @@
     other = shift(other.astype(BF16), "xh", 1)
     mine = mine[1] + (far[1].astype(F32) + up[1].astype(F32) + down[1].astype(F32))
     mine = (mine + other.astype(F32)) * (ROOT * SCALE)
+    mine = jnp.swapaxes(mine.reshape(NZ, NSP // NZ, QROWS, DH), 0, 1)
     mine = mine.reshape(NSP, QROWS, DH).astype(BF16)
     packed = lax.dynamic_update_slice(packed, mine, (0, 2 * KROWS, 0))
     packed = regroup(packed)

time: 148 us -> 147 us (level)
  waiting for transfers between devices: 46.7 us -> 44.7 us
  blocking collectives: 36.5 us -> 38.1 us
    all_to_all x2, waiting for transfers between devices: 19.5 us -> 17.3 us  [regroup(): return lax.all_to_all(x, TURN, split_axis=0, concat_axis=0, tiled=True)]
    all_to_all x1, blocking collectives: 36.5 us -> 38.1 us  [regroup(): return lax.all_to_all(x, TURN, split_axis=0, concat_axis=0, tiled=True)]
  transfers between devices with their start and end apart: 10 -> 10, of which waited for: 6 -> 7; matrix products, arithmetic and copies ran while one was open for 1% -> 1% of each run, Pallas kernels for 7% -> 7%
where the time goes in v3:
time: 147 us
  waiting for transfers between devices  44.7 us (30%)
  blocking collectives  38.1 us (26%)
  Pallas kernels  33.7 us (23%)
  starting transfers between devices  28.4 us (19%)
    all_to_all x1, blocking collectives, regroup(): return lax.all_to_all(x, TURN, split_axis=0, concat_axis=0, tiled=True)  38.1 us
    ppermute x8, waiting for transfers between devices, shift(): return lax.ppermute(x, axis, [(i, (i + by) % n) for i in range(n)])  27.3 us
    pallas_call x3, Pallas kernels, grads_call(): pl.pallas_call(functools.partial(grads, count, first, last), grid_spec=pl...  26.4 us
    all_to_all x2, waiting for transfers between devices, regroup(): return lax.all_to_all(x, TURN, split_axis=0, concat_axis=0, tiled=True)  17.3 us
    all_to_all x2, starting transfers between devices, regroup(): return lax.all_to_all(x, TURN, split_axis=0, concat_axis=0, tiled=True)  16.2 us
    ppermute x8, starting transfers between devices, shift(): return lax.ppermute(x, axis, [(i, (i + by) % n) for i in range(n)])  12.2 us
    pallas_call x1, Pallas kernels, packed_keys(): pl.pallas_call(pack_keys, grid_spec=pltpu.PrefetchScalarGridSpec(num_scal...  3.83 us
  transfers between devices with their start and end apart: 10, of which 7 were waited for; matrix products, arithmetic and copies ran while one was open for 1% of the time, Pallas kernels for 7%

profile of v3, /device:TPU:1, one launch (start us, length us, event | category | flops | bytes accessed | tf_op | source)
XLA Modules:
  0.0 146.8 jit_solution(17439762047211375862)
XLA Ops:
  0.6 1.9 %pack_queries.1 = bf16[32,64,128]{2,1,0:T(8,128)(2,1)} custom-call(s32[1]{0:T(128)} %bitcast.2.y_ref, bf16[128,4096]{1,0:T(8,128)(2,1)} %q_ref.1, bf16[128,4096]{1,0:T(8,128)(2,1)} %g_ref.3), custom_call_target="tpu_custom_call" | custom-call | flops 1000000 | bytes 1000000 | tf_op jit(solution)/shard_map/pack_queries/pallas_call | solution.py:61
  2.6 11.0 %all-to-all-start = ((bf16[32,64,128]{2,1,0:T(8,128)(2,1)}), bf16[32,64,128]{2,1,0:T(8,128)(2,1)S(1)}, u32[]{:S(2)}, u32[]{:S(2)}) async-start(bf16[32,64,128]{2,1,0:T(8,128)(2,1)} %pack_queries.1), calls=%async_computation | async-start | bytes 1048576 | tf_op jit(solution)/shard_map/all_to_all | solution.py:273
  13.6 3.8 %pack_keys.1 = bf16[32,136,128]{2,1,0:T(8,128)(2,1)} custom-call(s32[1]{0:T(128)} %bitcast.2.y_ref, bf16[64,4096]{1,0:T(8,128)(2,1)} %k_ref.1, bf16[64,4096]{1,0:T(8,128)(2,1)} %v_ref.1, bf16[128,4096]{1,0:T(8,128)(2,1)} %g_ref.3, bf16[128,4096]{1,0:T(8,128)(2,1)} %o_ref.1, f32[32,128]{1,0:T(8,128)} %bitcast.48), custom_call_target="tpu_custom_call" | custom-call | flops 1000000 | bytes 4000000 | tf_op jit(solution)/shard_map/pack_keys/pallas_call | solution.py:101
  17.4 12.2 %all-to-all-done = bf16[32,64,128]{2,1,0:T(8,128)(2,1)S(1)} async-done(((bf16[32,64,128]{2,1,0:T(8,128)(2,1)}), bf16[32,64,128]{2,1,0:T(8,128)(2,1)S(1)}, u32[]{:S(2)}, u32[]{:S(2)}) %all-to-all-start) | async-done | bytes 524320 | tf_op jit(solution)/shard_map/all_to_all | solution.py:273
  29.7 5.1 %all-to-all-start.1 = ((bf16[32,136,128]{2,1,0:T(8,128)(2,1)}), bf16[32,136,128]{2,1,0:T(8,128)(2,1)S(1)}, u32[]{:S(2)}, u32[]{:S(2)}) async-start(bf16[32,136,128]{2,1,0:T(8,128)(2,1)} %pack_keys.1), calls=%async_computation.1 | async-start | bytes 2228224 | tf_op jit(solution)/shard_map/all_to_all | solution.py:273
  34.8 1.4 collective-permute-start.1
  36.2 1.5 %collective-permute-start = (bf16[32,64,128]{2,1,0:T(8,128)(2,1)S(1)}, bf16[32,64,128]{2,1,0:T(8,128)(2,1)S(1)}, u32[]{:S(2)}, u32[]{:S(2)}) collective-permute-start(bf16[32,64,128]{2,1,0:T(8,128)(2,1)S(1)} %all-to-all-done), channel_id=1, source_target_pairs={{0,192},{64,0},{128,64},{192,128},{1,193},{65,1},{129,65},{193,129... | collective-permute-start | bytes 1572872 | tf_op jit(solution)/shard_map/ppermute | solution.py:269
  37.7 11.8 %collective-permute-done.1 = bf16[32,64,128]{2,1,0:T(8,128)(2,1)S(1)} collective-permute-done((bf16[32,64,128]{2,1,0:T(8,128)(2,1)S(1)}, bf16[32,64,128]{2,1,0:T(8,128)(2,1)S(1)}, u32[]{:S(2)}, u32[]{:S(2)}) %collective-permute-start.1) | collective-permute-done | bytes 524320 | tf_op jit(solution)/shard_map/ppermute | solution.py:269
  49.5 0.1 collective-permute-start.2
  49.6 0.0 collective-permute-done
  49.6 0.7 slice.41
  50.3 2.7 %collective-permute-start.3 = (bf16[16,64,128]{2,1,0:T(8,128)(2,1)}, bf16[16,64,128]{2,1,0:T(8,128)(2,1)S(1)}, u32[]{:S(2)}, u32[]{:S(2)}) collective-permute-start(bf16[16,64,128]{2,1,0:T(8,128)(2,1)} %slice.41), channel_id=1, source_target_pairs={{0,192},{64,0},{128,64},{192,128},{1,193},{65,1},{129,65},{193,129... | collective-permute-start | bytes 786440 | tf_op jit(solution)/shard_map/ppermute | solution.py:269
  53.0 0.1 concatenate.11.tab
  53.1 0.1 add_add_fusion.1
  53.1 4.5 %collective-permute-done.2 = bf16[16,64,128]{2,1,0:T(8,128)(2,1)S(1)} collective-permute-done((bf16[16,64,128]{2,1,0:T(8,128)(2,1)S(1)}, bf16[16,64,128]{2,1,0:T(8,128)(2,1)S(1)}, u32[]{:S(2)}, u32[]{:S(2)}) %collective-permute-start.2) | collective-permute-done | bytes 262176 | tf_op jit(solution)/shard_map/ppermute | solution.py:269
  57.6 0.0 collective-permute-done.3
  57.6 5.1 %all-to-all-done.1 = bf16[32,136,128]{2,1,0:T(8,128)(2,1)S(1)} async-done(((bf16[32,136,128]{2,1,0:T(8,128)(2,1)}), bf16[32,136,128]{2,1,0:T(8,128)(2,1)S(1)}, u32[]{:S(2)}, u32[]{:S(2)}) %all-to-all-start.1) | async-done | bytes 1114144 | tf_op jit(solution)/shard_map/all_to_all | solution.py:273
  62.7 12.8 %grads.3 = (bf16[2,4,4,32,128]{4,3,2,1,0:T(8,128)(2,1)S(1)}, bf16[2,4,4,32,128]{4,3,2,1,0:T(8,128)(2,1)S(1)}, f32[2048,128]{1,0:T(8,128)S(1)}, f32[2048,128]{1,0:T(8,128)S(1)}) custom-call(s32[8]{0:T(128)S(1)} %concatenate.11.tab, bf16[4,8,64,128]{3,2,1,0:T(8,128)(2,1)S(1)} %bitcast.31, bf16[4,8,64,128]{3,2,1,0:T(8,128)(2,1)S(1)} %bitcast.37, ...), custom_call_target="tpu_custom_call" | custom-call | flops 5368709120 | bytes 4194304 | tf_op jit(solution)/shard_map/grads/pallas_call | solution.py:217
  75.6 6.8 %grads.4 = (bf16[2,4,4,32,128]{4,3,2,1,0:T(8,128)(2,1)S(1)}, f32[2048,128]{1,0:T(8,128)S(1)}, f32[2048,128]{1,0:T(8,128)S(1)}) custom-call(s32[6]{0:T(128)S(1)} %get-tuple-element.21.tab, bf16[4,8,64,128]{3,2,1,0:T(8,128)(2,1)S(1)} %bitcast.32, bf16[4,8,64,128]{3,2,1,0:T(8,128)(2,1)S(1)} %bitcast.38, bf16[2,8,64,128]{3,2,1,0:T(8,128)(2,1)S(1)} %bitcast.41, ...), custom_call_target="tpu_custom_call" | custom-call | flops 2684354560 | bytes 4194304 | tf_op jit(solution)/shard_map/grads/pallas_call | solution.py:217
  82.3 3.0 %collective-permute-start.6 = (bf16[2,4,4,32,128]{4,3,2,1,0:T(8,128)(2,1)S(1)}, bf16[2,4,4,32,128]{4,3,2,1,0:T(8,128)(2,1)S(1)}, u32[]{:S(2)}, u32[]{:S(2)}) collective-permute-start(bf16[2,4,4,32,128]{4,3,2,1,0:T(8,128)(2,1)S(1)} %get-tuple-element.20), channel_id=1, source_target_pairs={{0,192},{64,0},{128,64},{192,128},{1,193},{65,1},{129,65},{193,129... | collective-permute-start | bytes 786440 | tf_op jit(solution)/shard_map/ppermute | solution.py:269
  85.3 0.4 collective-permute-start.4
  85.7 0.7 collective-permute-start.5
  86.4 6.9 %grads.5 = (f32[2,4,4,32,128]{4,3,2,1,0:T(8,128)S(1)}, bf16[32,144,128]{2,1,0:T(8,128)(2,1)S(1)}) custom-call(s32[6]{0:T(128)S(1)} %get-tuple-element.22.tab, bf16[4,8,64,128]{3,2,1,0:T(8,128)(2,1)S(1)} %bitcast.33, bf16[4,8,64,128]{3,2,1,0:T(8,128)(2,1)S(1)} %bitcast.39, bf16[2,8,64,128]{3,2,1,0:T(8,128)(2,1)S(1)} %bitcast.42, ...), custom_call_target="tpu_custom_call" | custom-call | flops 2684354560 | bytes 4194304 | tf_op jit(solution)/shard_map/grads/pallas_call | solution.py:217
  93.2 3.5 %collective-permute-done.6 = bf16[2,4,4,32,128]{4,3,2,1,0:T(8,128)(2,1)S(1)} collective-permute-done((bf16[2,4,4,32,128]{4,3,2,1,0:T(8,128)(2,1)S(1)}, bf16[2,4,4,32,128]{4,3,2,1,0:T(8,128)(2,1)S(1)}, u32[]{:S(2)}, u32[]{:S(2)}) %collective-permute-start.6) | collective-permute-done | bytes 262176 | tf_op jit(solution)/shard_map/ppermute | solution.py:269
  96.7 0.0 collective-permute-done.4
  96.7 4.0 %collective-permute-done.5 = bf16[2,4,4,32,128]{4,3,2,1,0:T(8,128)(2,1)S(1)} collective-permute-done((bf16[2,4,4,32,128]{4,3,2,1,0:T(8,128)(2,1)S(1)}, bf16[2,4,4,32,128]{4,3,2,1,0:T(8,128)(2,1)S(1)}, u32[]{:S(2)}, u32[]{:S(2)}) %collective-permute-start.5) | collective-permute-done | bytes 262176 | tf_op jit(solution)/shard_map/ppermute | solution.py:269
  100.7 0.1 fusion.2
  100.8 2.5 %collective-permute-start.7 = (bf16[4,4,32,128]{3,2,1,0:T(8,128)(2,1)S(1)}, bf16[4,4,32,128]{3,2,1,0:T(8,128)(2,1)S(1)}, u32[]{:S(2)}, u32[]{:S(2)}) collective-permute-start(bf16[4,4,32,128]{3,2,1,0:T(8,128)(2,1)S(1)} %fusion.2), channel_id=1, source_target_pairs={{0,32},{32,0},{1,33},{33,1},{2,34},{34,2},{3,35},{35,3},{4,36},{36... | collective-permute-start | bytes 393224 | tf_op jit(solution)/shard_map/ppermute | solution.py:269
  103.3 3.6 %collective-permute-done.7 = bf16[4,4,32,128]{3,2,1,0:T(8,128)(2,1)S(1)} collective-permute-done((bf16[4,4,32,128]{3,2,1,0:T(8,128)(2,1)S(1)}, bf16[4,4,32,128]{3,2,1,0:T(8,128)(2,1)S(1)}, u32[]{:S(2)}, u32[]{:S(2)}) %collective-permute-start.7) | collective-permute-done | bytes 131104 | tf_op jit(solution)/shard_map/ppermute | solution.py:269
  106.9 0.1 fusion.1
  107.1 38.1 %all_to_all.15.x_ref = bf16[32,144,128]{2,1,0:T(8,128)(2,1)S(1)} all-to-all(bf16[32,144,128]{2,1,0:T(8,128)(2,1)S(1)} %constant_dynamic-update-slice_fusion), channel_id=1, replica_groups=mesh['y'=4,'xh'=2,'z'=8,'xl'=2,'c'=2] {'xl','c','z'}, dimensions={0} | all-to-all | bytes 2359296 | tf_op jit(solution)/shard_map/all_to_all | solution.py:273
  145.1 1.5 unpack.1
  (4 shorter events, 0.1 us)
Async XLA Ops:
  2.6 27.1 %all-to-all-start = ((bf16[32,64,128]{2,1,0:T(8,128)(2,1)}), bf16[32,64,128]{2,1,0:T(8,128)(2,1)S(1)}, u32[]{:S(2)}, u32[]{:S(2)}) async-start(bf16[32,64,128]{2,1,0:T(8,128)(2,1)} %pack_queries.1), calls=%async_computation | async-start | bytes 1048576 | tf_op jit(solution)/shard_map/all_to_all | solution.py:273
  29.7 33.1 %all-to-all-start.1 = ((bf16[32,136,128]{2,1,0:T(8,128)(2,1)}), bf16[32,136,128]{2,1,0:T(8,128)(2,1)S(1)}, u32[]{:S(2)}, u32[]{:S(2)}) async-start(bf16[32,136,128]{2,1,0:T(8,128)(2,1)} %pack_keys.1), calls=%async_computation.1 | async-start | bytes 2228224 | tf_op jit(solution)/shard_map/all_to_all | solution.py:273
  34.8 14.7 %collective-permute-start.1 = (bf16[32,64,128]{2,1,0:T(8,128)(2,1)S(1)}, bf16[32,64,128]{2,1,0:T(8,128)(2,1)S(1)}, u32[]{:S(2)}, u32[]{:S(2)}) collective-permute-start(bf16[32,64,128]{2,1,0:T(8,128)(2,1)S(1)} %all-to-all-done), channel_id=1, source_target_pairs={{0,64},{64,128},{128,192},{192,0},{1,65},{65,129},{129,193},{193,1... | collective-permute-start | bytes 1572872 | tf_op jit(solution)/shard_map/ppermute | solution.py:269
  36.2 13.4 %collective-permute-start = (bf16[32,64,128]{2,1,0:T(8,128)(2,1)S(1)}, bf16[32,64,128]{2,1,0:T(8,128)(2,1)S(1)}, u32[]{:S(2)}, u32[]{:S(2)}) collective-permute-start(bf16[32,64,128]{2,1,0:T(8,128)(2,1)S(1)} %all-to-all-done), channel_id=1, source_target_pairs={{0,192},{64,0},{128,64},{192,128},{1,193},{65,1},{129,65},{193,129... | collective-permute-start | bytes 1572872 | tf_op jit(solution)/shard_map/ppermute | solution.py:269
  49.5 8.1 %collective-permute-start.2 = (bf16[16,64,128]{2,1,0:T(8,128)(2,1)S(1)}, bf16[16,64,128]{2,1,0:T(8,128)(2,1)S(1)}, u32[]{:S(2)}, u32[]{:S(2)}) collective-permute-start(bf16[16,64,128]{2,1,0:T(8,128)(2,1)S(1)} %slice.40), channel_id=1, source_target_pairs={{0,64},{64,128},{128,192},{192,0},{1,65},{65,129},{129,193},{193,1... | collective-permute-start | bytes 786440 | tf_op jit(solution)/shard_map/ppermute | solution.py:269
  50.3 7.3 %collective-permute-start.3 = (bf16[16,64,128]{2,1,0:T(8,128)(2,1)}, bf16[16,64,128]{2,1,0:T(8,128)(2,1)S(1)}, u32[]{:S(2)}, u32[]{:S(2)}) collective-permute-start(bf16[16,64,128]{2,1,0:T(8,128)(2,1)} %slice.41), channel_id=1, source_target_pairs={{0,192},{64,0},{128,64},{192,128},{1,193},{65,1},{129,65},{193,129... | collective-permute-start | bytes 786440 | tf_op jit(solution)/shard_map/ppermute | solution.py:269
  82.3 14.4 %collective-permute-start.6 = (bf16[2,4,4,32,128]{4,3,2,1,0:T(8,128)(2,1)S(1)}, bf16[2,4,4,32,128]{4,3,2,1,0:T(8,128)(2,1)S(1)}, u32[]{:S(2)}, u32[]{:S(2)}) collective-permute-start(bf16[2,4,4,32,128]{4,3,2,1,0:T(8,128)(2,1)S(1)} %get-tuple-element.20), channel_id=1, source_target_pairs={{0,192},{64,0},{128,64},{192,128},{1,193},{65,1},{129,65},{193,129... | collective-permute-start | bytes 786440 | tf_op jit(solution)/shard_map/ppermute | solution.py:269
  85.3 11.4 %collective-permute-start.4 = (bf16[2,4,4,32,128]{4,3,2,1,0:T(8,128)(2,1)S(1)}, bf16[2,4,4,32,128]{4,3,2,1,0:T(8,128)(2,1)S(1)}, u32[]{:S(2)}, u32[]{:S(2)}) collective-permute-start(bf16[2,4,4,32,128]{4,3,2,1,0:T(8,128)(2,1)S(1)} %get-tuple-element.18), channel_id=1, source_target_pairs={{0,128},{64,192},{128,0},{192,64},{1,129},{65,193},{129,1},{193,65... | collective-permute-start | bytes 786440 | tf_op jit(solution)/shard_map/ppermute | solution.py:269
  85.7 15.0 %collective-permute-start.5 = (bf16[2,4,4,32,128]{4,3,2,1,0:T(8,128)(2,1)S(1)}, bf16[2,4,4,32,128]{4,3,2,1,0:T(8,128)(2,1)S(1)}, u32[]{:S(2)}, u32[]{:S(2)}) collective-permute-start(bf16[2,4,4,32,128]{4,3,2,1,0:T(8,128)(2,1)S(1)} %get-tuple-element.19), channel_id=1, source_target_pairs={{0,64},{64,128},{128,192},{192,0},{1,65},{65,129},{129,193},{193,1... | collective-permute-start | bytes 786440 | tf_op jit(solution)/shard_map/ppermute | solution.py:269
  100.8 6.2 %collective-permute-start.7 = (bf16[4,4,32,128]{3,2,1,0:T(8,128)(2,1)S(1)}, bf16[4,4,32,128]{3,2,1,0:T(8,128)(2,1)S(1)}, u32[]{:S(2)}, u32[]{:S(2)}) collective-permute-start(bf16[4,4,32,128]{3,2,1,0:T(8,128)(2,1)S(1)} %fusion.2), channel_id=1, source_target_pairs={{0,32},{32,0},{1,33},{33,1},{2,34},{34,2},{3,35},{35,3},{4,36},{36... | collective-permute-start | bytes 393224 | tf_op jit(solution)/shard_map/ppermute | solution.py:269

commit v4 on v0

v4 whole, which is shorter than its diff:
```python
import functools
import math

import jax
import jax.numpy as jnp
from jax import lax
from jax.experimental import pallas as pl
from jax.experimental.pallas import tpu as pltpu
from jax.sharding import Mesh
from jax.sharding import PartitionSpec as P


H = 32
DH = 128
QLEN = 4096
KLEN = 2048
NY, NX, NZ = 4, 2, 8
NKV = NY * NX
SP = ("z", "xl", "c")
ALL = ("y", "xh", "z", "xl", "c")
PLANE = ("xl", "c", "y", "xh")
NSP = 32
NXC = 4
ROWS = QLEN // NSP
SHARE = ROWS // NKV
WIDE = 2 * SHARE
TALL = WIDE + 8
KROWS = KLEN // NSP
QB = QLEN // NZ
PART = QB // NZ
QROWS = QB // NSP
LOG2E = math.log2(math.e)
ROOT = 1.0 / math.sqrt(DH)
SCALE = 1.0 / (KLEN * NKV)
F32 = jnp.float32
BF16 = jnp.bfloat16


def dot(a, b, dims):
    return lax.dot_general(a, b, ((dims[0], dims[1]), ((), ())), preferred_element_type=F32)


def cost(flops, size, trans=0):
    return pl.CostEstimate(flops=flops, bytes_accessed=size, transcendentals=trans)


def three(x):
    hi = x.astype(BF16).astype(F32)
    mid = (x - hi).astype(BF16).astype(F32)
    return hi, mid, x - hi - mid


def pack_queries(b_ref, q_ref, g_ref, o_ref, s_ref, out_ref):
    cols = []
    for h in range(H):
        c = slice(h * DH, (h + 1) * DH)
        out_ref[h, 0:SHARE, :] = q_ref[:, c]
        out_ref[h, SHARE:WIDE, :] = g_ref[:, c]
        prod = g_ref[:, c].astype(F32) * o_ref[:, c].astype(F32)
        cols.append(jnp.sum(prod, axis=1, keepdims=True))
    delta = jnp.transpose(jnp.concatenate(cols, axis=1))
    lane = lax.broadcasted_iota(jnp.int32, (H, DH), 1)
    here = lane // SHARE == b_ref[0]
    row = lax.broadcasted_iota(jnp.int32, (H, 8, DH), 1)
    tile = jnp.zeros((H, 8, DH), F32)
    delta = jnp.concatenate([delta] * NKV, axis=1)
    for r, x in enumerate(three(s_ref[...] * LOG2E) + three(delta)):
        x = jnp.where(here, x, 0.0)
        tile = jnp.where(row == r, x[:, None, :], tile)
    out_ref[:, WIDE:TALL, :] = tile.astype(BF16)


def packed_queries(b, queries, out_grad, outputs, stats):
    wide = pl.BlockSpec((SHARE, H * DH), lambda i, b: (b[0], 0))
    return pl.pallas_call(
        pack_queries,
        grid_spec=pltpu.PrefetchScalarGridSpec(
            num_scalar_prefetch=1,
            grid=(1,),
            in_specs=[wide, wide, wide, pl.BlockSpec((H, ROWS), lambda i, b: (0, 0))],
            out_specs=pl.BlockSpec((H, TALL, DH), lambda i, b: (0, 0, 0)),
        ),
        out_shape=jax.ShapeDtypeStruct((H, TALL, DH), BF16),
        cost_estimate=cost(10**6, 10**6),
        name="pack_queries",
    )(b, queries, out_grad, outputs, jnp.transpose(stats))


def gather_stats(x_ref, out_ref):
    out_ref[0:NSP] = x_ref[:, 0:WIDE, :]
    tile = x_ref[:, WIDE:TALL, :].astype(F32).reshape(NXC, NKV, 8, DH)
    out_ref[NSP] = jnp.sum(tile, axis=1).reshape(WIDE, DH).astype(BF16)


def with_stats(x):
    return pl.pallas_call(
        gather_stats,
        out_shape=jax.ShapeDtypeStruct((NSP + 1, WIDE, DH), BF16),
        compiler_params=pltpu.CompilerParams(vmem_limit_bytes=8 << 20),
        cost_estimate=cost(10**6, 10**6),
        name="gather_stats",
    )(x)


def pack_keys(k_ref, v_ref, out_ref):
    for h in range(H):
        c = slice(h * DH, (h + 1) * DH)
        out_ref[h, 0:KROWS, :] = k_ref[:, c]
        out_ref[h, KROWS : 2 * KROWS, :] = v_ref[:, c]


def packed_keys(keys, values):
    return pl.pallas_call(
        pack_keys,
        out_shape=jax.ShapeDtypeStruct((H, 2 * KROWS, DH), BF16),
        cost_estimate=cost(10**6, 2 * 10**6),
        name="pack_keys",
    )(keys, values)


def queries_of(to_z, parts, tiles):
    q = jnp.concatenate([p[:, 0:SHARE, :].reshape(PART, DH) for p in parts], axis=0)
    g = jnp.concatenate([p[:, SHARE:WIDE, :].reshape(PART, DH) for p in parts], axis=0)
    st, de = [], []
    for tile in tiles:
        x = tile[0].astype(F32)
        x = jnp.where(to_z % 2 == 0, x[:, :PART], x[:, PART:])
        st.append(x[0:1] + x[1:2] + x[2:3])
        de.append(x[3:4] + x[4:5] + x[5:6])
    return q, g, jnp.concatenate(st, axis=1), jnp.concatenate(de, axis=1)


def block_grads(to_z, parts, tiles, kv_ref, dk_ref, dv_ref):
    q, g, st, de = queries_of(to_z, parts, tiles)
    per = 8
    bk = per * KROWS
    total = None
    for j in range(NSP // per):
        k = kv_ref[j * per : (j + 1) * per, 0:KROWS, :].reshape(bk, DH)
        v = kv_ref[j * per : (j + 1) * per, KROWS : 2 * KROWS, :].reshape(bk, DH)
        at = slice(j * bk, (j + 1) * bk)
        p = jnp.exp2(dot(k, q, ((1,), (1,))) * (ROOT * LOG2E) - st)
        ds = (p * (dot(v, g, ((1,), (1,))) - de)).astype(BF16)
        dv_ref[at, :] += dot(p.astype(BF16), g, ((1,), (0,)))
        dk_ref[at, :] += dot(ds, q, ((1,), (0,)))
        part = dot(ds, k, ((0,), (0,)))
        total = part if total is None else total + part
    return total.reshape(NZ, PART, DH)


def grads(count, first, last, tab, *refs):
    parts = refs[:NZ]
    tiles = refs[NZ : 2 * NZ]
    kv_ref = refs[2 * NZ]
    rest = refs[2 * NZ + 1 :]
    if not first:
        dk_in, dv_in = rest[:2]
        rest = rest[2:]
    dq_refs = rest[:count]
    dk_ref, dv_ref = rest[-2:]
    step = pl.program_id(0)

    @pl.when(step == 0)
    def _():
        dk_ref[...] = jnp.zeros_like(dk_ref) if first else dk_in[...]
        dv_ref[...] = jnp.zeros_like(dv_ref) if first else dv_in[...]

    total = block_grads(tab[step], parts, tiles, kv_ref, dk_ref, dv_ref)
    for n, dq_ref in enumerate(dq_refs):

        @pl.when(step == n)
        def _(dq_ref=dq_ref):
            for j in range(NZ):
                dq_ref[tab[count + j]] = total[j].astype(dq_ref.dtype)

    if last:
        out_ref = rest[count]

        @pl.when(step == count - 1)
        def _():
            dk = (dk_ref[...] * (ROOT * SCALE)).astype(BF16)
            dv = (dv_ref[...] * SCALE).astype(BF16)
            out_ref[:, 0:KROWS, :] = dk.reshape(NSP, KROWS, DH)
            out_ref[:, KROWS : 2 * KROWS, :] = dv.reshape(NSP, KROWS, DH)


OUT_ROWS = 2 * KROWS + QROWS


def grads_call(count, first, last, tab, parts, kv, sums=()):
    pairs = count * QB * KLEN
    whole = pl.BlockSpec((KLEN, DH), lambda i, t: (0, 0))
    part = pl.BlockSpec((PART // SHARE, WIDE, DH), lambda i, t: (t[i], 0, 0))
    tile = pl.BlockSpec((1, 8, DH), lambda i, t: (NSP, t[i] // 2, 0))
    in_specs = [part] * NZ + [tile] * NZ
    in_specs.append(pl.BlockSpec((NSP, 2 * KROWS, DH), lambda i, t: (0, 0, 0)))
    out_specs = [pl.BlockSpec((NZ, PART, DH), lambda i, t: (0, 0, 0))] * count
    out_shape = [jax.ShapeDtypeStruct((NZ, PART, DH), F32 if last else BF16)] * count
    scratch = []
    if last:
        out_specs.append(pl.BlockSpec((NSP, OUT_ROWS, DH), lambda i, t: (0, 0, 0)))
        out_shape.append(jax.ShapeDtypeStruct((NSP, OUT_ROWS, DH), BF16))
        scratch = [pltpu.VMEM((KLEN, DH), F32)] * 2
    else:
        out_specs += [whole] * 2
        out_shape += [jax.ShapeDtypeStruct((KLEN, DH), F32)] * 2
    return pl.pallas_call(
        functools.partial(grads, count, first, last),
        grid_spec=pltpu.PrefetchScalarGridSpec(
            num_scalar_prefetch=1,
            grid=(count,),
            in_specs=in_specs + [whole] * len(sums),
            out_specs=out_specs,
            scratch_shapes=scratch,
        ),
        out_shape=out_shape,
        compiler_params=pltpu.CompilerParams(vmem_limit_bytes=26 << 20),
        cost_estimate=cost(pairs * 10 * DH, 4 << 20, pairs),
        name="grads",
    )(tab, *parts, *parts, kv, *sums)


def unpack(x_ref, *refs):
    outs, bufs, sems = refs[:3], refs[3:6], refs[6]
    copies = []
    pieces = [(0, 0, QROWS, 2 * KROWS)]
    for n in (1, 2):
        for r in range(0, KROWS, KROWS // 2):
            pieces.append((n, r, KROWS // 2, (n - 1) * KROWS + r))
    for p, (n, r, rows, at) in enumerate(pieces):
        for h in range(H):
            bufs[n][r : r + rows, h * DH : (h + 1) * DH] = x_ref[h, at : at + rows, :].astype(F32)
        copy = pltpu.make_async_copy(
            bufs[n].at[r : r + rows], outs[n].at[r : r + rows], sems.at[p]
        )
        copy.start()
        copies.append(copy)
    for copy in copies:
        copy.wait()


def unpacked(x):
    shapes = [(QROWS, H * DH), (KROWS, H * DH), (KROWS, H * DH)]
    return pl.pallas_call(
        unpack,
        in_specs=[pl.BlockSpec(memory_space=pltpu.VMEM)],
        out_specs=[pl.BlockSpec(memory_space=pl.ANY)] * 3,
        out_shape=[jax.ShapeDtypeStruct(shape, F32) for shape in shapes],
        scratch_shapes=[pltpu.VMEM(shape, F32) for shape in shapes]
        + [pltpu.SemaphoreType.DMA((5,))],
        compiler_params=pltpu.CompilerParams(vmem_limit_bytes=8 << 20),
        cost_estimate=cost(10**6, 3 * 10**6),
        name="unpack",
    )(x)


def shift(x, axis, by):
    n = lax.axis_size(axis)
    return lax.ppermute(x, axis, [(i, (i + by) % n) for i in range(n)])


def regroup(x):
    return lax.all_to_all(x, PLANE, split_axis=0, concat_axis=0, tiled=True)


def body(queries, keys, values, outputs, out_grad, stats):
    z = lax.axis_index("z")
    b = lax.axis_index(("y", "xh")).astype(jnp.int32).reshape(1)
    own = packed_queries(b, queries, out_grad, outputs, stats)
    own = regroup(own)
    kv = packed_keys(keys, values)
    kv = regroup(kv)
    own = with_stats(own)

    up, down = [own], [own]
    for n in range(1, NZ // 2 + 1):
        up.append(shift(up[-1], "z", 1))
        if n < NZ // 2:
            down.append(shift(down[-1], "z", -1))
    parts = up[::-1] + down[1:]
    half = NZ // 2
    where = (z + jnp.arange(-half, half, dtype=jnp.int32)) % NZ

    sent = []
    sums = ()
    groups = ((4, 3, -3), (2, -2), (1, -1), (0,))
    for n, group in enumerate(groups):
        tab = jnp.concatenate([(z + jnp.array(group, jnp.int32)) % NZ, where])
        first, last = n == 0, n == len(groups) - 1
        out = grads_call(
            len(group), first, last, tab.astype(jnp.int32), parts, kv, sums
        )
        sums = out[len(group) :]
        for by, dq in zip(group, out):
            if by:
                sent.append(shift(dq, "z", by))
            else:
                mine = dq
    mine = mine + sum(x.astype(F32) for x in sent)
    mine = (mine * (ROOT * SCALE)).reshape(NKV, NXC, QROWS, DH)
    mine = jnp.swapaxes(mine, 0, 1).reshape(NSP, QROWS, DH).astype(BF16)
    packed = lax.dynamic_update_slice(sums[0], mine, (0, 2 * KROWS, 0))
    packed = regroup(packed)
    return unpacked(packed)


def solution(mesh):
    torus = Mesh(mesh.devices.reshape(NY, NX, NZ, 2, 2), ALL)
    return jax.shard_map(
        body,
        mesh=torus,
        in_specs=(P(SP), P(ALL), P(ALL), P(SP), P(SP), P(SP)),
        out_specs=(P(ALL), P(ALL), P(ALL)),
        check_vma=False,
    )
```

time: 151 us -> 134 us (0.89)
  waiting for transfers between devices: 47.4 us -> 20 us
  blocking collectives: 39.4 us -> 48.2 us
  starting transfers between devices: 26.6 us -> 31.4 us
  local copies, waits for them, and re-layouts: 2.86 us -> 0.04 us
    ppermute x8 -> x14, waiting for transfers between devices: 31.6 us -> 14.9 us  [shift(): return lax.ppermute(x, axis, [(i, (i + by) % n) for i in range(n)])]
    ppermute x8 -> x14, starting transfers between devices: 10.9 us -> 27.2 us  [shift(): return lax.ppermute(x, axis, [(i, (i + by) % n) for i in range(n)])]
    all_to_all x2 -> x1, starting transfers between devices: 15.8 us -> 4.16 us  [regroup(): return lax.all_to_all(x, PLANE, split_axis=0, concat_axis=0, tiled=True)]
    all_to_all x2 -> x1, waiting for transfers between devices: 15.8 us -> 5.05 us  [regroup(): return lax.all_to_all(x, PLANE, split_axis=0, concat_axis=0, tiled=True)]
    all_to_all x1 -> x2, blocking collectives: 39.4 us -> 48.2 us  [regroup(): return lax.all_to_all(x, PLANE, split_axis=0, concat_axis=0, tiled=True)]
    pallas_call x3 -> x4, Pallas kernels: 25.9 us -> 26.7 us  [grads_call(): pl.pallas_call(functools.partial(grads, count, first, last), grid_spec=pl...]
  transfers between devices with their start and end apart: 10 -> 15, of which waited for: 5 -> 4; matrix products, arithmetic and copies ran while one was open for 2% -> 0% of each run, Pallas kernels for 6% -> 14%
where the time goes in v4:
time: 134 us
  blocking collectives  48.2 us (36%)
  Pallas kernels  32.7 us (24%)
  starting transfers between devices  31.4 us (23%)
  waiting for transfers between devices  20 us (15%)
    all_to_all x2, blocking collectives, regroup(): return lax.all_to_all(x, PLANE, split_axis=0, concat_axis=0, tiled=True)  48.2 us
    ppermute x14, starting transfers between devices, shift(): return lax.ppermute(x, axis, [(i, (i + by) % n) for i in range(n)])  27.2 us
    pallas_call x4, Pallas kernels, grads_call(): pl.pallas_call(functools.partial(grads, count, first, last), grid_spec=pl...  26.7 us
    ppermute x14, waiting for transfers between devices, shift(): return lax.ppermute(x, axis, [(i, (i + by) % n) for i in range(n)])  14.9 us
    all_to_all x1, waiting for transfers between devices, regroup(): return lax.all_to_all(x, PLANE, split_axis=0, concat_axis=0, tiled=True)  5.05 us
    all_to_all x1, starting transfers between devices, regroup(): return lax.all_to_all(x, PLANE, split_axis=0, concat_axis=0, tiled=True)  4.16 us
  transfers between devices with their start and end apart: 15, of which 4 were waited for; matrix products, arithmetic and copies ran while one was open for 0% of the time, Pallas kernels for 14%

profile of v4, /device:TPU:1, one launch (start us, length us, event | category | flops | bytes accessed | tf_op | source)
XLA Modules:
  0.0 133.8 jit_solution(11860212342604093523)
XLA Ops:
  0.6 2.1 %pack_queries.1 = bf16[32,40,128]{2,1,0:T(8,128)(2,1)} custom-call(s32[1]{0:T(128)} %bitcast.1.b_ref, bf16[128,4096]{1,0:T(8,128)(2,1)} %q_ref.1, bf16[128,4096]{1,0:T(8,128)(2,1)} %g_ref.1, bf16[128,4096]{1,0:T(8,128)(2,1)} %o_ref.1, f32[32,128]{1,0:T(8,128)} %bitcast.9), custom_call_target="tpu_custom_call" | custom-call | flops 1000000 | bytes 1000000 | tf_op jit(solution)/shard_map/pack_queries/pallas_call | solution.py:75
  2.8 18.3 %all_to_all.15.x_ref = bf16[32,40,128]{2,1,0:T(8,128)(2,1)S(1)} all-to-all(bf16[32,40,128]{2,1,0:T(8,128)(2,1)} %pack_queries.1), channel_id=1, replica_groups=mesh['y'=4,'xh'=2,'z'=8,'xl'=2,'c'=2] {'xl','c','y','xh'}, dimensions={0} | all-to-all | bytes 655360 | tf_op jit(solution)/shard_map/all_to_all | solution.py:263
  21.1 1.7 %collective-permute-start = (bf16[33,32,128]{2,1,0:T(8,128)(2,1)S(1)}, bf16[33,32,128]{2,1,0:T(8,128)(2,1)S(1)}, u32[]{:S(2)}, u32[]{:S(2)}) collective-permute-start(bf16[33,32,128]{2,1,0:T(8,128)(2,1)S(1)} %gather_stats.1.refs_4_.refs_12_), channel_id=1, source_target_pairs={{0,4},{4,8},{8,12},{12,16},{16,20},{20,24},{24,28},{28,0},{1,5},{5... | collective-permute-start | bytes 811016 | tf_op jit(solution)/shard_map/ppermute | solution.py:259
  22.8 4.0 %collective-permute-start.4 = (bf16[33,32,128]{2,1,0:T(8,128)(2,1)S(1)}, bf16[33,32,128]{2,1,0:T(8,128)(2,1)S(1)}, u32[]{:S(2)}, u32[]{:S(2)}) collective-permute-start(bf16[33,32,128]{2,1,0:T(8,128)(2,1)S(1)} %gather_stats.1.refs_4_.refs_12_), channel_id=1, source_target_pairs={{0,28},{4,0},{8,4},{12,8},{16,12},{20,16},{24,20},{28,24},{1,29},{... | collective-permute-start | bytes 811016 | tf_op jit(solution)/shard_map/ppermute | solution.py:259
  26.8 6.9 %collective-permute-done.refs_3_.refs_11_ = bf16[33,32,128]{2,1,0:T(8,128)(2,1)S(1)} collective-permute-done((bf16[33,32,128]{2,1,0:T(8,128)(2,1)S(1)}, bf16[33,32,128]{2,1,0:T(8,128)(2,1)S(1)}, u32[]{:S(2)}, u32[]{:S(2)}) %collective-permute-start) | collective-permute-done | bytes 270368 | tf_op jit(solution)/shard_map/ppermute | solution.py:259
  33.7 0.0 collective-permute-start.1
  33.7 2.4 %pack_keys.1 = bf16[32,128,128]{2,1,0:T(8,128)(2,1)} custom-call(bf16[64,4096]{1,0:T(8,128)(2,1)} %k_ref.1, bf16[64,4096]{1,0:T(8,128)(2,1)} %v_ref.1), custom_call_target="tpu_custom_call" | custom-call | flops 1000000 | bytes 2000000 | tf_op jit(solution)/shard_map/pack_keys/pallas_call | solution.py:113
  36.1 0.0 copy-start.2
  36.1 0.0 copy-start
  36.1 0.0 copy-start.1
  36.1 4.2 %all-to-all-start.1 = ((bf16[32,128,128]{2,1,0:T(8,128)(2,1)}), bf16[32,128,128]{2,1,0:T(8,128)(2,1)S(1)}, u32[]{:S(2)}, u32[]{:S(2)}) async-start(bf16[32,128,128]{2,1,0:T(8,128)(2,1)} %pack_keys.1), calls=%async_computation.1 | async-start | bytes 2097152 | tf_op jit(solution)/shard_map/all_to_all | solution.py:263
  40.2 0.0 collective-permute-done.4.refs_5_.refs_13_
  40.2 3.0 %collective-permute-start.5 = (bf16[33,32,128]{2,1,0:T(8,128)(2,1)S(1)}, bf16[33,32,128]{2,1,0:T(8,128)(2,1)S(1)}, u32[]{:S(2)}, u32[]{:S(2)}) collective-permute-start(bf16[33,32,128]{2,1,0:T(8,128)(2,1)S(1)} %collective-permute-done.4.refs_5_.refs_13_), channel_id=1, source_target_pairs={{0,28},{4,0},{8,4},{12,8},{16,12},{20,16},{24,20},{28,24},{1,29},{... | collective-permute-start | bytes 811016 | tf_op jit(solution)/shard_map/ppermute | solution.py:259
  43.3 0.0 collective-permute-done.1.refs_2_.refs_10_
  43.3 0.0 collective-permute-start.2
  43.3 0.0 copy-done.2
  43.3 0.0 copy-done
  43.3 0.0 copy-done.1
  43.3 5.5 %collective-permute-done.5.refs_6_.refs_14_ = bf16[33,32,128]{2,1,0:T(8,128)(2,1)S(1)} collective-permute-done((bf16[33,32,128]{2,1,0:T(8,128)(2,1)S(1)}, bf16[33,32,128]{2,1,0:T(8,128)(2,1)S(1)}, u32[]{:S(2)}, u32[]{:S(2)}) %collective-permute-start.5) | collective-permute-done | bytes 270368 | tf_op jit(solution)/shard_map/ppermute | solution.py:259
  48.8 3.4 %collective-permute-start.6 = (bf16[33,32,128]{2,1,0:T(8,128)(2,1)S(1)}, bf16[33,32,128]{2,1,0:T(8,128)(2,1)S(1)}, u32[]{:S(2)}, u32[]{:S(2)}) collective-permute-start(bf16[33,32,128]{2,1,0:T(8,128)(2,1)S(1)} %collective-permute-done.5.refs_6_.refs_14_), channel_id=1, source_target_pairs={{0,28},{4,0},{8,4},{12,8},{16,12},{20,16},{24,20},{28,24},{1,29},{... | collective-permute-start | bytes 811016 | tf_op jit(solution)/shard_map/ppermute | solution.py:259
  52.2 0.0 collective-permute-done.2.refs_1_.refs_9_
  52.2 0.0 collective-permute-start.3
  52.2 0.1 pad_add_fusion.3.tab
  52.3 0.1 pad_add_fusion.2
  52.4 5.0 %all-to-all-done.1.refs_16_ = bf16[32,128,128]{2,1,0:T(8,128)(2,1)S(1)} async-done(((bf16[32,128,128]{2,1,0:T(8,128)(2,1)}), bf16[32,128,128]{2,1,0:T(8,128)(2,1)S(1)}, u32[]{:S(2)}, u32[]{:S(2)}) %all-to-all-start.1) | async-done | bytes 1048608 | tf_op jit(solution)/shard_map/all_to_all | solution.py:263
  57.4 0.0 collective-permute-done.6.refs_7_.refs_15_
  57.4 2.6 %collective-permute-done.3.refs_0_.refs_8_ = bf16[33,32,128]{2,1,0:T(8,128)(2,1)S(1)} collective-permute-done((bf16[33,32,128]{2,1,0:T(8,128)(2,1)S(1)}, bf16[33,32,128]{2,1,0:T(8,128)(2,1)S(1)}, u32[]{:S(2)}, u32[]{:S(2)}) %collective-permute-start.3) | collective-permute-done | bytes 270368 | tf_op jit(solution)/shard_map/ppermute | solution.py:259
  60.0 9.8 %grads.4 = (bf16[8,64,128]{2,1,0:T(8,128)(2,1)S(1)}, bf16[8,64,128]{2,1,0:T(8,128)(2,1)S(1)}, bf16[8,64,128]{2,1,0:T(8,128)(2,1)S(1)}, f32[2048,128]{1,0:T(8,128)S(1)}, f32[2048,128]{1,0:T(8,128)S(1)}) custom-call(s32[11]{0:T(128)S(1)} %pad_add_fusion.3.tab, bf16[33,32,128]{2,1,0:T(8,128)(2,1)S(1)} %collective-permute-done.3.refs_0_.refs_8_, ...), custom_call_target="tpu_custom_call" | custom-call | flops 4026531840 | bytes 4194304 | tf_op jit(solution)/shard_map/grads/pallas_call | solution.py:207
  69.8 4.2 %collective-permute-start.7 = (bf16[8,64,128]{2,1,0:T(8,128)(2,1)S(1)}, bf16[8,64,128]{2,1,0:T(8,128)(2,1)S(1)}, u32[]{:S(2)}, u32[]{:S(2)}) collective-permute-start(bf16[8,64,128]{2,1,0:T(8,128)(2,1)S(1)} %get-tuple-element.26), channel_id=1, source_target_pairs={{0,16},{4,20},{8,24},{12,28},{16,0},{20,4},{24,8},{28,12},{1,17},{... | collective-permute-start | bytes 393224 | tf_op jit(solution)/shard_map/ppermute | solution.py:259
  74.0 0.0 collective-permute-start.8
  74.0 4.5 %collective-permute-start.9 = (bf16[8,64,128]{2,1,0:T(8,128)(2,1)S(1)}, bf16[8,64,128]{2,1,0:T(8,128)(2,1)S(1)}, u32[]{:S(2)}, u32[]{:S(2)}) collective-permute-start(bf16[8,64,128]{2,1,0:T(8,128)(2,1)S(1)} %get-tuple-element.28), channel_id=1, source_target_pairs={{0,20},{4,24},{8,28},{12,0},{16,4},{20,8},{24,12},{28,16},{1,21},{... | collective-permute-start | bytes 393224 | tf_op jit(solution)/shard_map/ppermute | solution.py:259
  78.5 6.7 %grads.5 = (bf16[8,64,128]{2,1,0:T(8,128)(2,1)S(1)}, bf16[8,64,128]{2,1,0:T(8,128)(2,1)S(1)}, f32[2048,128]{1,0:T(8,128)S(1)}, f32[2048,128]{1,0:T(8,128)S(1)}) custom-call(s32[10]{0:T(128)S(1)} %get-tuple-element.33.tab, bf16[33,32,128]{2,1,0:T(8,128)(2,1)S(1)} %collective-permute-done.3.refs_0_.refs_8_, ...), custom_call_target="tpu_custom_call" | custom-call | flops 2684354560 | bytes 4194304 | tf_op jit(solution)/shard_map/grads/pallas_call | solution.py:207
  85.2 0.1 collective-permute-start.10
  85.3 3.6 %collective-permute-start.11 = (bf16[8,64,128]{2,1,0:T(8,128)(2,1)S(1)}, bf16[8,64,128]{2,1,0:T(8,128)(2,1)S(1)}, u32[]{:S(2)}, u32[]{:S(2)}) collective-permute-start(bf16[8,64,128]{2,1,0:T(8,128)(2,1)S(1)} %get-tuple-element.30), channel_id=1, source_target_pairs={{0,24},{4,28},{8,0},{12,4},{16,8},{20,12},{24,16},{28,20},{1,25},{... | collective-permute-start | bytes 393224 | tf_op jit(solution)/shard_map/ppermute | solution.py:259
  88.9 6.7 %grads.6 = (bf16[8,64,128]{2,1,0:T(8,128)(2,1)S(1)}, bf16[8,64,128]{2,1,0:T(8,128)(2,1)S(1)}, f32[2048,128]{1,0:T(8,128)S(1)}, f32[2048,128]{1,0:T(8,128)S(1)}) custom-call(s32[10]{0:T(128)S(1)} %get-tuple-element.34.tab, bf16[33,32,128]{2,1,0:T(8,128)(2,1)S(1)} %collective-permute-done.3.refs_0_.refs_8_, ...), custom_call_target="tpu_custom_call" | custom-call | flops 2684354560 | bytes 4194304 | tf_op jit(solution)/shard_map/grads/pallas_call | solution.py:207
  95.6 0.0 collective-permute-done.7
  95.6 0.1 collective-permute-start.12
  95.7 0.0 collective-permute-done.8
  95.7 2.7 %collective-permute-start.13 = (bf16[8,64,128]{2,1,0:T(8,128)(2,1)S(1)}, bf16[8,64,128]{2,1,0:T(8,128)(2,1)S(1)}, u32[]{:S(2)}, u32[]{:S(2)}) collective-permute-start(bf16[8,64,128]{2,1,0:T(8,128)(2,1)S(1)} %get-tuple-element.32), channel_id=1, source_target_pairs={{0,28},{4,0},{8,4},{12,8},{16,12},{20,16},{24,20},{28,24},{1,29},{... | collective-permute-start | bytes 393224 | tf_op jit(solution)/shard_map/ppermute | solution.py:259
  98.4 0.1 pad_add_fusion.tab
  98.5 3.5 %grads.7 = (f32[8,64,128]{2,1,0:T(8,128)S(1)}, bf16[32,144,128]{2,1,0:T(8,128)(2,1)S(1)}) custom-call(s32[9]{0:T(128)S(1)} %pad_add_fusion.tab, bf16[33,32,128]{2,1,0:T(8,128)(2,1)S(1)} %collective-permute-done.3.refs_0_.refs_8_, bf16[33,32,128]{2,1,0:T(8,128)(2,1)S(1)} %collective-permute-done.2.refs_1_.refs_9_, ...), custom_call_target="tpu_custom_call" | custom-call | flops 1342177280 | bytes 4194304 | tf_op jit(solution)/shard_map/grads/pallas_call | solution.py:207
  101.9 0.0 collective-permute-done.9
  101.9 0.0 collective-permute-done.10
  101.9 0.0 collective-permute-done.11
  102.0 0.0 collective-permute-done.12
  102.0 0.0 collective-permute-done.13
  102.0 0.2 multiply_convert_fusion
  102.2 29.9 %all_to_all.16.x_ref = bf16[32,144,128]{2,1,0:T(8,128)(2,1)S(1)} all-to-all(bf16[32,144,128]{2,1,0:T(8,128)(2,1)S(1)} %constant_dynamic-update-slice_fusion), channel_id=1, replica_groups=mesh['y'=4,'xh'=2,'z'=8,'xl'=2,'c'=2] {'xl','c','y','xh'}, dimensions={0} | all-to-all | bytes 2359296 | tf_op jit(solution)/shard_map/all_to_all | solution.py:263
  132.1 1.5 %unpack.1 = (f32[16,4096]{1,0:T(8,128)}, f32[64,4096]{1,0:T(8,128)}, f32[64,4096]{1,0:T(8,128)}) custom-call(bf16[32,144,128]{2,1,0:T(8,128)(2,1)S(1)} %all_to_all.16.x_ref), custom_call_target="tpu_custom_call" | custom-call | flops 1000000 | bytes 3000000 | tf_op jit(solution)/shard_map/unpack/pallas_call | solution.py:244
  (6 shorter events, 0.1 us)
Async XLA Ops:
  21.1 12.6 %collective-permute-start = (bf16[33,32,128]{2,1,0:T(8,128)(2,1)S(1)}, bf16[33,32,128]{2,1,0:T(8,128)(2,1)S(1)}, u32[]{:S(2)}, u32[]{:S(2)}) collective-permute-start(bf16[33,32,128]{2,1,0:T(8,128)(2,1)S(1)} %gather_stats.1.refs_4_.refs_12_), channel_id=1, source_target_pairs={{0,4},{4,8},{8,12},{12,16},{16,20},{20,24},{24,28},{28,0},{1,5},{5... | collective-permute-start | bytes 811016 | tf_op jit(solution)/shard_map/ppermute | solution.py:259
  22.8 17.4 %collective-permute-start.4 = (bf16[33,32,128]{2,1,0:T(8,128)(2,1)S(1)}, bf16[33,32,128]{2,1,0:T(8,128)(2,1)S(1)}, u32[]{:S(2)}, u32[]{:S(2)}) collective-permute-start(bf16[33,32,128]{2,1,0:T(8,128)(2,1)S(1)} %gather_stats.1.refs_4_.refs_12_), channel_id=1, source_target_pairs={{0,28},{4,0},{8,4},{12,8},{16,12},{20,16},{24,20},{28,24},{1,29},{... | collective-permute-start | bytes 811016 | tf_op jit(solution)/shard_map/ppermute | solution.py:259
  33.7 9.6 %collective-permute-start.1 = (bf16[33,32,128]{2,1,0:T(8,128)(2,1)S(1)}, bf16[33,32,128]{2,1,0:T(8,128)(2,1)S(1)}, u32[]{:S(2)}, u32[]{:S(2)}) collective-permute-start(bf16[33,32,128]{2,1,0:T(8,128)(2,1)S(1)} %collective-permute-done.refs_3_.refs_11_), channel_id=1, source_target_pairs={{0,4},{4,8},{8,12},{12,16},{16,20},{20,24},{24,28},{28,0},{1,5},{5... | collective-permute-start | bytes 811016 | tf_op jit(solution)/shard_map/ppermute | solution.py:259
  36.1 7.2 %copy-start.2 = (s32[3]{0:T(128)S(1)}, s32[3]{0:T(128)}, u32[]{:S(2)}) copy-start(s32[3]{0:T(128)} %constant.85.clone) | copy-start | bytes 40
  36.1 7.2 %copy-start = (s32[2]{0:T(128)S(1)}, s32[2]{0:T(128)}, u32[]{:S(2)}) copy-start(s32[2]{0:T(128)} %constant.87.clone) | copy-start | bytes 28
  36.1 7.2 %copy-start.1 = (s32[2]{0:T(128)S(1)}, s32[2]{0:T(128)}, u32[]{:S(2)}) copy-start(s32[2]{0:T(128)} %constant.86.clone) | copy-start | bytes 28
  36.1 21.4 %all-to-all-start.1 = ((bf16[32,128,128]{2,1,0:T(8,128)(2,1)}), bf16[32,128,128]{2,1,0:T(8,128)(2,1)S(1)}, u32[]{:S(2)}, u32[]{:S(2)}) async-start(bf16[32,128,128]{2,1,0:T(8,128)(2,1)} %pack_keys.1), calls=%async_computation.1 | async-start | bytes 2097152 | tf_op jit(solution)/shard_map/all_to_all | solution.py:263
  40.2 8.6 %collective-permute-start.5 = (bf16[33,32,128]{2,1,0:T(8,128)(2,1)S(1)}, bf16[33,32,128]{2,1,0:T(8,128)(2,1)S(1)}, u32[]{:S(2)}, u32[]{:S(2)}) collective-permute-start(bf16[33,32,128]{2,1,0:T(8,128)(2,1)S(1)} %collective-permute-done.4.refs_5_.refs_13_), channel_id=1, source_target_pairs={{0,28},{4,0},{8,4},{12,8},{16,12},{20,16},{24,20},{28,24},{1,29},{... | collective-permute-start | bytes 811016 | tf_op jit(solution)/shard_map/ppermute | solution.py:259
  43.3 8.9 %collective-permute-start.2 = (bf16[33,32,128]{2,1,0:T(8,128)(2,1)S(1)}, bf16[33,32,128]{2,1,0:T(8,128)(2,1)S(1)}, u32[]{:S(2)}, u32[]{:S(2)}) collective-permute-start(bf16[33,32,128]{2,1,0:T(8,128)(2,1)S(1)} %collective-permute-done.1.refs_2_.refs_10_), channel_id=1, source_target_pairs={{0,4},{4,8},{8,12},{12,16},{16,20},{20,24},{24,28},{28,0},{1,5},{5... | collective-permute-start | bytes 811016 | tf_op jit(solution)/shard_map/ppermute | solution.py:259
  48.8 8.6 %collective-permute-start.6 = (bf16[33,32,128]{2,1,0:T(8,128)(2,1)S(1)}, bf16[33,32,128]{2,1,0:T(8,128)(2,1)S(1)}, u32[]{:S(2)}, u32[]{:S(2)}) collective-permute-start(bf16[33,32,128]{2,1,0:T(8,128)(2,1)S(1)} %collective-permute-done.5.refs_6_.refs_14_), channel_id=1, source_target_pairs={{0,28},{4,0},{8,4},{12,8},{16,12},{20,16},{24,20},{28,24},{1,29},{... | collective-permute-start | bytes 811016 | tf_op jit(solution)/shard_map/ppermute | solution.py:259
  52.2 7.8 %collective-permute-start.3 = (bf16[33,32,128]{2,1,0:T(8,128)(2,1)S(1)}, bf16[33,32,128]{2,1,0:T(8,128)(2,1)S(1)}, u32[]{:S(2)}, u32[]{:S(2)}) collective-permute-start(bf16[33,32,128]{2,1,0:T(8,128)(2,1)S(1)} %collective-permute-done.2.refs_1_.refs_9_), channel_id=1, source_target_pairs={{0,4},{4,8},{8,12},{12,16},{16,20},{20,24},{24,28},{28,0},{1,5},{5... | collective-permute-start | bytes 811016 | tf_op jit(solution)/shard_map/ppermute | solution.py:259
  69.8 25.8 %collective-permute-start.7 = (bf16[8,64,128]{2,1,0:T(8,128)(2,1)S(1)}, bf16[8,64,128]{2,1,0:T(8,128)(2,1)S(1)}, u32[]{:S(2)}, u32[]{:S(2)}) collective-permute-start(bf16[8,64,128]{2,1,0:T(8,128)(2,1)S(1)} %get-tuple-element.26), channel_id=1, source_target_pairs={{0,16},{4,20},{8,24},{12,28},{16,0},{20,4},{24,8},{28,12},{1,17},{... | collective-permute-start | bytes 393224 | tf_op jit(solution)/shard_map/ppermute | solution.py:259
  74.0 21.7 %collective-permute-start.8 = (bf16[8,64,128]{2,1,0:T(8,128)(2,1)S(1)}, bf16[8,64,128]{2,1,0:T(8,128)(2,1)S(1)}, u32[]{:S(2)}, u32[]{:S(2)}) collective-permute-start(bf16[8,64,128]{2,1,0:T(8,128)(2,1)S(1)} %get-tuple-element.27), channel_id=1, source_target_pairs={{0,12},{4,16},{8,20},{12,24},{16,28},{20,0},{24,4},{28,8},{1,13},{... | collective-permute-start | bytes 393224 | tf_op jit(solution)/shard_map/ppermute | solution.py:259
  74.0 27.9 %collective-permute-start.9 = (bf16[8,64,128]{2,1,0:T(8,128)(2,1)S(1)}, bf16[8,64,128]{2,1,0:T(8,128)(2,1)S(1)}, u32[]{:S(2)}, u32[]{:S(2)}) collective-permute-start(bf16[8,64,128]{2,1,0:T(8,128)(2,1)S(1)} %get-tuple-element.28), channel_id=1, source_target_pairs={{0,20},{4,24},{8,28},{12,0},{16,4},{20,8},{24,12},{28,16},{1,21},{... | collective-permute-start | bytes 393224 | tf_op jit(solution)/shard_map/ppermute | solution.py:259
  85.2 16.7 %collective-permute-start.10 = (bf16[8,64,128]{2,1,0:T(8,128)(2,1)S(1)}, bf16[8,64,128]{2,1,0:T(8,128)(2,1)S(1)}, u32[]{:S(2)}, u32[]{:S(2)}) collective-permute-start(bf16[8,64,128]{2,1,0:T(8,128)(2,1)S(1)} %get-tuple-element.29), channel_id=1, source_target_pairs={{0,8},{4,12},{8,16},{12,20},{16,24},{20,28},{24,0},{28,4},{1,9},{5... | collective-permute-start | bytes 393224 | tf_op jit(solution)/shard_map/ppermute | solution.py:259
  85.3 16.6 %collective-permute-start.11 = (bf16[8,64,128]{2,1,0:T(8,128)(2,1)S(1)}, bf16[8,64,128]{2,1,0:T(8,128)(2,1)S(1)}, u32[]{:S(2)}, u32[]{:S(2)}) collective-permute-start(bf16[8,64,128]{2,1,0:T(8,128)(2,1)S(1)} %get-tuple-element.30), channel_id=1, source_target_pairs={{0,24},{4,28},{8,0},{12,4},{16,8},{20,12},{24,16},{28,20},{1,25},{... | collective-permute-start | bytes 393224 | tf_op jit(solution)/shard_map/ppermute | solution.py:259
  95.6 6.3 %collective-permute-start.12 = (bf16[8,64,128]{2,1,0:T(8,128)(2,1)S(1)}, bf16[8,64,128]{2,1,0:T(8,128)(2,1)S(1)}, u32[]{:S(2)}, u32[]{:S(2)}) collective-permute-start(bf16[8,64,128]{2,1,0:T(8,128)(2,1)S(1)} %get-tuple-element.31), channel_id=1, source_target_pairs={{0,4},{4,8},{8,12},{12,16},{16,20},{20,24},{24,28},{28,0},{1,5},{5... | collective-permute-start | bytes 393224 | tf_op jit(solution)/shard_map/ppermute | solution.py:259
  95.7 6.2 %collective-permute-start.13 = (bf16[8,64,128]{2,1,0:T(8,128)(2,1)S(1)}, bf16[8,64,128]{2,1,0:T(8,128)(2,1)S(1)}, u32[]{:S(2)}, u32[]{:S(2)}) collective-permute-start(bf16[8,64,128]{2,1,0:T(8,128)(2,1)S(1)} %get-tuple-element.32), channel_id=1, source_target_pairs={{0,28},{4,0},{8,4},{12,8},{16,12},{20,16},{24,20},{28,24},{1,29},{... | collective-permute-start | bytes 393224 | tf_op jit(solution)/shard_map/ppermute | solution.py:259

commit v5 on v4

--- a/solution.py
+++ b/solution.py
@@ -254,9 +254,12 @@
     )(x)
 
 
-def shift(x, axis, by):
-    n = lax.axis_size(axis)
-    return lax.ppermute(x, axis, [(i, (i + by) % n) for i in range(n)])
+def turn(x, by):
+    pairs = []
+    for z in range(NZ):
+        for c in range(2):
+            pairs.append((z * 2 + c, (z + (1 - 2 * c) * by) % NZ * 2 + c))
+    return lax.ppermute(x, ("z", "c"), pairs)
 
 
 def regroup(x):
@@ -272,20 +275,21 @@
     kv = regroup(kv)
     own = with_stats(own)
 
-    up, down = [own], [own]
+    one, two = [own], [own]
     for n in range(1, NZ // 2 + 1):
-        up.append(shift(up[-1], "z", 1))
+        one.append(turn(one[-1], 1))
         if n < NZ // 2:
-            down.append(shift(down[-1], "z", -1))
-    parts = up[::-1] + down[1:]
+            two.append(turn(two[-1], -1))
+    parts = one[::-1] + two[1:]
     half = NZ // 2
-    where = (z + jnp.arange(-half, half, dtype=jnp.int32)) % NZ
+    sign = 1 - 2 * lax.axis_index("c")
+    where = (z + sign * jnp.arange(-half, half, dtype=jnp.int32)) % NZ
 
     sent = []
     sums = ()
     groups = ((4, 3, -3), (2, -2), (1, -1), (0,))
     for n, group in enumerate(groups):
-        tab = jnp.concatenate([(z + jnp.array(group, jnp.int32)) % NZ, where])
+        tab = jnp.concatenate([(z + sign * jnp.array(group, jnp.int32)) % NZ, where])
         first, last = n == 0, n == len(groups) - 1
         out = grads_call(
             len(group), first, last, tab.astype(jnp.int32), parts, kv, sums
@@ -293,7 +297,7 @@
         sums = out[len(group) :]
         for by, dq in zip(group, out):
             if by:
-                sent.append(shift(dq, "z", by))
+                sent.append(turn(dq, by))
             else:
                 mine = dq
     mine = mine + sum(x.astype(F32) for x in sent)

time: 134 us -> 133 us (level)
  transfers between devices with their start and end apart: 15 -> 15, of which waited for: 4 -> 6; matrix products, arithmetic and copies ran while one was open for 0% -> 0% of each run, Pallas kernels for 14% -> 15%
where the time goes in v5:
time: 133 us
  blocking collectives  48 us (36%)
  Pallas kernels  32.7 us (25%)
  starting transfers between devices  32.1 us (24%)
  waiting for transfers between devices  18.8 us (14%)
    all_to_all x2, blocking collectives, regroup(): return lax.all_to_all(x, PLANE, split_axis=0, concat_axis=0, tiled=True)  48 us
    ppermute x14, starting transfers between devices, turn(): return lax.ppermute(x, ('z', 'c'), pairs)  28.2 us
    pallas_call x4, Pallas kernels, grads_call(): pl.pallas_call(functools.partial(grads, count, first, last), grid_spec=pl...  26.7 us
    ppermute x14, waiting for transfers between devices, turn(): return lax.ppermute(x, ('z', 'c'), pairs)  14.1 us
    all_to_all x1, waiting for transfers between devices, regroup(): return lax.all_to_all(x, PLANE, split_axis=0, concat_axis=0, tiled=True)  4.61 us
    all_to_all x1, starting transfers between devices, regroup(): return lax.all_to_all(x, PLANE, split_axis=0, concat_axis=0, tiled=True)  3.85 us
  transfers between devices with their start and end apart: 15, of which 6 were waited for; matrix products, arithmetic and copies ran while one was open for 0% of the time, Pallas kernels for 15%

profile of v5, /device:TPU:1, one launch (start us, length us, event | category | flops | bytes accessed | tf_op | source)
XLA Modules:
  0.0 133.0 jit_solution(4906787909490581513)
XLA Ops:
  0.6 2.1 %pack_queries.1 = bf16[32,40,128]{2,1,0:T(8,128)(2,1)} custom-call(s32[1]{0:T(128)} %bitcast.1.b_ref, bf16[128,4096]{1,0:T(8,128)(2,1)} %q_ref.1, bf16[128,4096]{1,0:T(8,128)(2,1)} %g_ref.1, bf16[128,4096]{1,0:T(8,128)(2,1)} %o_ref.1, f32[32,128]{1,0:T(8,128)} %bitcast.9), custom_call_target="tpu_custom_call" | custom-call | flops 1000000 | bytes 1000000 | tf_op jit(solution)/shard_map/pack_queries/pallas_call | solution.py:75
  2.8 18.3 %all_to_all.15.x_ref = bf16[32,40,128]{2,1,0:T(8,128)(2,1)S(1)} all-to-all(bf16[32,40,128]{2,1,0:T(8,128)(2,1)} %pack_queries.1), channel_id=1, replica_groups=mesh['y'=4,'xh'=2,'z'=8,'xl'=2,'c'=2] {'xl','c','y','xh'}, dimensions={0} | all-to-all | bytes 655360 | tf_op jit(solution)/shard_map/all_to_all | solution.py:266
  21.1 5.7 %collective-permute-start = (bf16[33,32,128]{2,1,0:T(8,128)(2,1)S(1)}, bf16[33,32,128]{2,1,0:T(8,128)(2,1)S(1)}, u32[]{:S(2)}, u32[]{:S(2)}) collective-permute-start(bf16[33,32,128]{2,1,0:T(8,128)(2,1)S(1)} %gather_stats.1.refs_4_.refs_12_), channel_id=1, source_target_pairs={{0,4},{1,29},{4,8},{5,1},{8,12},{9,5},{12,16},{13,9},{16,20},{17,1... | collective-permute-start | bytes 811016 | tf_op jit(solution)/shard_map/ppermute | solution.py:262
  26.8 0.0 collective-permute-start.4
  26.8 6.0 %collective-permute-done.refs_3_.refs_11_ = bf16[33,32,128]{2,1,0:T(8,128)(2,1)S(1)} collective-permute-done((bf16[33,32,128]{2,1,0:T(8,128)(2,1)S(1)}, bf16[33,32,128]{2,1,0:T(8,128)(2,1)S(1)}, u32[]{:S(2)}, u32[]{:S(2)}) %collective-permute-start) | collective-permute-done | bytes 270368 | tf_op jit(solution)/shard_map/ppermute | solution.py:262
  32.7 3.4 %collective-permute-start.1 = (bf16[33,32,128]{2,1,0:T(8,128)(2,1)S(1)}, bf16[33,32,128]{2,1,0:T(8,128)(2,1)S(1)}, u32[]{:S(2)}, u32[]{:S(2)}) collective-permute-start(bf16[33,32,128]{2,1,0:T(8,128)(2,1)S(1)} %collective-permute-done.refs_3_.refs_11_), channel_id=1, source_target_pairs={{0,4},{1,29},{4,8},{5,1},{8,12},{9,5},{12,16},{13,9},{16,20},{17,1... | collective-permute-start | bytes 811016 | tf_op jit(solution)/shard_map/ppermute | solution.py:262
  36.1 2.4 %pack_keys.1 = bf16[32,128,128]{2,1,0:T(8,128)(2,1)} custom-call(bf16[64,4096]{1,0:T(8,128)(2,1)} %k_ref.1, bf16[64,4096]{1,0:T(8,128)(2,1)} %v_ref.1), custom_call_target="tpu_custom_call" | custom-call | flops 1000000 | bytes 2000000 | tf_op jit(solution)/shard_map/pack_keys/pallas_call | solution.py:113
  38.5 0.0 copy-start.2
  38.5 0.0 copy-start
  38.5 0.0 copy-start.1
  38.5 3.8 %all-to-all-start.1 = ((bf16[32,128,128]{2,1,0:T(8,128)(2,1)}), bf16[32,128,128]{2,1,0:T(8,128)(2,1)S(1)}, u32[]{:S(2)}, u32[]{:S(2)}) async-start(bf16[32,128,128]{2,1,0:T(8,128)(2,1)} %pack_keys.1), calls=%async_computation.1 | async-start | bytes 2097152 | tf_op jit(solution)/shard_map/all_to_all | solution.py:266
  42.4 0.0 collective-permute-done.4.refs_5_.refs_13_
  42.4 0.1 collective-permute-start.5
  42.5 0.0 collective-permute-done.1.refs_2_.refs_10_
  42.5 2.7 %collective-permute-start.2 = (bf16[33,32,128]{2,1,0:T(8,128)(2,1)S(1)}, bf16[33,32,128]{2,1,0:T(8,128)(2,1)S(1)}, u32[]{:S(2)}, u32[]{:S(2)}) collective-permute-start(bf16[33,32,128]{2,1,0:T(8,128)(2,1)S(1)} %collective-permute-done.1.refs_2_.refs_10_), channel_id=1, source_target_pairs={{0,4},{1,29},{4,8},{5,1},{8,12},{9,5},{12,16},{13,9},{16,20},{17,1... | collective-permute-start | bytes 811016 | tf_op jit(solution)/shard_map/ppermute | solution.py:262
  45.1 0.0 copy-done.2
  45.1 0.0 copy-done
  45.2 0.0 copy-done.1
  45.2 5.8 %collective-permute-done.5.refs_6_.refs_14_ = bf16[33,32,128]{2,1,0:T(8,128)(2,1)S(1)} collective-permute-done((bf16[33,32,128]{2,1,0:T(8,128)(2,1)S(1)}, bf16[33,32,128]{2,1,0:T(8,128)(2,1)S(1)}, u32[]{:S(2)}, u32[]{:S(2)}) %collective-permute-start.5) | collective-permute-done | bytes 270368 | tf_op jit(solution)/shard_map/ppermute | solution.py:262
  51.0 0.0 collective-permute-start.6
  51.0 0.0 collective-permute-done.2.refs_1_.refs_9_
  51.0 2.7 %collective-permute-start.3 = (bf16[33,32,128]{2,1,0:T(8,128)(2,1)S(1)}, bf16[33,32,128]{2,1,0:T(8,128)(2,1)S(1)}, u32[]{:S(2)}, u32[]{:S(2)}) collective-permute-start(bf16[33,32,128]{2,1,0:T(8,128)(2,1)S(1)} %collective-permute-done.2.refs_1_.refs_9_), channel_id=1, source_target_pairs={{0,4},{1,29},{4,8},{5,1},{8,12},{9,5},{12,16},{13,9},{16,20},{17,1... | collective-permute-start | bytes 811016 | tf_op jit(solution)/shard_map/ppermute | solution.py:262
  53.7 0.1 pad_add_fusion.3.tab
  53.7 0.1 pad_add_fusion.2
  53.8 4.6 %all-to-all-done.1.refs_16_ = bf16[32,128,128]{2,1,0:T(8,128)(2,1)S(1)} async-done(((bf16[32,128,128]{2,1,0:T(8,128)(2,1)}), bf16[32,128,128]{2,1,0:T(8,128)(2,1)S(1)}, u32[]{:S(2)}, u32[]{:S(2)}) %all-to-all-start.1) | async-done | bytes 1048608 | tf_op jit(solution)/shard_map/all_to_all | solution.py:266
  58.4 0.2 collective-permute-done.6.refs_7_.refs_15_
  58.6 0.7 collective-permute-done.3.refs_0_.refs_8_
  59.4 9.8 %grads.4 = (bf16[8,64,128]{2,1,0:T(8,128)(2,1)S(1)}, bf16[8,64,128]{2,1,0:T(8,128)(2,1)S(1)}, bf16[8,64,128]{2,1,0:T(8,128)(2,1)S(1)}, f32[2048,128]{1,0:T(8,128)S(1)}, f32[2048,128]{1,0:T(8,128)S(1)}) custom-call(s32[11]{0:T(128)S(1)} %pad_add_fusion.3.tab, bf16[33,32,128]{2,1,0:T(8,128)(2,1)S(1)} %collective-permute-done.3.refs_0_.refs_8_, ...), custom_call_target="tpu_custom_call" | custom-call | flops 4026531840 | bytes 4194304 | tf_op jit(solution)/shard_map/grads/pallas_call | solution.py:207
  69.1 2.4 %collective-permute-start.7 = (bf16[8,64,128]{2,1,0:T(8,128)(2,1)S(1)}, bf16[8,64,128]{2,1,0:T(8,128)(2,1)S(1)}, u32[]{:S(2)}, u32[]{:S(2)}) collective-permute-start(bf16[8,64,128]{2,1,0:T(8,128)(2,1)S(1)} %get-tuple-element.26), channel_id=1, source_target_pairs={{0,16},{1,17},{4,20},{5,21},{8,24},{9,25},{12,28},{13,29},{16,0},{... | collective-permute-start | bytes 393224 | tf_op jit(solution)/shard_map/ppermute | solution.py:262
  71.5 2.0 %collective-permute-start.8 = (bf16[8,64,128]{2,1,0:T(8,128)(2,1)S(1)}, bf16[8,64,128]{2,1,0:T(8,128)(2,1)S(1)}, u32[]{:S(2)}, u32[]{:S(2)}) collective-permute-start(bf16[8,64,128]{2,1,0:T(8,128)(2,1)S(1)} %get-tuple-element.27), channel_id=1, source_target_pairs={{0,12},{1,21},{4,16},{5,25},{8,20},{9,29},{12,24},{13,1},{16,28},{... | collective-permute-start | bytes 393224 | tf_op jit(solution)/shard_map/ppermute | solution.py:262
  73.5 1.2 collective-permute-start.9
  74.8 6.7 %grads.5 = (bf16[8,64,128]{2,1,0:T(8,128)(2,1)S(1)}, bf16[8,64,128]{2,1,0:T(8,128)(2,1)S(1)}, f32[2048,128]{1,0:T(8,128)S(1)}, f32[2048,128]{1,0:T(8,128)S(1)}) custom-call(s32[10]{0:T(128)S(1)} %get-tuple-element.33.tab, bf16[33,32,128]{2,1,0:T(8,128)(2,1)S(1)} %collective-permute-done.3.refs_0_.refs_8_, ...), custom_call_target="tpu_custom_call" | custom-call | flops 2684354560 | bytes 4194304 | tf_op jit(solution)/shard_map/grads/pallas_call | solution.py:207
  81.5 3.2 %collective-permute-start.10 = (bf16[8,64,128]{2,1,0:T(8,128)(2,1)S(1)}, bf16[8,64,128]{2,1,0:T(8,128)(2,1)S(1)}, u32[]{:S(2)}, u32[]{:S(2)}) collective-permute-start(bf16[8,64,128]{2,1,0:T(8,128)(2,1)S(1)} %get-tuple-element.29), channel_id=1, source_target_pairs={{0,8},{1,25},{4,12},{5,29},{8,16},{9,1},{12,20},{13,5},{16,24},{17... | collective-permute-start | bytes 393224 | tf_op jit(solution)/shard_map/ppermute | solution.py:262
  84.8 0.0 collective-permute-start.11
  84.8 6.7 %grads.6 = (bf16[8,64,128]{2,1,0:T(8,128)(2,1)S(1)}, bf16[8,64,128]{2,1,0:T(8,128)(2,1)S(1)}, f32[2048,128]{1,0:T(8,128)S(1)}, f32[2048,128]{1,0:T(8,128)S(1)}) custom-call(s32[10]{0:T(128)S(1)} %get-tuple-element.34.tab, bf16[33,32,128]{2,1,0:T(8,128)(2,1)S(1)} %collective-permute-done.3.refs_0_.refs_8_, ...), custom_call_target="tpu_custom_call" | custom-call | flops 2684354560 | bytes 4194304 | tf_op jit(solution)/shard_map/grads/pallas_call | solution.py:207
  91.5 0.0 collective-permute-done.7
  91.5 4.9 %collective-permute-start.12 = (bf16[8,64,128]{2,1,0:T(8,128)(2,1)S(1)}, bf16[8,64,128]{2,1,0:T(8,128)(2,1)S(1)}, u32[]{:S(2)}, u32[]{:S(2)}) collective-permute-start(bf16[8,64,128]{2,1,0:T(8,128)(2,1)S(1)} %get-tuple-element.31), channel_id=1, source_target_pairs={{0,4},{1,29},{4,8},{5,1},{8,12},{9,5},{12,16},{13,9},{16,20},{17,1... | collective-permute-start | bytes 393224 | tf_op jit(solution)/shard_map/ppermute | solution.py:262
  96.4 0.0 collective-permute-done.8
  96.4 0.0 collective-permute-start.13
  96.4 0.1 pad_add_fusion.tab
  96.4 3.5 %grads.7 = (f32[8,64,128]{2,1,0:T(8,128)S(1)}, bf16[32,144,128]{2,1,0:T(8,128)(2,1)S(1)}) custom-call(s32[9]{0:T(128)S(1)} %pad_add_fusion.tab, bf16[33,32,128]{2,1,0:T(8,128)(2,1)S(1)} %collective-permute-done.3.refs_0_.refs_8_, bf16[33,32,128]{2,1,0:T(8,128)(2,1)S(1)} %collective-permute-done.2.refs_1_.refs_9_, ...), custom_call_target="tpu_custom_call" | custom-call | flops 1342177280 | bytes 4194304 | tf_op jit(solution)/shard_map/grads/pallas_call | solution.py:207
  99.9 0.0 collective-permute-done.9
  99.9 0.0 collective-permute-done.10
  99.9 0.0 collective-permute-done.11
  99.9 0.0 collective-permute-done.12
  100.0 1.4 %collective-permute-done.13 = bf16[8,64,128]{2,1,0:T(8,128)(2,1)S(1)} collective-permute-done((bf16[8,64,128]{2,1,0:T(8,128)(2,1)S(1)}, bf16[8,64,128]{2,1,0:T(8,128)(2,1)S(1)}, u32[]{:S(2)}, u32[]{:S(2)}) %collective-permute-start.13) | collective-permute-done | bytes 131104 | tf_op jit(solution)/shard_map/ppermute | solution.py:262
  101.4 0.2 multiply_convert_fusion
  101.6 29.7 %all_to_all.16.x_ref = bf16[32,144,128]{2,1,0:T(8,128)(2,1)S(1)} all-to-all(bf16[32,144,128]{2,1,0:T(8,128)(2,1)S(1)} %constant_dynamic-update-slice_fusion), channel_id=1, replica_groups=mesh['y'=4,'xh'=2,'z'=8,'xl'=2,'c'=2] {'xl','c','y','xh'}, dimensions={0} | all-to-all | bytes 2359296 | tf_op jit(solution)/shard_map/all_to_all | solution.py:266
  131.3 1.5 %unpack.1 = (f32[16,4096]{1,0:T(8,128)}, f32[64,4096]{1,0:T(8,128)}, f32[64,4096]{1,0:T(8,128)}) custom-call(bf16[32,144,128]{2,1,0:T(8,128)(2,1)S(1)} %all_to_all.16.x_ref), custom_call_target="tpu_custom_call" | custom-call | flops 1000000 | bytes 3000000 | tf_op jit(solution)/shard_map/unpack/pallas_call | solution.py:244
  (6 shorter events, 0.1 us)
Async XLA Ops:
  21.1 11.6 %collective-permute-start = (bf16[33,32,128]{2,1,0:T(8,128)(2,1)S(1)}, bf16[33,32,128]{2,1,0:T(8,128)(2,1)S(1)}, u32[]{:S(2)}, u32[]{:S(2)}) collective-permute-start(bf16[33,32,128]{2,1,0:T(8,128)(2,1)S(1)} %gather_stats.1.refs_4_.refs_12_), channel_id=1, source_target_pairs={{0,4},{1,29},{4,8},{5,1},{8,12},{9,5},{12,16},{13,9},{16,20},{17,1... | collective-permute-start | bytes 811016 | tf_op jit(solution)/shard_map/ppermute | solution.py:262
  26.8 15.6 %collective-permute-start.4 = (bf16[33,32,128]{2,1,0:T(8,128)(2,1)S(1)}, bf16[33,32,128]{2,1,0:T(8,128)(2,1)S(1)}, u32[]{:S(2)}, u32[]{:S(2)}) collective-permute-start(bf16[33,32,128]{2,1,0:T(8,128)(2,1)S(1)} %gather_stats.1.refs_4_.refs_12_), channel_id=1, source_target_pairs={{0,28},{1,5},{4,0},{5,9},{8,4},{9,13},{12,8},{13,17},{16,12},{17,2... | collective-permute-start | bytes 811016 | tf_op jit(solution)/shard_map/ppermute | solution.py:262
  32.7 9.7 %collective-permute-start.1 = (bf16[33,32,128]{2,1,0:T(8,128)(2,1)S(1)}, bf16[33,32,128]{2,1,0:T(8,128)(2,1)S(1)}, u32[]{:S(2)}, u32[]{:S(2)}) collective-permute-start(bf16[33,32,128]{2,1,0:T(8,128)(2,1)S(1)} %collective-permute-done.refs_3_.refs_11_), channel_id=1, source_target_pairs={{0,4},{1,29},{4,8},{5,1},{8,12},{9,5},{12,16},{13,9},{16,20},{17,1... | collective-permute-start | bytes 811016 | tf_op jit(solution)/shard_map/ppermute | solution.py:262
  38.5 6.6 %copy-start.2 = (s32[3]{0:T(128)S(1)}, s32[3]{0:T(128)}, u32[]{:S(2)}) copy-start(s32[3]{0:T(128)} %constant.89.clone) | copy-start | bytes 40
  38.5 6.7 %copy-start = (s32[2]{0:T(128)S(1)}, s32[2]{0:T(128)}, u32[]{:S(2)}) copy-start(s32[2]{0:T(128)} %constant.91.clone) | copy-start | bytes 28
  38.5 6.7 %copy-start.1 = (s32[2]{0:T(128)S(1)}, s32[2]{0:T(128)}, u32[]{:S(2)}) copy-start(s32[2]{0:T(128)} %constant.90.clone) | copy-start | bytes 28
  38.5 19.9 %all-to-all-start.1 = ((bf16[32,128,128]{2,1,0:T(8,128)(2,1)}), bf16[32,128,128]{2,1,0:T(8,128)(2,1)S(1)}, u32[]{:S(2)}, u32[]{:S(2)}) async-start(bf16[32,128,128]{2,1,0:T(8,128)(2,1)} %pack_keys.1), calls=%async_computation.1 | async-start | bytes 2097152 | tf_op jit(solution)/shard_map/all_to_all | solution.py:266
  42.4 8.6 %collective-permute-start.5 = (bf16[33,32,128]{2,1,0:T(8,128)(2,1)S(1)}, bf16[33,32,128]{2,1,0:T(8,128)(2,1)S(1)}, u32[]{:S(2)}, u32[]{:S(2)}) collective-permute-start(bf16[33,32,128]{2,1,0:T(8,128)(2,1)S(1)} %collective-permute-done.4.refs_5_.refs_13_), channel_id=1, source_target_pairs={{0,28},{1,5},{4,0},{5,9},{8,4},{9,13},{12,8},{13,17},{16,12},{17,2... | collective-permute-start | bytes 811016 | tf_op jit(solution)/shard_map/ppermute | solution.py:262
  42.5 8.5 %collective-permute-start.2 = (bf16[33,32,128]{2,1,0:T(8,128)(2,1)S(1)}, bf16[33,32,128]{2,1,0:T(8,128)(2,1)S(1)}, u32[]{:S(2)}, u32[]{:S(2)}) collective-permute-start(bf16[33,32,128]{2,1,0:T(8,128)(2,1)S(1)} %collective-permute-done.1.refs_2_.refs_10_), channel_id=1, source_target_pairs={{0,4},{1,29},{4,8},{5,1},{8,12},{9,5},{12,16},{13,9},{16,20},{17,1... | collective-permute-start | bytes 811016 | tf_op jit(solution)/shard_map/ppermute | solution.py:262
  51.0 7.7 %collective-permute-start.6 = (bf16[33,32,128]{2,1,0:T(8,128)(2,1)S(1)}, bf16[33,32,128]{2,1,0:T(8,128)(2,1)S(1)}, u32[]{:S(2)}, u32[]{:S(2)}) collective-permute-start(bf16[33,32,128]{2,1,0:T(8,128)(2,1)S(1)} %collective-permute-done.5.refs_6_.refs_14_), channel_id=1, source_target_pairs={{0,28},{1,5},{4,0},{5,9},{8,4},{9,13},{12,8},{13,17},{16,12},{17,2... | collective-permute-start | bytes 811016 | tf_op jit(solution)/shard_map/ppermute | solution.py:262
  51.0 8.4 %collective-permute-start.3 = (bf16[33,32,128]{2,1,0:T(8,128)(2,1)S(1)}, bf16[33,32,128]{2,1,0:T(8,128)(2,1)S(1)}, u32[]{:S(2)}, u32[]{:S(2)}) collective-permute-start(bf16[33,32,128]{2,1,0:T(8,128)(2,1)S(1)} %collective-permute-done.2.refs_1_.refs_9_), channel_id=1, source_target_pairs={{0,4},{1,29},{4,8},{5,1},{8,12},{9,5},{12,16},{13,9},{16,20},{17,1... | collective-permute-start | bytes 811016 | tf_op jit(solution)/shard_map/ppermute | solution.py:262
  69.1 22.4 %collective-permute-start.7 = (bf16[8,64,128]{2,1,0:T(8,128)(2,1)S(1)}, bf16[8,64,128]{2,1,0:T(8,128)(2,1)S(1)}, u32[]{:S(2)}, u32[]{:S(2)}) collective-permute-start(bf16[8,64,128]{2,1,0:T(8,128)(2,1)S(1)} %get-tuple-element.26), channel_id=1, source_target_pairs={{0,16},{1,17},{4,20},{5,21},{8,24},{9,25},{12,28},{13,29},{16,0},{... | collective-permute-start | bytes 393224 | tf_op jit(solution)/shard_map/ppermute | solution.py:262
  71.5 24.9 %collective-permute-start.8 = (bf16[8,64,128]{2,1,0:T(8,128)(2,1)S(1)}, bf16[8,64,128]{2,1,0:T(8,128)(2,1)S(1)}, u32[]{:S(2)}, u32[]{:S(2)}) collective-permute-start(bf16[8,64,128]{2,1,0:T(8,128)(2,1)S(1)} %get-tuple-element.27), channel_id=1, source_target_pairs={{0,12},{1,21},{4,16},{5,25},{8,20},{9,29},{12,24},{13,1},{16,28},{... | collective-permute-start | bytes 393224 | tf_op jit(solution)/shard_map/ppermute | solution.py:262
  73.5 26.4 %collective-permute-start.9 = (bf16[8,64,128]{2,1,0:T(8,128)(2,1)S(1)}, bf16[8,64,128]{2,1,0:T(8,128)(2,1)S(1)}, u32[]{:S(2)}, u32[]{:S(2)}) collective-permute-start(bf16[8,64,128]{2,1,0:T(8,128)(2,1)S(1)} %get-tuple-element.28), channel_id=1, source_target_pairs={{0,20},{1,13},{4,24},{5,17},{8,28},{9,21},{12,0},{13,25},{16,4},{1... | collective-permute-start | bytes 393224 | tf_op jit(solution)/shard_map/ppermute | solution.py:262
  81.5 18.4 %collective-permute-start.10 = (bf16[8,64,128]{2,1,0:T(8,128)(2,1)S(1)}, bf16[8,64,128]{2,1,0:T(8,128)(2,1)S(1)}, u32[]{:S(2)}, u32[]{:S(2)}) collective-permute-start(bf16[8,64,128]{2,1,0:T(8,128)(2,1)S(1)} %get-tuple-element.29), channel_id=1, source_target_pairs={{0,8},{1,25},{4,12},{5,29},{8,16},{9,1},{12,20},{13,5},{16,24},{17... | collective-permute-start | bytes 393224 | tf_op jit(solution)/shard_map/ppermute | solution.py:262
  84.8 15.2 %collective-permute-start.11 = (bf16[8,64,128]{2,1,0:T(8,128)(2,1)S(1)}, bf16[8,64,128]{2,1,0:T(8,128)(2,1)S(1)}, u32[]{:S(2)}, u32[]{:S(2)}) collective-permute-start(bf16[8,64,128]{2,1,0:T(8,128)(2,1)S(1)} %get-tuple-element.30), channel_id=1, source_target_pairs={{0,24},{1,9},{4,28},{5,13},{8,0},{9,17},{12,4},{13,21},{16,8},{17,... | collective-permute-start | bytes 393224 | tf_op jit(solution)/shard_map/ppermute | solution.py:262
  91.5 8.4 %collective-permute-start.12 = (bf16[8,64,128]{2,1,0:T(8,128)(2,1)S(1)}, bf16[8,64,128]{2,1,0:T(8,128)(2,1)S(1)}, u32[]{:S(2)}, u32[]{:S(2)}) collective-permute-start(bf16[8,64,128]{2,1,0:T(8,128)(2,1)S(1)} %get-tuple-element.31), channel_id=1, source_target_pairs={{0,4},{1,29},{4,8},{5,1},{8,12},{9,5},{12,16},{13,9},{16,20},{17,1... | collective-permute-start | bytes 393224 | tf_op jit(solution)/shard_map/ppermute | solution.py:262
  96.4 5.0 %collective-permute-start.13 = (bf16[8,64,128]{2,1,0:T(8,128)(2,1)S(1)}, bf16[8,64,128]{2,1,0:T(8,128)(2,1)S(1)}, u32[]{:S(2)}, u32[]{:S(2)}) collective-permute-start(bf16[8,64,128]{2,1,0:T(8,128)(2,1)S(1)} %get-tuple-element.32), channel_id=1, source_target_pairs={{0,28},{1,5},{4,0},{5,9},{8,4},{9,13},{12,8},{13,17},{16,12},{17,2... | collective-permute-start | bytes 393224 | tf_op jit(solution)/shard_map/ppermute | solution.py:262

commit v6 on v5

--- a/solution.py
+++ b/solution.py
@@ -130,72 +130,79 @@
     return q, g, jnp.concatenate(st, axis=1), jnp.concatenate(de, axis=1)
 
 
-def block_grads(to_z, parts, tiles, kv_ref, dk_ref, dv_ref):
+def block_grads(to_z, parts, tiles, kv_ref, dk_ref, dv_ref, total_ref):
     q, g, st, de = queries_of(to_z, parts, tiles)
     per = 8
     bk = per * KROWS
-    total = None
-    for j in range(NSP // per):
-        k = kv_ref[j * per : (j + 1) * per, 0:KROWS, :].reshape(bk, DH)
-        v = kv_ref[j * per : (j + 1) * per, KROWS : 2 * KROWS, :].reshape(bk, DH)
-        at = slice(j * bk, (j + 1) * bk)
+
+    def one(j):
+        sources = pl.ds(pl.multiple_of(j * per, per), per)
+        k = kv_ref[sources, 0:KROWS, :].reshape(bk, DH)
+        v = kv_ref[sources, KROWS : 2 * KROWS, :].reshape(bk, DH)
+        at = pl.ds(pl.multiple_of(j * bk, bk), bk)
         p = jnp.exp2(dot(k, q, ((1,), (1,))) * (ROOT * LOG2E) - st)
         ds = (p * (dot(v, g, ((1,), (1,))) - de)).astype(BF16)
         dv_ref[at, :] += dot(p.astype(BF16), g, ((1,), (0,)))
         dk_ref[at, :] += dot(ds, q, ((1,), (0,)))
-        part = dot(ds, k, ((0,), (0,)))
-        total = part if total is None else total + part
-    return total.reshape(NZ, PART, DH)
-
-
-def grads(count, first, last, tab, *refs):
+        return dot(ds, k, ((0,), (0,)))
+
+    total_ref[...] = jnp.zeros_like(total_ref)
+
+    def some(i, nothing):
+        parts = [one(i * UNROLL + j) for j in range(UNROLL)]
+        total_ref[...] += functools.reduce(jnp.add, parts)
+        return nothing
+
+    lax.fori_loop(0, NSP // per // UNROLL, some, 0)
+    return total_ref[...].reshape(NZ, PART, DH)
+
+
+def grads(first, added, last, tab, *refs):
     parts = refs[:NZ]
     tiles = refs[NZ : 2 * NZ]
     kv_ref = refs[2 * NZ]
-    rest = refs[2 * NZ + 1 :]
+    rest, total_ref = refs[2 * NZ + 1 : -1], refs[-1]
     if not first:
         dk_in, dv_in = rest[:2]
         rest = rest[2:]
-    dq_refs = rest[:count]
+    if added:
+        sum_ref = rest[0]
+        rest = rest[1:]
+    dq_ref = rest[0]
     dk_ref, dv_ref = rest[-2:]
-    step = pl.program_id(0)
-
-    @pl.when(step == 0)
-    def _():
-        dk_ref[...] = jnp.zeros_like(dk_ref) if first else dk_in[...]
-        dv_ref[...] = jnp.zeros_like(dv_ref) if first else dv_in[...]
-
-    total = block_grads(tab[step], parts, tiles, kv_ref, dk_ref, dv_ref)
-    for n, dq_ref in enumerate(dq_refs):
-
-        @pl.when(step == n)
-        def _(dq_ref=dq_ref):
-            for j in range(NZ):
-                dq_ref[tab[count + j]] = total[j].astype(dq_ref.dtype)
-
+    dk_ref[...] = jnp.zeros_like(dk_ref) if first else dk_in[...]
+    dv_ref[...] = jnp.zeros_like(dv_ref) if first else dv_in[...]
+    total = block_grads(tab[0], parts, tiles, kv_ref, dk_ref, dv_ref, total_ref)
+    for j in range(NZ):
+        at = tab[1 + j]
+        part = total[j]
+        if added:
+            part = part + sum_ref[at].astype(F32)
+        dq_ref[at] = part.astype(dq_ref.dtype)
     if last:
-        out_ref = rest[count]
-
-        @pl.when(step == count - 1)
-        def _():
-            dk = (dk_ref[...] * (ROOT * SCALE)).astype(BF16)
-            dv = (dv_ref[...] * SCALE).astype(BF16)
-            out_ref[:, 0:KROWS, :] = dk.reshape(NSP, KROWS, DH)
-            out_ref[:, KROWS : 2 * KROWS, :] = dv.reshape(NSP, KROWS, DH)
+        out_ref = rest[1]
+        dk = (dk_ref[...] * (ROOT * SCALE)).astype(BF16)
+        dv = (dv_ref[...] * SCALE).astype(BF16)
+        out_ref[:, 0:KROWS, :] = dk.reshape(NSP, KROWS, DH)
+        out_ref[:, KROWS : 2 * KROWS, :] = dv.reshape(NSP, KROWS, DH)
 
 
 OUT_ROWS = 2 * KROWS + QROWS
-
-
-def grads_call(count, first, last, tab, parts, kv, sums=()):
-    pairs = count * QB * KLEN
+UNROLL = 2
+ORDER = (4, -3, 3, -2, 2, -1, 1, 0)
+
+
+def grads_call(last, tab, parts, kv, sums, arrived):
+    pairs = QB * KLEN
     whole = pl.BlockSpec((KLEN, DH), lambda i, t: (0, 0))
     part = pl.BlockSpec((PART // SHARE, WIDE, DH), lambda i, t: (t[i], 0, 0))
     tile = pl.BlockSpec((1, 8, DH), lambda i, t: (NSP, t[i] // 2, 0))
+    dq = pl.BlockSpec((NZ, PART, DH), lambda i, t: (0, 0, 0))
     in_specs = [part] * NZ + [tile] * NZ
     in_specs.append(pl.BlockSpec((NSP, 2 * KROWS, DH), lambda i, t: (0, 0, 0)))
-    out_specs = [pl.BlockSpec((NZ, PART, DH), lambda i, t: (0, 0, 0))] * count
-    out_shape = [jax.ShapeDtypeStruct((NZ, PART, DH), F32 if last else BF16)] * count
+    in_specs += [whole] * len(sums) + [dq] * len(arrived)
+    out_specs = [dq]
+    out_shape = [jax.ShapeDtypeStruct((NZ, PART, DH), F32 if last else BF16)]
     scratch = []
     if last:
         out_specs.append(pl.BlockSpec((NSP, OUT_ROWS, DH), lambda i, t: (0, 0, 0)))
@@ -205,19 +212,19 @@
         out_specs += [whole] * 2
         out_shape += [jax.ShapeDtypeStruct((KLEN, DH), F32)] * 2
     return pl.pallas_call(
-        functools.partial(grads, count, first, last),
+        functools.partial(grads, not sums, bool(arrived), last),
         grid_spec=pltpu.PrefetchScalarGridSpec(
             num_scalar_prefetch=1,
-            grid=(count,),
-            in_specs=in_specs + [whole] * len(sums),
+            grid=(1,),
+            in_specs=in_specs,
             out_specs=out_specs,
-            scratch_shapes=scratch,
+            scratch_shapes=[*scratch, pltpu.VMEM((QB, DH), F32)],
         ),
         out_shape=out_shape,
         compiler_params=pltpu.CompilerParams(vmem_limit_bytes=26 << 20),
         cost_estimate=cost(pairs * 10 * DH, 4 << 20, pairs),
         name="grads",
-    )(tab, *parts, *parts, kv, *sums)
+    )(tab, *parts, *parts, kv, *sums, *arrived)
 
 
 def unpack(x_ref, *refs):
@@ -285,22 +292,15 @@
     sign = 1 - 2 * lax.axis_index("c")
     where = (z + sign * jnp.arange(-half, half, dtype=jnp.int32)) % NZ
 
-    sent = []
+    chain = {1: (), -1: ()}
     sums = ()
-    groups = ((4, 3, -3), (2, -2), (1, -1), (0,))
-    for n, group in enumerate(groups):
-        tab = jnp.concatenate([(z + sign * jnp.array(group, jnp.int32)) % NZ, where])
-        first, last = n == 0, n == len(groups) - 1
-        out = grads_call(
-            len(group), first, last, tab.astype(jnp.int32), parts, kv, sums
-        )
-        sums = out[len(group) :]
-        for by, dq in zip(group, out):
-            if by:
-                sent.append(turn(dq, by))
-            else:
-                mine = dq
-    mine = mine + sum(x.astype(F32) for x in sent)
+    for to in ORDER:
+        tab = jnp.concatenate([((z + sign * to) % NZ).reshape(1), where]).astype(jnp.int32)
+        way = 1 if to > 0 else -1
+        dq, *sums = grads_call(to == 0, tab, parts, kv, sums, chain[way] if to else ())
+        if to:
+            chain[way] = (turn(dq, way),)
+    mine = dq + (chain[1][0].astype(F32) + chain[-1][0].astype(F32))
     mine = (mine * (ROOT * SCALE)).reshape(NKV, NXC, QROWS, DH)
     mine = jnp.swapaxes(mine, 0, 1).reshape(NSP, QROWS, DH).astype(BF16)
     packed = lax.dynamic_update_slice(sums[0], mine, (0, 2 * KROWS, 0))

time: 133 us -> 133 us (level)
  Pallas kernels: 32.7 us -> 37.3 us
  starting transfers between devices: 32.1 us -> 29.6 us
  waiting for transfers between devices: 18.8 us -> 16.7 us
    pallas_call x4 -> x8, Pallas kernels: 26.7 us -> 31.3 us  [grads_call(): pl.pallas_call(functools.partial(grads, not sums, bool(arrived), last), g...]
    all_to_all x1, waiting for transfers between devices: 4.61 us -> 0.01 us  [regroup(): return lax.all_to_all(x, PLANE, split_axis=0, concat_axis=0, tiled=True)]
    ppermute x14, waiting for transfers between devices: 14.1 us -> 16.7 us  [turn(): return lax.ppermute(x, ('z', 'c'), pairs)]
    ppermute x14, starting transfers between devices: 28.2 us -> 25.8 us  [turn(): return lax.ppermute(x, ('z', 'c'), pairs)]
  transfers between devices with their start and end apart: 15 -> 15, of which waited for: 6 -> 4; matrix products, arithmetic and copies ran while one was open for 0% -> 0% of each run, Pallas kernels for 15% -> 22%
where the time goes in v6:
time: 133 us
  blocking collectives  48 us (36%)
  Pallas kernels  37.3 us (28%)
  starting transfers between devices  29.6 us (22%)
  waiting for transfers between devices  16.7 us (13%)
    all_to_all x2, blocking collectives, regroup(): return lax.all_to_all(x, PLANE, split_axis=0, concat_axis=0, tiled=True)  48 us
    pallas_call x8, Pallas kernels, grads_call(): pl.pallas_call(functools.partial(grads, not sums, bool(arrived), last), g...  31.3 us
    ppermute x14, starting transfers between devices, turn(): return lax.ppermute(x, ('z', 'c'), pairs)  25.8 us
    ppermute x14, waiting for transfers between devices, turn(): return lax.ppermute(x, ('z', 'c'), pairs)  16.7 us
    all_to_all x1, starting transfers between devices, regroup(): return lax.all_to_all(x, PLANE, split_axis=0, concat_axis=0, tiled=True)  3.72 us
  transfers between devices with their start and end apart: 15, of which 4 were waited for; matrix products, arithmetic and copies ran while one was open for 0% of the time, Pallas kernels for 22%

profile of v6, /device:TPU:1, one launch (start us, length us, event | category | flops | bytes accessed | tf_op | source)
XLA Modules:
  0.0 132.9 jit_solution(11894194513335622159)
XLA Ops:
  0.6 2.1 %pack_queries.1 = bf16[32,40,128]{2,1,0:T(8,128)(2,1)} custom-call(s32[1]{0:T(128)} %bitcast.1.b_ref, bf16[128,4096]{1,0:T(8,128)(2,1)} %q_ref.1, bf16[128,4096]{1,0:T(8,128)(2,1)} %g_ref.1, bf16[128,4096]{1,0:T(8,128)(2,1)} %o_ref.1, f32[32,128]{1,0:T(8,128)} %bitcast.16), custom_call_target="tpu_custom_call" | custom-call | flops 1000000 | bytes 1000000 | tf_op jit(solution)/shard_map/pack_queries/pallas_call | solution.py:75
  2.8 18.3 %all_to_all.15.x_ref = bf16[32,40,128]{2,1,0:T(8,128)(2,1)S(1)} all-to-all(bf16[32,40,128]{2,1,0:T(8,128)(2,1)} %pack_queries.1), channel_id=1, replica_groups=mesh['y'=4,'xh'=2,'z'=8,'xl'=2,'c'=2] {'xl','c','y','xh'}, dimensions={0} | all-to-all | bytes 655360 | tf_op jit(solution)/shard_map/all_to_all | solution.py:273
  21.1 5.7 %collective-permute-start = (bf16[33,32,128]{2,1,0:T(8,128)(2,1)S(1)}, bf16[33,32,128]{2,1,0:T(8,128)(2,1)S(1)}, u32[]{:S(2)}, u32[]{:S(2)}) collective-permute-start(bf16[33,32,128]{2,1,0:T(8,128)(2,1)S(1)} %gather_stats.1.refs_4_.refs_12_), channel_id=1, source_target_pairs={{0,4},{1,29},{4,8},{5,1},{8,12},{9,5},{12,16},{13,9},{16,20},{17,1... | collective-permute-start | bytes 811016 | tf_op jit(solution)/shard_map/ppermute | solution.py:269
  26.8 2.4 %pack_keys.1 = bf16[32,128,128]{2,1,0:T(8,128)(2,1)} custom-call(bf16[64,4096]{1,0:T(8,128)(2,1)} %k_ref.1, bf16[64,4096]{1,0:T(8,128)(2,1)} %v_ref.1), custom_call_target="tpu_custom_call" | custom-call | flops 1000000 | bytes 2000000 | tf_op jit(solution)/shard_map/pack_keys/pallas_call | solution.py:113
  29.1 3.7 %all-to-all-start.1 = ((bf16[32,128,128]{2,1,0:T(8,128)(2,1)}), bf16[32,128,128]{2,1,0:T(8,128)(2,1)S(1)}, u32[]{:S(2)}, u32[]{:S(2)}) async-start(bf16[32,128,128]{2,1,0:T(8,128)(2,1)} %pack_keys.1), calls=%async_computation.1 | async-start | bytes 2097152 | tf_op jit(solution)/shard_map/all_to_all | solution.py:273
  32.8 0.1 collective-permute-start.4
  32.9 0.0 collective-permute-done.refs_3_.refs_11_
  32.9 2.7 %collective-permute-start.1 = (bf16[33,32,128]{2,1,0:T(8,128)(2,1)S(1)}, bf16[33,32,128]{2,1,0:T(8,128)(2,1)S(1)}, u32[]{:S(2)}, u32[]{:S(2)}) collective-permute-start(bf16[33,32,128]{2,1,0:T(8,128)(2,1)S(1)} %collective-permute-done.refs_3_.refs_11_), channel_id=1, source_target_pairs={{0,4},{1,29},{4,8},{5,1},{8,12},{9,5},{12,16},{13,9},{16,20},{17,1... | collective-permute-start | bytes 811016 | tf_op jit(solution)/shard_map/ppermute | solution.py:269
  35.6 5.9 %collective-permute-done.4.refs_5_.refs_13_ = bf16[33,32,128]{2,1,0:T(8,128)(2,1)S(1)} collective-permute-done((bf16[33,32,128]{2,1,0:T(8,128)(2,1)S(1)}, bf16[33,32,128]{2,1,0:T(8,128)(2,1)S(1)}, u32[]{:S(2)}, u32[]{:S(2)}) %collective-permute-start.4) | collective-permute-done | bytes 270368 | tf_op jit(solution)/shard_map/ppermute | solution.py:269
  41.5 0.0 collective-permute-start.5
  41.5 0.0 collective-permute-done.1.refs_2_.refs_10_
  41.5 2.7 %collective-permute-start.2 = (bf16[33,32,128]{2,1,0:T(8,128)(2,1)S(1)}, bf16[33,32,128]{2,1,0:T(8,128)(2,1)S(1)}, u32[]{:S(2)}, u32[]{:S(2)}) collective-permute-start(bf16[33,32,128]{2,1,0:T(8,128)(2,1)S(1)} %collective-permute-done.1.refs_2_.refs_10_), channel_id=1, source_target_pairs={{0,4},{1,29},{4,8},{5,1},{8,12},{9,5},{12,16},{13,9},{16,20},{17,1... | collective-permute-start | bytes 811016 | tf_op jit(solution)/shard_map/ppermute | solution.py:269
  44.2 5.0 %collective-permute-done.5.refs_6_.refs_14_ = bf16[33,32,128]{2,1,0:T(8,128)(2,1)S(1)} collective-permute-done((bf16[33,32,128]{2,1,0:T(8,128)(2,1)S(1)}, bf16[33,32,128]{2,1,0:T(8,128)(2,1)S(1)}, u32[]{:S(2)}, u32[]{:S(2)}) %collective-permute-start.5) | collective-permute-done | bytes 270368 | tf_op jit(solution)/shard_map/ppermute | solution.py:269
  49.2 0.0 collective-permute-start.6
  49.2 0.0 collective-permute-done.2.refs_1_.refs_9_
  49.2 2.8 %collective-permute-start.3 = (bf16[33,32,128]{2,1,0:T(8,128)(2,1)S(1)}, bf16[33,32,128]{2,1,0:T(8,128)(2,1)S(1)}, u32[]{:S(2)}, u32[]{:S(2)}) collective-permute-start(bf16[33,32,128]{2,1,0:T(8,128)(2,1)S(1)} %collective-permute-done.2.refs_1_.refs_9_), channel_id=1, source_target_pairs={{0,4},{1,29},{4,8},{5,1},{8,12},{9,5},{12,16},{13,9},{16,20},{17,1... | collective-permute-start | bytes 811016 | tf_op jit(solution)/shard_map/ppermute | solution.py:269
  52.0 0.1 pad_add_fusion.7
  52.1 0.0 all-to-all-done.1.refs_16_
  52.1 4.0 %collective-permute-done.6.refs_7_.refs_15_ = bf16[33,32,128]{2,1,0:T(8,128)(2,1)S(1)} collective-permute-done((bf16[33,32,128]{2,1,0:T(8,128)(2,1)S(1)}, bf16[33,32,128]{2,1,0:T(8,128)(2,1)S(1)}, u32[]{:S(2)}, u32[]{:S(2)}) %collective-permute-start.6) | collective-permute-done | bytes 270368 | tf_op jit(solution)/shard_map/ppermute | solution.py:269
  56.1 1.8 %collective-permute-done.3.refs_0_.refs_8_ = bf16[33,32,128]{2,1,0:T(8,128)(2,1)S(1)} collective-permute-done((bf16[33,32,128]{2,1,0:T(8,128)(2,1)S(1)}, bf16[33,32,128]{2,1,0:T(8,128)(2,1)S(1)}, u32[]{:S(2)}, u32[]{:S(2)}) %collective-permute-start.3) | collective-permute-done | bytes 270368 | tf_op jit(solution)/shard_map/ppermute | solution.py:269
  57.8 3.9 %grads.8 = (bf16[8,64,128]{2,1,0:T(8,128)(2,1)S(1)}, f32[2048,128]{1,0:T(8,128)S(1)}, f32[2048,128]{1,0:T(8,128)S(1)}) custom-call(s32[9]{0:T(128)S(1)} %get-tuple-element.49.tab, bf16[33,32,128]{2,1,0:T(8,128)(2,1)S(1)} %collective-permute-done.3.refs_0_.refs_8_, bf16[33,32,128]{2,1,0:T(8,128)(2,1)S(1)} %collective-permute-done.2.refs_1_.refs_9_, ...), custom_call_target="tpu_custom_call" | custom-call | flops 1342177280 | bytes 4194304 | tf_op jit(solution)/shard_map/grads/pallas_call | solution.py:214
  61.7 3.2 %collective-permute-start.7 = (bf16[8,64,128]{2,1,0:T(8,128)(2,1)S(1)}, bf16[8,64,128]{2,1,0:T(8,128)(2,1)S(1)}, u32[]{:S(2)}, u32[]{:S(2)}) collective-permute-start(bf16[8,64,128]{2,1,0:T(8,128)(2,1)S(1)} %get-tuple-element.30), channel_id=1, source_target_pairs={{0,4},{1,29},{4,8},{5,1},{8,12},{9,5},{12,16},{13,9},{16,20},{17,1... | collective-permute-start | bytes 393224 | tf_op jit(solution)/shard_map/ppermute | solution.py:269
  64.9 0.1 pad_add_fusion.6
  64.9 3.9 %grads.9 = (bf16[8,64,128]{2,1,0:T(8,128)(2,1)S(1)}, f32[2048,128]{1,0:T(8,128)S(1)}, f32[2048,128]{1,0:T(8,128)S(1)}) custom-call(s32[9]{0:T(128)S(1)} %get-tuple-element.55.tab, bf16[33,32,128]{2,1,0:T(8,128)(2,1)S(1)} %collective-permute-done.3.refs_0_.refs_8_, bf16[33,32,128]{2,1,0:T(8,128)(2,1)S(1)} %collective-permute-done.2.refs_1_.refs_9_, ...), custom_call_target="tpu_custom_call" | custom-call | flops 1342177280 | bytes 4194304 | tf_op jit(solution)/shard_map/grads/pallas_call | solution.py:214
  68.8 0.3 collective-permute-start.8
  69.1 0.0 collective-permute-done.7.refs_19_
  69.1 3.9 %grads.10 = (bf16[8,64,128]{2,1,0:T(8,128)(2,1)S(1)}, f32[2048,128]{1,0:T(8,128)S(1)}, f32[2048,128]{1,0:T(8,128)S(1)}) custom-call(s32[9]{0:T(128)S(1)} %get-tuple-element.54.tab, bf16[33,32,128]{2,1,0:T(8,128)(2,1)S(1)} %collective-permute-done.3.refs_0_.refs_8_, bf16[33,32,128]{2,1,0:T(8,128)(2,1)S(1)} %collective-permute-done.2.refs_1_.refs_9_, ...), custom_call_target="tpu_custom_call" | custom-call | flops 1342177280 | bytes 4194304 | tf_op jit(solution)/shard_map/grads/pallas_call | solution.py:214
  73.0 2.7 %collective-permute-start.9 = (bf16[8,64,128]{2,1,0:T(8,128)(2,1)S(1)}, bf16[8,64,128]{2,1,0:T(8,128)(2,1)S(1)}, u32[]{:S(2)}, u32[]{:S(2)}) collective-permute-start(bf16[8,64,128]{2,1,0:T(8,128)(2,1)S(1)} %get-tuple-element.36), channel_id=1, source_target_pairs={{0,4},{1,29},{4,8},{5,1},{8,12},{9,5},{12,16},{13,9},{16,20},{17,1... | collective-permute-start | bytes 393224 | tf_op jit(solution)/shard_map/ppermute | solution.py:269
  75.8 0.0 collective-permute-done.8.refs_19_
  75.8 3.9 %grads.11 = (bf16[8,64,128]{2,1,0:T(8,128)(2,1)S(1)}, f32[2048,128]{1,0:T(8,128)S(1)}, f32[2048,128]{1,0:T(8,128)S(1)}) custom-call(s32[9]{0:T(128)S(1)} %get-tuple-element.53.tab, bf16[33,32,128]{2,1,0:T(8,128)(2,1)S(1)} %collective-permute-done.3.refs_0_.refs_8_, bf16[33,32,128]{2,1,0:T(8,128)(2,1)S(1)} %collective-permute-done.2.refs_1_.refs_9_, ...), custom_call_target="tpu_custom_call" | custom-call | flops 1342177280 | bytes 4194304 | tf_op jit(solution)/shard_map/grads/pallas_call | solution.py:214
  79.7 0.1 collective-permute-start.10
  79.8 0.0 collective-permute-done.9.refs_19_
  79.8 3.9 %grads.12 = (bf16[8,64,128]{2,1,0:T(8,128)(2,1)S(1)}, f32[2048,128]{1,0:T(8,128)S(1)}, f32[2048,128]{1,0:T(8,128)S(1)}) custom-call(s32[9]{0:T(128)S(1)} %get-tuple-element.52.tab, bf16[33,32,128]{2,1,0:T(8,128)(2,1)S(1)} %collective-permute-done.3.refs_0_.refs_8_, bf16[33,32,128]{2,1,0:T(8,128)(2,1)S(1)} %collective-permute-done.2.refs_1_.refs_9_, ...), custom_call_target="tpu_custom_call" | custom-call | flops 1342177280 | bytes 4194304 | tf_op jit(solution)/shard_map/grads/pallas_call | solution.py:214
  83.7 2.7 %collective-permute-start.11 = (bf16[8,64,128]{2,1,0:T(8,128)(2,1)S(1)}, bf16[8,64,128]{2,1,0:T(8,128)(2,1)S(1)}, u32[]{:S(2)}, u32[]{:S(2)}) collective-permute-start(bf16[8,64,128]{2,1,0:T(8,128)(2,1)S(1)} %get-tuple-element.42), channel_id=1, source_target_pairs={{0,4},{1,29},{4,8},{5,1},{8,12},{9,5},{12,16},{13,9},{16,20},{17,1... | collective-permute-start | bytes 393224 | tf_op jit(solution)/shard_map/ppermute | solution.py:269
  86.4 0.0 collective-permute-done.10.refs_19_
  86.4 3.9 %grads.13 = (bf16[8,64,128]{2,1,0:T(8,128)(2,1)S(1)}, f32[2048,128]{1,0:T(8,128)S(1)}, f32[2048,128]{1,0:T(8,128)S(1)}) custom-call(s32[9]{0:T(128)S(1)} %get-tuple-element.51.tab, bf16[33,32,128]{2,1,0:T(8,128)(2,1)S(1)} %collective-permute-done.3.refs_0_.refs_8_, bf16[33,32,128]{2,1,0:T(8,128)(2,1)S(1)} %collective-permute-done.2.refs_1_.refs_9_, ...), custom_call_target="tpu_custom_call" | custom-call | flops 1342177280 | bytes 4194304 | tf_op jit(solution)/shard_map/grads/pallas_call | solution.py:214
  90.3 0.1 collective-permute-start.13
  90.4 0.0 collective-permute-done.11.refs_19_
  90.4 3.9 %grads.14 = (bf16[8,64,128]{2,1,0:T(8,128)(2,1)S(1)}, f32[2048,128]{1,0:T(8,128)S(1)}, f32[2048,128]{1,0:T(8,128)S(1)}) custom-call(s32[9]{0:T(128)S(1)} %get-tuple-element.50.tab, bf16[33,32,128]{2,1,0:T(8,128)(2,1)S(1)} %collective-permute-done.3.refs_0_.refs_8_, bf16[33,32,128]{2,1,0:T(8,128)(2,1)S(1)} %collective-permute-done.2.refs_1_.refs_9_, ...), custom_call_target="tpu_custom_call" | custom-call | flops 1342177280 | bytes 4194304 | tf_op jit(solution)/shard_map/grads/pallas_call | solution.py:214
  94.4 2.9 %collective-permute-start.12 = (bf16[8,64,128]{2,1,0:T(8,128)(2,1)S(1)}, bf16[8,64,128]{2,1,0:T(8,128)(2,1)S(1)}, u32[]{:S(2)}, u32[]{:S(2)}) collective-permute-start(bf16[8,64,128]{2,1,0:T(8,128)(2,1)S(1)} %get-tuple-element.47), channel_id=1, source_target_pairs={{0,4},{1,29},{4,8},{5,1},{8,12},{9,5},{12,16},{13,9},{16,20},{17,1... | collective-permute-start | bytes 393224 | tf_op jit(solution)/shard_map/ppermute | solution.py:269
  97.3 4.0 %grads.15 = (f32[8,64,128]{2,1,0:T(8,128)S(1)}, bf16[32,144,128]{2,1,0:T(8,128)(2,1)S(1)}) custom-call(s32[9]{0:T(128)S(1)} %get-tuple-element.56.tab, bf16[33,32,128]{2,1,0:T(8,128)(2,1)S(1)} %collective-permute-done.3.refs_0_.refs_8_, bf16[33,32,128]{2,1,0:T(8,128)(2,1)S(1)} %collective-permute-done.2.refs_1_.refs_9_, ...), custom_call_target="tpu_custom_call" | custom-call | flops 1342177280 | bytes 4194304 | tf_op jit(solution)/shard_map/grads/pallas_call | solution.py:214
  101.3 0.0 collective-permute-done.13
  101.3 0.0 collective-permute-done.12
  101.4 0.1 multiply_convert_fusion
  101.5 29.8 %all_to_all.16.x_ref = bf16[32,144,128]{2,1,0:T(8,128)(2,1)S(1)} all-to-all(bf16[32,144,128]{2,1,0:T(8,128)(2,1)S(1)} %constant_dynamic-update-slice_fusion), channel_id=1, replica_groups=mesh['y'=4,'xh'=2,'z'=8,'xl'=2,'c'=2] {'xl','c','y','xh'}, dimensions={0} | all-to-all | bytes 2359296 | tf_op jit(solution)/shard_map/all_to_all | solution.py:273
  131.2 1.5 %unpack.1 = (f32[16,4096]{1,0:T(8,128)}, f32[64,4096]{1,0:T(8,128)}, f32[64,4096]{1,0:T(8,128)}) custom-call(bf16[32,144,128]{2,1,0:T(8,128)(2,1)S(1)} %all_to_all.16.x_ref), custom_call_target="tpu_custom_call" | custom-call | flops 1000000 | bytes 3000000 | tf_op jit(solution)/shard_map/unpack/pallas_call | solution.py:251
  (4 shorter events, 0.1 us)
Async XLA Ops:
  21.1 11.8 %collective-permute-start = (bf16[33,32,128]{2,1,0:T(8,128)(2,1)S(1)}, bf16[33,32,128]{2,1,0:T(8,128)(2,1)S(1)}, u32[]{:S(2)}, u32[]{:S(2)}) collective-permute-start(bf16[33,32,128]{2,1,0:T(8,128)(2,1)S(1)} %gather_stats.1.refs_4_.refs_12_), channel_id=1, source_target_pairs={{0,4},{1,29},{4,8},{5,1},{8,12},{9,5},{12,16},{13,9},{16,20},{17,1... | collective-permute-start | bytes 811016 | tf_op jit(solution)/shard_map/ppermute | solution.py:269
  29.1 23.0 %all-to-all-start.1 = ((bf16[32,128,128]{2,1,0:T(8,128)(2,1)}), bf16[32,128,128]{2,1,0:T(8,128)(2,1)S(1)}, u32[]{:S(2)}, u32[]{:S(2)}) async-start(bf16[32,128,128]{2,1,0:T(8,128)(2,1)} %pack_keys.1), calls=%async_computation.1 | async-start | bytes 2097152 | tf_op jit(solution)/shard_map/all_to_all | solution.py:273
  32.8 8.6 %collective-permute-start.4 = (bf16[33,32,128]{2,1,0:T(8,128)(2,1)S(1)}, bf16[33,32,128]{2,1,0:T(8,128)(2,1)S(1)}, u32[]{:S(2)}, u32[]{:S(2)}) collective-permute-start(bf16[33,32,128]{2,1,0:T(8,128)(2,1)S(1)} %gather_stats.1.refs_4_.refs_12_), channel_id=1, source_target_pairs={{0,28},{1,5},{4,0},{5,9},{8,4},{9,13},{12,8},{13,17},{16,12},{17,2... | collective-permute-start | bytes 811016 | tf_op jit(solution)/shard_map/ppermute | solution.py:269
  32.9 8.6 %collective-permute-start.1 = (bf16[33,32,128]{2,1,0:T(8,128)(2,1)S(1)}, bf16[33,32,128]{2,1,0:T(8,128)(2,1)S(1)}, u32[]{:S(2)}, u32[]{:S(2)}) collective-permute-start(bf16[33,32,128]{2,1,0:T(8,128)(2,1)S(1)} %collective-permute-done.refs_3_.refs_11_), channel_id=1, source_target_pairs={{0,4},{1,29},{4,8},{5,1},{8,12},{9,5},{12,16},{13,9},{16,20},{17,1... | collective-permute-start | bytes 811016 | tf_op jit(solution)/shard_map/ppermute | solution.py:269
  41.5 7.7 %collective-permute-start.5 = (bf16[33,32,128]{2,1,0:T(8,128)(2,1)S(1)}, bf16[33,32,128]{2,1,0:T(8,128)(2,1)S(1)}, u32[]{:S(2)}, u32[]{:S(2)}) collective-permute-start(bf16[33,32,128]{2,1,0:T(8,128)(2,1)S(1)} %collective-permute-done.4.refs_5_.refs_13_), channel_id=1, source_target_pairs={{0,28},{1,5},{4,0},{5,9},{8,4},{9,13},{12,8},{13,17},{16,12},{17,2... | collective-permute-start | bytes 811016 | tf_op jit(solution)/shard_map/ppermute | solution.py:269
  41.5 7.7 %collective-permute-start.2 = (bf16[33,32,128]{2,1,0:T(8,128)(2,1)S(1)}, bf16[33,32,128]{2,1,0:T(8,128)(2,1)S(1)}, u32[]{:S(2)}, u32[]{:S(2)}) collective-permute-start(bf16[33,32,128]{2,1,0:T(8,128)(2,1)S(1)} %collective-permute-done.1.refs_2_.refs_10_), channel_id=1, source_target_pairs={{0,4},{1,29},{4,8},{5,1},{8,12},{9,5},{12,16},{13,9},{16,20},{17,1... | collective-permute-start | bytes 811016 | tf_op jit(solution)/shard_map/ppermute | solution.py:269
  49.2 6.9 %collective-permute-start.6 = (bf16[33,32,128]{2,1,0:T(8,128)(2,1)S(1)}, bf16[33,32,128]{2,1,0:T(8,128)(2,1)S(1)}, u32[]{:S(2)}, u32[]{:S(2)}) collective-permute-start(bf16[33,32,128]{2,1,0:T(8,128)(2,1)S(1)} %collective-permute-done.5.refs_6_.refs_14_), channel_id=1, source_target_pairs={{0,28},{1,5},{4,0},{5,9},{8,4},{9,13},{12,8},{13,17},{16,12},{17,2... | collective-permute-start | bytes 811016 | tf_op jit(solution)/shard_map/ppermute | solution.py:269
  49.2 8.6 %collective-permute-start.3 = (bf16[33,32,128]{2,1,0:T(8,128)(2,1)S(1)}, bf16[33,32,128]{2,1,0:T(8,128)(2,1)S(1)}, u32[]{:S(2)}, u32[]{:S(2)}) collective-permute-start(bf16[33,32,128]{2,1,0:T(8,128)(2,1)S(1)} %collective-permute-done.2.refs_1_.refs_9_), channel_id=1, source_target_pairs={{0,4},{1,29},{4,8},{5,1},{8,12},{9,5},{12,16},{13,9},{16,20},{17,1... | collective-permute-start | bytes 811016 | tf_op jit(solution)/shard_map/ppermute | solution.py:269
  61.7 7.4 %collective-permute-start.7 = (bf16[8,64,128]{2,1,0:T(8,128)(2,1)S(1)}, bf16[8,64,128]{2,1,0:T(8,128)(2,1)S(1)}, u32[]{:S(2)}, u32[]{:S(2)}) collective-permute-start(bf16[8,64,128]{2,1,0:T(8,128)(2,1)S(1)} %get-tuple-element.30), channel_id=1, source_target_pairs={{0,4},{1,29},{4,8},{5,1},{8,12},{9,5},{12,16},{13,9},{16,20},{17,1... | collective-permute-start | bytes 393224 | tf_op jit(solution)/shard_map/ppermute | solution.py:269
  68.8 6.9 %collective-permute-start.8 = (bf16[8,64,128]{2,1,0:T(8,128)(2,1)S(1)}, bf16[8,64,128]{2,1,0:T(8,128)(2,1)S(1)}, u32[]{:S(2)}, u32[]{:S(2)}) collective-permute-start(bf16[8,64,128]{2,1,0:T(8,128)(2,1)S(1)} %get-tuple-element.33), channel_id=1, source_target_pairs={{0,28},{1,5},{4,0},{5,9},{8,4},{9,13},{12,8},{13,17},{16,12},{17,2... | collective-permute-start | bytes 393224 | tf_op jit(solution)/shard_map/ppermute | solution.py:269
  73.0 6.7 %collective-permute-start.9 = (bf16[8,64,128]{2,1,0:T(8,128)(2,1)S(1)}, bf16[8,64,128]{2,1,0:T(8,128)(2,1)S(1)}, u32[]{:S(2)}, u32[]{:S(2)}) collective-permute-start(bf16[8,64,128]{2,1,0:T(8,128)(2,1)S(1)} %get-tuple-element.36), channel_id=1, source_target_pairs={{0,4},{1,29},{4,8},{5,1},{8,12},{9,5},{12,16},{13,9},{16,20},{17,1... | collective-permute-start | bytes 393224 | tf_op jit(solution)/shard_map/ppermute | solution.py:269
  79.7 6.7 %collective-permute-start.10 = (bf16[8,64,128]{2,1,0:T(8,128)(2,1)S(1)}, bf16[8,64,128]{2,1,0:T(8,128)(2,1)S(1)}, u32[]{:S(2)}, u32[]{:S(2)}) collective-permute-start(bf16[8,64,128]{2,1,0:T(8,128)(2,1)S(1)} %get-tuple-element.39), channel_id=1, source_target_pairs={{0,28},{1,5},{4,0},{5,9},{8,4},{9,13},{12,8},{13,17},{16,12},{17,2... | collective-permute-start | bytes 393224 | tf_op jit(solution)/shard_map/ppermute | solution.py:269
  83.7 6.7 %collective-permute-start.11 = (bf16[8,64,128]{2,1,0:T(8,128)(2,1)S(1)}, bf16[8,64,128]{2,1,0:T(8,128)(2,1)S(1)}, u32[]{:S(2)}, u32[]{:S(2)}) collective-permute-start(bf16[8,64,128]{2,1,0:T(8,128)(2,1)S(1)} %get-tuple-element.42), channel_id=1, source_target_pairs={{0,4},{1,29},{4,8},{5,1},{8,12},{9,5},{12,16},{13,9},{16,20},{17,1... | collective-permute-start | bytes 393224 | tf_op jit(solution)/shard_map/ppermute | solution.py:269
  90.3 11.0 %collective-permute-start.13 = (bf16[8,64,128]{2,1,0:T(8,128)(2,1)S(1)}, bf16[8,64,128]{2,1,0:T(8,128)(2,1)S(1)}, u32[]{:S(2)}, u32[]{:S(2)}) collective-permute-start(bf16[8,64,128]{2,1,0:T(8,128)(2,1)S(1)} %get-tuple-element.48), channel_id=1, source_target_pairs={{0,28},{1,5},{4,0},{5,9},{8,4},{9,13},{12,8},{13,17},{16,12},{17,2... | collective-permute-start | bytes 393224 | tf_op jit(solution)/shard_map/ppermute | solution.py:269
  94.4 7.0 %collective-permute-start.12 = (bf16[8,64,128]{2,1,0:T(8,128)(2,1)S(1)}, bf16[8,64,128]{2,1,0:T(8,128)(2,1)S(1)}, u32[]{:S(2)}, u32[]{:S(2)}) collective-permute-start(bf16[8,64,128]{2,1,0:T(8,128)(2,1)S(1)} %get-tuple-element.47), channel_id=1, source_target_pairs={{0,4},{1,29},{4,8},{5,1},{8,12},{9,5},{12,16},{13,9},{16,20},{17,1... | collective-permute-start | bytes 393224 | tf_op jit(solution)/shard_map/ppermute | solution.py:269

commit v7 on v5

--- a/solution.py
+++ b/solution.py
@@ -1,4 +1,3 @@
-import functools
 import math
 
 import jax
@@ -148,22 +147,18 @@
     return total.reshape(NZ, PART, DH)
 
 
-def grads(count, first, last, tab, *refs):
+def grads(tab, *refs):
     parts = refs[:NZ]
     tiles = refs[NZ : 2 * NZ]
     kv_ref = refs[2 * NZ]
-    rest = refs[2 * NZ + 1 :]
-    if not first:
-        dk_in, dv_in = rest[:2]
-        rest = rest[2:]
-    dq_refs = rest[:count]
-    dk_ref, dv_ref = rest[-2:]
+    dq_refs = refs[2 * NZ + 1 : 3 * NZ + 1]
+    out_ref, dk_ref, dv_ref = refs[3 * NZ + 1 :]
     step = pl.program_id(0)
 
     @pl.when(step == 0)
     def _():
-        dk_ref[...] = jnp.zeros_like(dk_ref) if first else dk_in[...]
-        dv_ref[...] = jnp.zeros_like(dv_ref) if first else dv_in[...]
+        dk_ref[...] = jnp.zeros_like(dk_ref)
+        dv_ref[...] = jnp.zeros_like(dv_ref)
 
     total = block_grads(tab[step], parts, tiles, kv_ref, dk_ref, dv_ref)
     for n, dq_ref in enumerate(dq_refs):
@@ -171,86 +166,91 @@
         @pl.when(step == n)
         def _(dq_ref=dq_ref):
             for j in range(NZ):
-                dq_ref[tab[count + j]] = total[j].astype(dq_ref.dtype)
-
-    if last:
-        out_ref = rest[count]
-
-        @pl.when(step == count - 1)
-        def _():
-            dk = (dk_ref[...] * (ROOT * SCALE)).astype(BF16)
-            dv = (dv_ref[...] * SCALE).astype(BF16)
-            out_ref[:, 0:KROWS, :] = dk.reshape(NSP, KROWS, DH)
-            out_ref[:, KROWS : 2 * KROWS, :] = dv.reshape(NSP, KROWS, DH)
-
-
-OUT_ROWS = 2 * KROWS + QROWS
-
-
-def grads_call(count, first, last, tab, parts, kv, sums=()):
-    pairs = count * QB * KLEN
-    whole = pl.BlockSpec((KLEN, DH), lambda i, t: (0, 0))
+                dq_ref[tab[NZ + j]] = total[j].astype(dq_ref.dtype)
+
+    @pl.when(step == NZ - 1)
+    def _():
+        dk = (dk_ref[...] * (ROOT * SCALE)).astype(BF16)
+        dv = (dv_ref[...] * SCALE).astype(BF16)
+        out_ref[:, 0:KROWS, :] = dk.reshape(NSP, KROWS, DH)
+        out_ref[:, KROWS : 2 * KROWS, :] = dv.reshape(NSP, KROWS, DH)
+
+
+ORDER = (4, 3, -3, 2, -2, 1, -1, 0)
+
+
+def grads_call(tab, parts, kv):
+    pairs = QLEN * KLEN
     part = pl.BlockSpec((PART // SHARE, WIDE, DH), lambda i, t: (t[i], 0, 0))
     tile = pl.BlockSpec((1, 8, DH), lambda i, t: (NSP, t[i] // 2, 0))
-    in_specs = [part] * NZ + [tile] * NZ
-    in_specs.append(pl.BlockSpec((NSP, 2 * KROWS, DH), lambda i, t: (0, 0, 0)))
-    out_specs = [pl.BlockSpec((NZ, PART, DH), lambda i, t: (0, 0, 0))] * count
-    out_shape = [jax.ShapeDtypeStruct((NZ, PART, DH), F32 if last else BF16)] * count
-    scratch = []
-    if last:
-        out_specs.append(pl.BlockSpec((NSP, OUT_ROWS, DH), lambda i, t: (0, 0, 0)))
-        out_shape.append(jax.ShapeDtypeStruct((NSP, OUT_ROWS, DH), BF16))
-        scratch = [pltpu.VMEM((KLEN, DH), F32)] * 2
-    else:
-        out_specs += [whole] * 2
-        out_shape += [jax.ShapeDtypeStruct((KLEN, DH), F32)] * 2
-    return pl.pallas_call(
-        functools.partial(grads, count, first, last),
+    keys = pl.BlockSpec((NSP, 2 * KROWS, DH), lambda i, t: (0, 0, 0))
+    dq = pl.BlockSpec((NZ, PART, DH), lambda i, t: (0, 0, 0))
+    return pl.pallas_call(
+        grads,
         grid_spec=pltpu.PrefetchScalarGridSpec(
             num_scalar_prefetch=1,
-            grid=(count,),
-            in_specs=in_specs + [whole] * len(sums),
-            out_specs=out_specs,
-            scratch_shapes=scratch,
+            grid=(NZ,),
+            in_specs=[part] * NZ + [tile] * NZ + [keys],
+            out_specs=[dq] * NZ + [keys],
+            scratch_shapes=[pltpu.VMEM((KLEN, DH), F32)] * 2,
         ),
-        out_shape=out_shape,
+        out_shape=[
+            pltpu.HBM((NZ, PART, DH), BF16) if to else jax.ShapeDtypeStruct((NZ, PART, DH), F32)
+            for to in ORDER
+        ]
+        + [jax.ShapeDtypeStruct((NSP, 2 * KROWS, DH), BF16)],
         compiler_params=pltpu.CompilerParams(vmem_limit_bytes=26 << 20),
-        cost_estimate=cost(pairs * 10 * DH, 4 << 20, pairs),
+        cost_estimate=cost(pairs * 10 * DH, 8 << 20, pairs),
         name="grads",
-    )(tab, *parts, *parts, kv, *sums)
-
-
-def unpack(x_ref, *refs):
-    outs, bufs, sems = refs[:3], refs[3:6], refs[6]
+    )(tab, *parts, *parts, kv)
+
+
+def unpack_keys(x_ref, *refs):
+    outs, bufs, sems = refs[:2], refs[2:4], refs[4]
     copies = []
-    pieces = [(0, 0, QROWS, 2 * KROWS)]
-    for n in (1, 2):
-        for r in range(0, KROWS, KROWS // 2):
-            pieces.append((n, r, KROWS // 2, (n - 1) * KROWS + r))
-    for p, (n, r, rows, at) in enumerate(pieces):
-        for h in range(H):
-            bufs[n][r : r + rows, h * DH : (h + 1) * DH] = x_ref[h, at : at + rows, :].astype(F32)
-        copy = pltpu.make_async_copy(
-            bufs[n].at[r : r + rows], outs[n].at[r : r + rows], sems.at[p]
-        )
-        copy.start()
-        copies.append(copy)
+    some = KROWS // 2
+    for n in range(2):
+        for r in range(0, KROWS, some):
+            at = n * KROWS + r
+            for h in range(H):
+                bufs[n][r : r + some, h * DH : (h + 1) * DH] = x_ref[
+                    h, at : at + some, :
+                ].astype(F32)
+            copy = pltpu.make_async_copy(
+                bufs[n].at[r : r + some], outs[n].at[r : r + some], sems.at[len(copies)]
+            )
+            copy.start()
+            copies.append(copy)
     for copy in copies:
         copy.wait()
 
 
-def unpacked(x):
-    shapes = [(QROWS, H * DH), (KROWS, H * DH), (KROWS, H * DH)]
-    return pl.pallas_call(
-        unpack,
+def unpacked_keys(x):
+    shape = (KROWS, H * DH)
+    return pl.pallas_call(
+        unpack_keys,
         in_specs=[pl.BlockSpec(memory_space=pltpu.VMEM)],
-        out_specs=[pl.BlockSpec(memory_space=pl.ANY)] * 3,
-        out_shape=[jax.ShapeDtypeStruct(shape, F32) for shape in shapes],
-        scratch_shapes=[pltpu.VMEM(shape, F32) for shape in shapes]
-        + [pltpu.SemaphoreType.DMA((5,))],
+        out_specs=[pl.BlockSpec(memory_space=pl.ANY)] * 2,
+        out_shape=[jax.ShapeDtypeStruct(shape, F32)] * 2,
+        scratch_shapes=[pltpu.VMEM(shape, F32)] * 2 + [pltpu.SemaphoreType.DMA((4,))],
         compiler_params=pltpu.CompilerParams(vmem_limit_bytes=8 << 20),
         cost_estimate=cost(10**6, 3 * 10**6),
-        name="unpack",
+        name="unpack_keys",
+    )(x)
+
+
+def unpack_queries(x_ref, dq_ref):
+    for h in range(H):
+        dq_ref[:, h * DH : (h + 1) * DH] = x_ref[h].astype(F32)
+
+
+def unpacked_queries(x):
+    return pl.pallas_call(
+        unpack_queries,
+        out_shape=jax.ShapeDtypeStruct((QROWS, H * DH), F32),
+        compiler_params=pltpu.CompilerParams(vmem_limit_bytes=4 << 20),
+        cost_estimate=cost(10**6, 10**6),
+        name="unpack_queries",
     )(x)
 
 
@@ -285,27 +285,16 @@
     sign = 1 - 2 * lax.axis_index("c")
     where = (z + sign * jnp.arange(-half, half, dtype=jnp.int32)) % NZ
 
-    sent = []
-    sums = ()
-    groups = ((4, 3, -3), (2, -2), (1, -1), (0,))
-    for n, group in enumerate(groups):
-        tab = jnp.concatenate([(z + sign * jnp.array(group, jnp.int32)) % NZ, where])
-        first, last = n == 0, n == len(groups) - 1
-        out = grads_call(
-            len(group), first, last, tab.astype(jnp.int32), parts, kv, sums
-        )
-        sums = out[len(group) :]
-        for by, dq in zip(group, out):
-            if by:
-                sent.append(turn(dq, by))
-            else:
-                mine = dq
-    mine = mine + sum(x.astype(F32) for x in sent)
+    tab = jnp.concatenate([(z + sign * jnp.array(ORDER, jnp.int32)) % NZ, where])
+    *dqs, mine, packed = grads_call(tab.astype(jnp.int32), parts, kv)
+    packed = regroup(packed)
+    for n, dq in enumerate(dqs):
+        mine = mine + turn(dq, ORDER[n]).astype(F32)
     mine = (mine * (ROOT * SCALE)).reshape(NKV, NXC, QROWS, DH)
     mine = jnp.swapaxes(mine, 0, 1).reshape(NSP, QROWS, DH).astype(BF16)
-    packed = lax.dynamic_update_slice(sums[0], mine, (0, 2 * KROWS, 0))
-    packed = regroup(packed)
-    return unpacked(packed)
+    mine = regroup(mine)
+    dk, dv = unpacked_keys(packed)
+    return unpacked_queries(mine), dk, dv
 
 
 def solution(mesh):

time: 133 us -> 153 us (1.15)
  waiting for transfers between devices: 18.8 us -> 43.8 us
  blocking collectives: 48 us -> 34.3 us
  starting transfers between devices: 32.1 us -> 39.9 us
    all_to_all x2, blocking collectives: 48 us -> 34.3 us  [regroup(): return lax.all_to_all(x, PLANE, split_axis=0, concat_axis=0, tiled=True)]
    ppermute x14, waiting for transfers between devices: 14.1 us -> 27.3 us  [turn(): return lax.ppermute(x, ('z', 'c'), pairs)]
    all_to_all x1 -> x2, waiting for transfers between devices: 4.61 us -> 16.5 us  [regroup(): return lax.all_to_all(x, PLANE, split_axis=0, concat_axis=0, tiled=True)]
    ppermute x14, starting transfers between devices: 28.2 us -> 32.2 us  [turn(): return lax.ppermute(x, ('z', 'c'), pairs)]
    all_to_all x1 -> x2, starting transfers between devices: 3.85 us -> 7.65 us  [regroup(): return lax.all_to_all(x, PLANE, split_axis=0, concat_axis=0, tiled=True)]
    pallas_call x5 -> x3, Pallas kernels: 28.2 us -> 28.7 us  [the longest x1 26.6 us: grads_call(): pl.pallas_call(grads, grid_spec=pltpu.PrefetchScalarGridSpec(num_scalar_p...]
  transfers between devices with their start and end apart: 15 -> 16, of which waited for: 6 -> 9; matrix products, arithmetic and copies ran while one was open for 0% -> 0% of each run, Pallas kernels for 15% -> 2%
where the time goes in v7:
time: 153 us; the launch traced here: 152 us
  waiting for transfers between devices  43.8 us (29%)
  starting transfers between devices  39.9 us (26%)
  blocking collectives  34.3 us (22%)
  Pallas kernels  33.2 us (22%)
    all_to_all x2, blocking collectives, regroup(): return lax.all_to_all(x, PLANE, split_axis=0, concat_axis=0, tiled=True)  34.3 us
    ppermute x14, starting transfers between devices, turn(): return lax.ppermute(x, ('z', 'c'), pairs)  32.2 us
    ppermute x14, waiting for transfers between devices, turn(): return lax.ppermute(x, ('z', 'c'), pairs)  27.3 us
    pallas_call x1, Pallas kernels, grads_call(): pl.pallas_call(grads, grid_spec=pltpu.PrefetchScalarGridSpec(num_scalar_p...  26.6 us
    all_to_all x2, waiting for transfers between devices, regroup(): return lax.all_to_all(x, PLANE, split_axis=0, concat_axis=0, tiled=True)  16.5 us
    all_to_all x2, starting transfers between devices, regroup(): return lax.all_to_all(x, PLANE, split_axis=0, concat_axis=0, tiled=True)  7.65 us
  transfers between devices with their start and end apart: 16, of which 9 were waited for; matrix products, arithmetic and copies ran while one was open for 0% of the time, Pallas kernels for 2%

profile of v7, /device:TPU:1, one launch (start us, length us, event | category | flops | bytes accessed | tf_op | source)
XLA Modules:
  0.0 152.4 jit_solution(4055057707951673943)
XLA Ops:
  0.6 2.1 %pack_queries.1 = bf16[32,40,128]{2,1,0:T(8,128)(2,1)} custom-call(s32[1]{0:T(128)} %bitcast.b_ref, bf16[128,4096]{1,0:T(8,128)(2,1)} %q_ref.1, bf16[128,4096]{1,0:T(8,128)(2,1)} %g_ref.1, bf16[128,4096]{1,0:T(8,128)(2,1)} %o_ref.1, f32[32,128]{1,0:T(8,128)} %bitcast.8), custom_call_target="tpu_custom_call" | custom-call | flops 1000000 | bytes 1000000 | tf_op jit(solution)/shard_map/pack_queries/pallas_call | solution.py:74
  2.8 18.3 %all_to_all.20.x_ref = bf16[32,40,128]{2,1,0:T(8,128)(2,1)S(1)} all-to-all(bf16[32,40,128]{2,1,0:T(8,128)(2,1)} %pack_queries.1), channel_id=1, replica_groups=mesh['y'=4,'xh'=2,'z'=8,'xl'=2,'c'=2] {'xl','c','y','xh'}, dimensions={0} | all-to-all | bytes 655360 | tf_op jit(solution)/shard_map/all_to_all | solution.py:266
  21.1 5.7 %collective-permute-start = (bf16[33,32,128]{2,1,0:T(8,128)(2,1)S(1)}, bf16[33,32,128]{2,1,0:T(8,128)(2,1)S(1)}, u32[]{:S(2)}, u32[]{:S(2)}) collective-permute-start(bf16[33,32,128]{2,1,0:T(8,128)(2,1)S(1)} %gather_stats.1.refs_4_.refs_12_), channel_id=1, source_target_pairs={{0,4},{1,29},{4,8},{5,1},{8,12},{9,5},{12,16},{13,9},{16,20},{17,1... | collective-permute-start | bytes 811016 | tf_op jit(solution)/shard_map/ppermute | solution.py:262
  26.8 2.4 %pack_keys.1 = bf16[32,128,128]{2,1,0:T(8,128)(2,1)} custom-call(bf16[64,4096]{1,0:T(8,128)(2,1)} %k_ref.1, bf16[64,4096]{1,0:T(8,128)(2,1)} %v_ref.1), custom_call_target="tpu_custom_call" | custom-call | flops 1000000 | bytes 2000000 | tf_op jit(solution)/shard_map/pack_keys/pallas_call | solution.py:112
  29.1 3.7 %all-to-all-start.1 = ((bf16[32,128,128]{2,1,0:T(8,128)(2,1)}), bf16[32,128,128]{2,1,0:T(8,128)(2,1)S(1)}, u32[]{:S(2)}, u32[]{:S(2)}) async-start(bf16[32,128,128]{2,1,0:T(8,128)(2,1)} %pack_keys.1), calls=%async_computation.1 | async-start | bytes 2097152 | tf_op jit(solution)/shard_map/all_to_all | solution.py:266
  32.8 0.1 collective-permute-start.4
  32.9 0.0 collective-permute-done.refs_3_.refs_11_
  32.9 2.7 %collective-permute-start.1 = (bf16[33,32,128]{2,1,0:T(8,128)(2,1)S(1)}, bf16[33,32,128]{2,1,0:T(8,128)(2,1)S(1)}, u32[]{:S(2)}, u32[]{:S(2)}) collective-permute-start(bf16[33,32,128]{2,1,0:T(8,128)(2,1)S(1)} %collective-permute-done.refs_3_.refs_11_), channel_id=1, source_target_pairs={{0,4},{1,29},{4,8},{5,1},{8,12},{9,5},{12,16},{13,9},{16,20},{17,1... | collective-permute-start | bytes 811016 | tf_op jit(solution)/shard_map/ppermute | solution.py:262
  35.6 5.9 %collective-permute-done.4.refs_5_.refs_13_ = bf16[33,32,128]{2,1,0:T(8,128)(2,1)S(1)} collective-permute-done((bf16[33,32,128]{2,1,0:T(8,128)(2,1)S(1)}, bf16[33,32,128]{2,1,0:T(8,128)(2,1)S(1)}, u32[]{:S(2)}, u32[]{:S(2)}) %collective-permute-start.4) | collective-permute-done | bytes 270368 | tf_op jit(solution)/shard_map/ppermute | solution.py:262
  41.5 0.0 collective-permute-start.5
  41.5 0.0 collective-permute-done.1.refs_2_.refs_10_
  41.5 2.7 %collective-permute-start.2 = (bf16[33,32,128]{2,1,0:T(8,128)(2,1)S(1)}, bf16[33,32,128]{2,1,0:T(8,128)(2,1)S(1)}, u32[]{:S(2)}, u32[]{:S(2)}) collective-permute-start(bf16[33,32,128]{2,1,0:T(8,128)(2,1)S(1)} %collective-permute-done.1.refs_2_.refs_10_), channel_id=1, source_target_pairs={{0,4},{1,29},{4,8},{5,1},{8,12},{9,5},{12,16},{13,9},{16,20},{17,1... | collective-permute-start | bytes 811016 | tf_op jit(solution)/shard_map/ppermute | solution.py:262
  44.2 0.0 copy-start
  44.2 5.0 %collective-permute-done.5.refs_6_.refs_14_ = bf16[33,32,128]{2,1,0:T(8,128)(2,1)S(1)} collective-permute-done((bf16[33,32,128]{2,1,0:T(8,128)(2,1)S(1)}, bf16[33,32,128]{2,1,0:T(8,128)(2,1)S(1)}, u32[]{:S(2)}, u32[]{:S(2)}) %collective-permute-start.5) | collective-permute-done | bytes 270368 | tf_op jit(solution)/shard_map/ppermute | solution.py:262
  49.2 0.0 collective-permute-start.6
  49.2 0.0 collective-permute-done.2.refs_1_.refs_9_
  49.2 2.8 %collective-permute-start.3 = (bf16[33,32,128]{2,1,0:T(8,128)(2,1)S(1)}, bf16[33,32,128]{2,1,0:T(8,128)(2,1)S(1)}, u32[]{:S(2)}, u32[]{:S(2)}) collective-permute-start(bf16[33,32,128]{2,1,0:T(8,128)(2,1)S(1)} %collective-permute-done.2.refs_1_.refs_9_), channel_id=1, source_target_pairs={{0,4},{1,29},{4,8},{5,1},{8,12},{9,5},{12,16},{13,9},{16,20},{17,1... | collective-permute-start | bytes 811016 | tf_op jit(solution)/shard_map/ppermute | solution.py:262
  52.0 0.0 copy-done
  52.0 0.1 pad_add_fusion.tab
  52.1 0.0 all-to-all-done.1.refs_16_
  52.1 4.0 %collective-permute-done.6.refs_7_.refs_15_ = bf16[33,32,128]{2,1,0:T(8,128)(2,1)S(1)} collective-permute-done((bf16[33,32,128]{2,1,0:T(8,128)(2,1)S(1)}, bf16[33,32,128]{2,1,0:T(8,128)(2,1)S(1)}, u32[]{:S(2)}, u32[]{:S(2)}) %collective-permute-start.6) | collective-permute-done | bytes 270368 | tf_op jit(solution)/shard_map/ppermute | solution.py:262
  56.1 1.8 %collective-permute-done.3.refs_0_.refs_8_ = bf16[33,32,128]{2,1,0:T(8,128)(2,1)S(1)} collective-permute-done((bf16[33,32,128]{2,1,0:T(8,128)(2,1)S(1)}, bf16[33,32,128]{2,1,0:T(8,128)(2,1)S(1)}, u32[]{:S(2)}, u32[]{:S(2)}) %collective-permute-start.3) | collective-permute-done | bytes 270368 | tf_op jit(solution)/shard_map/ppermute | solution.py:262
  57.8 26.6 %grads.1 = (bf16[8,64,128]{2,1,0:T(8,128)(2,1)}, bf16[8,64,128]{2,1,0:T(8,128)(2,1)}, bf16[8,64,128]{2,1,0:T(8,128)(2,1)}, bf16[8,64,128]{2,1,0:T(8,128)(2,1)}, ...) custom-call(s32[16]{0:T(128)S(1)} %pad_add_fusion.tab, ...), custom_call_target="tpu_custom_call" | custom-call | flops 10737418240 | bytes 8388608 | tf_op jit(solution)/shard_map/grads/pallas_call | solution.py:188
  84.4 3.5 %collective-permute-start.7 = (bf16[8,64,128]{2,1,0:T(8,128)(2,1)}, bf16[8,64,128]{2,1,0:T(8,128)(2,1)S(1)}, u32[]{:S(2)}, u32[]{:S(2)}) collective-permute-start(bf16[8,64,128]{2,1,0:T(8,128)(2,1)} %get-tuple-element.15), channel_id=1, source_target_pairs={{0,16},{1,17},{4,20},{5,21},{8,24},{9,25},{12,28},{13,29},{16,0},{... | collective-permute-start | bytes 393224 | tf_op jit(solution)/shard_map/ppermute | solution.py:262
  87.9 1.3 collective-permute-start.8
  89.2 2.0 %collective-permute-start.9 = (bf16[8,64,128]{2,1,0:T(8,128)(2,1)}, bf16[8,64,128]{2,1,0:T(8,128)(2,1)S(1)}, u32[]{:S(2)}, u32[]{:S(2)}) collective-permute-start(bf16[8,64,128]{2,1,0:T(8,128)(2,1)} %get-tuple-element.17), channel_id=1, source_target_pairs={{0,20},{1,13},{4,24},{5,17},{8,28},{9,21},{12,0},{13,25},{16,4},{1... | collective-permute-start | bytes 393224 | tf_op jit(solution)/shard_map/ppermute | solution.py:262
  91.2 3.4 %collective-permute-start.10 = (bf16[8,64,128]{2,1,0:T(8,128)(2,1)}, bf16[8,64,128]{2,1,0:T(8,128)(2,1)S(1)}, u32[]{:S(2)}, u32[]{:S(2)}) collective-permute-start(bf16[8,64,128]{2,1,0:T(8,128)(2,1)} %get-tuple-element.18), channel_id=1, source_target_pairs={{0,8},{1,25},{4,12},{5,29},{8,16},{9,1},{12,20},{13,5},{16,24},{17... | collective-permute-start | bytes 393224 | tf_op jit(solution)/shard_map/ppermute | solution.py:262
  94.6 0.0 collective-permute-start.11
  94.6 0.0 collective-permute-done.7
  94.6 8.2 %collective-permute-start.12 = (bf16[8,64,128]{2,1,0:T(8,128)(2,1)}, bf16[8,64,128]{2,1,0:T(8,128)(2,1)S(1)}, u32[]{:S(2)}, u32[]{:S(2)}) collective-permute-start(bf16[8,64,128]{2,1,0:T(8,128)(2,1)} %get-tuple-element.20), channel_id=1, source_target_pairs={{0,4},{1,29},{4,8},{5,1},{8,12},{9,5},{12,16},{13,9},{16,20},{17,1... | collective-permute-start | bytes 393224 | tf_op jit(solution)/shard_map/ppermute | solution.py:262
  102.8 3.4 %collective-permute-done.8 = bf16[8,64,128]{2,1,0:T(8,128)(2,1)S(1)} collective-permute-done((bf16[8,64,128]{2,1,0:T(8,128)(2,1)}, bf16[8,64,128]{2,1,0:T(8,128)(2,1)S(1)}, u32[]{:S(2)}, u32[]{:S(2)}) %collective-permute-start.8) | collective-permute-done | bytes 131104 | tf_op jit(solution)/shard_map/ppermute | solution.py:262
  106.2 0.0 collective-permute-start.13
  106.2 0.0 collective-permute-done.9
  106.2 5.5 %collective-permute-done.10 = bf16[8,64,128]{2,1,0:T(8,128)(2,1)S(1)} collective-permute-done((bf16[8,64,128]{2,1,0:T(8,128)(2,1)}, bf16[8,64,128]{2,1,0:T(8,128)(2,1)S(1)}, u32[]{:S(2)}, u32[]{:S(2)}) %collective-permute-start.10) | collective-permute-done | bytes 131104 | tf_op jit(solution)/shard_map/ppermute | solution.py:262
  111.7 0.0 collective-permute-done.11
  111.7 1.7 %collective-permute-done.12 = bf16[8,64,128]{2,1,0:T(8,128)(2,1)S(1)} collective-permute-done((bf16[8,64,128]{2,1,0:T(8,128)(2,1)}, bf16[8,64,128]{2,1,0:T(8,128)(2,1)S(1)}, u32[]{:S(2)}, u32[]{:S(2)}) %collective-permute-start.12) | collective-permute-done | bytes 131104 | tf_op jit(solution)/shard_map/ppermute | solution.py:262
  113.4 0.1 collective-permute-done.13
  113.5 0.2 multiply_convert_fusion
  113.7 16.1 %all_to_all.21.x_ref = bf16[32,16,128]{2,1,0:T(8,128)(2,1)S(1)} all-to-all(bf16[32,16,128]{2,1,0:T(8,128)(2,1)S(1)} %bitcast.7), channel_id=1, replica_groups=mesh['y'=4,'xh'=2,'z'=8,'xl'=2,'c'=2] {'xl','c','y','xh'}, dimensions={0} | all-to-all | bytes 262144 | tf_op jit(solution)/shard_map/all_to_all | solution.py:266
  129.7 3.9 %all-to-all-start.3 = ((bf16[32,128,128]{2,1,0:T(8,128)(2,1)}), bf16[32,128,128]{2,1,0:T(8,128)(2,1)S(1)}, u32[]{:S(2)}, u32[]{:S(2)}) async-start(bf16[32,128,128]{2,1,0:T(8,128)(2,1)} %get-tuple-element.22), calls=%async_computation.3 | async-start | bytes 2097152 | tf_op jit(solution)/shard_map/all_to_all | solution.py:266
  133.6 0.7 unpack_queries.1
  134.4 16.5 %all-to-all-done.3.x_ref = bf16[32,128,128]{2,1,0:T(8,128)(2,1)S(1)} async-done(((bf16[32,128,128]{2,1,0:T(8,128)(2,1)}), bf16[32,128,128]{2,1,0:T(8,128)(2,1)S(1)}, u32[]{:S(2)}, u32[]{:S(2)}) %all-to-all-start.3) | async-done | bytes 1048608 | tf_op jit(solution)/shard_map/all_to_all | solution.py:266
  150.8 1.4 unpack_keys.1
  (3 shorter events, 0.1 us)
Async XLA Ops:
  21.1 11.8 %collective-permute-start = (bf16[33,32,128]{2,1,0:T(8,128)(2,1)S(1)}, bf16[33,32,128]{2,1,0:T(8,128)(2,1)S(1)}, u32[]{:S(2)}, u32[]{:S(2)}) collective-permute-start(bf16[33,32,128]{2,1,0:T(8,128)(2,1)S(1)} %gather_stats.1.refs_4_.refs_12_), channel_id=1, source_target_pairs={{0,4},{1,29},{4,8},{5,1},{8,12},{9,5},{12,16},{13,9},{16,20},{17,1... | collective-permute-start | bytes 811016 | tf_op jit(solution)/shard_map/ppermute | solution.py:262
  29.1 23.0 %all-to-all-start.1 = ((bf16[32,128,128]{2,1,0:T(8,128)(2,1)}), bf16[32,128,128]{2,1,0:T(8,128)(2,1)S(1)}, u32[]{:S(2)}, u32[]{:S(2)}) async-start(bf16[32,128,128]{2,1,0:T(8,128)(2,1)} %pack_keys.1), calls=%async_computation.1 | async-start | bytes 2097152 | tf_op jit(solution)/shard_map/all_to_all | solution.py:266
  32.8 8.6 %collective-permute-start.4 = (bf16[33,32,128]{2,1,0:T(8,128)(2,1)S(1)}, bf16[33,32,128]{2,1,0:T(8,128)(2,1)S(1)}, u32[]{:S(2)}, u32[]{:S(2)}) collective-permute-start(bf16[33,32,128]{2,1,0:T(8,128)(2,1)S(1)} %gather_stats.1.refs_4_.refs_12_), channel_id=1, source_target_pairs={{0,28},{1,5},{4,0},{5,9},{8,4},{9,13},{12,8},{13,17},{16,12},{17,2... | collective-permute-start | bytes 811016 | tf_op jit(solution)/shard_map/ppermute | solution.py:262
  32.9 8.6 %collective-permute-start.1 = (bf16[33,32,128]{2,1,0:T(8,128)(2,1)S(1)}, bf16[33,32,128]{2,1,0:T(8,128)(2,1)S(1)}, u32[]{:S(2)}, u32[]{:S(2)}) collective-permute-start(bf16[33,32,128]{2,1,0:T(8,128)(2,1)S(1)} %collective-permute-done.refs_3_.refs_11_), channel_id=1, source_target_pairs={{0,4},{1,29},{4,8},{5,1},{8,12},{9,5},{12,16},{13,9},{16,20},{17,1... | collective-permute-start | bytes 811016 | tf_op jit(solution)/shard_map/ppermute | solution.py:262
  41.5 7.7 %collective-permute-start.5 = (bf16[33,32,128]{2,1,0:T(8,128)(2,1)S(1)}, bf16[33,32,128]{2,1,0:T(8,128)(2,1)S(1)}, u32[]{:S(2)}, u32[]{:S(2)}) collective-permute-start(bf16[33,32,128]{2,1,0:T(8,128)(2,1)S(1)} %collective-permute-done.4.refs_5_.refs_13_), channel_id=1, source_target_pairs={{0,28},{1,5},{4,0},{5,9},{8,4},{9,13},{12,8},{13,17},{16,12},{17,2... | collective-permute-start | bytes 811016 | tf_op jit(solution)/shard_map/ppermute | solution.py:262
  41.5 7.7 %collective-permute-start.2 = (bf16[33,32,128]{2,1,0:T(8,128)(2,1)S(1)}, bf16[33,32,128]{2,1,0:T(8,128)(2,1)S(1)}, u32[]{:S(2)}, u32[]{:S(2)}) collective-permute-start(bf16[33,32,128]{2,1,0:T(8,128)(2,1)S(1)} %collective-permute-done.1.refs_2_.refs_10_), channel_id=1, source_target_pairs={{0,4},{1,29},{4,8},{5,1},{8,12},{9,5},{12,16},{13,9},{16,20},{17,1... | collective-permute-start | bytes 811016 | tf_op jit(solution)/shard_map/ppermute | solution.py:262
  44.2 7.8 %copy-start = (s32[8]{0:T(128)S(1)}, s32[8]{0:T(128)}, u32[]{:S(2)}) copy-start(s32[8]{0:T(128)} %constant.49.clone) | copy-start | bytes 100
  49.2 6.9 %collective-permute-start.6 = (bf16[33,32,128]{2,1,0:T(8,128)(2,1)S(1)}, bf16[33,32,128]{2,1,0:T(8,128)(2,1)S(1)}, u32[]{:S(2)}, u32[]{:S(2)}) collective-permute-start(bf16[33,32,128]{2,1,0:T(8,128)(2,1)S(1)} %collective-permute-done.5.refs_6_.refs_14_), channel_id=1, source_target_pairs={{0,28},{1,5},{4,0},{5,9},{8,4},{9,13},{12,8},{13,17},{16,12},{17,2... | collective-permute-start | bytes 811016 | tf_op jit(solution)/shard_map/ppermute | solution.py:262
  49.2 8.6 %collective-permute-start.3 = (bf16[33,32,128]{2,1,0:T(8,128)(2,1)S(1)}, bf16[33,32,128]{2,1,0:T(8,128)(2,1)S(1)}, u32[]{:S(2)}, u32[]{:S(2)}) collective-permute-start(bf16[33,32,128]{2,1,0:T(8,128)(2,1)S(1)} %collective-permute-done.2.refs_1_.refs_9_), channel_id=1, source_target_pairs={{0,4},{1,29},{4,8},{5,1},{8,12},{9,5},{12,16},{13,9},{16,20},{17,1... | collective-permute-start | bytes 811016 | tf_op jit(solution)/shard_map/ppermute | solution.py:262
  84.4 10.2 %collective-permute-start.7 = (bf16[8,64,128]{2,1,0:T(8,128)(2,1)}, bf16[8,64,128]{2,1,0:T(8,128)(2,1)S(1)}, u32[]{:S(2)}, u32[]{:S(2)}) collective-permute-start(bf16[8,64,128]{2,1,0:T(8,128)(2,1)} %get-tuple-element.15), channel_id=1, source_target_pairs={{0,16},{1,17},{4,20},{5,21},{8,24},{9,25},{12,28},{13,29},{16,0},{... | collective-permute-start | bytes 393224 | tf_op jit(solution)/shard_map/ppermute | solution.py:262
  87.9 18.3 %collective-permute-start.8 = (bf16[8,64,128]{2,1,0:T(8,128)(2,1)}, bf16[8,64,128]{2,1,0:T(8,128)(2,1)S(1)}, u32[]{:S(2)}, u32[]{:S(2)}) collective-permute-start(bf16[8,64,128]{2,1,0:T(8,128)(2,1)} %get-tuple-element.16), channel_id=1, source_target_pairs={{0,12},{1,21},{4,16},{5,25},{8,20},{9,29},{12,24},{13,1},{16,28},{... | collective-permute-start | bytes 393224 | tf_op jit(solution)/shard_map/ppermute | solution.py:262
  89.2 17.0 %collective-permute-start.9 = (bf16[8,64,128]{2,1,0:T(8,128)(2,1)}, bf16[8,64,128]{2,1,0:T(8,128)(2,1)S(1)}, u32[]{:S(2)}, u32[]{:S(2)}) collective-permute-start(bf16[8,64,128]{2,1,0:T(8,128)(2,1)} %get-tuple-element.17), channel_id=1, source_target_pairs={{0,20},{1,13},{4,24},{5,17},{8,28},{9,21},{12,0},{13,25},{16,4},{1... | collective-permute-start | bytes 393224 | tf_op jit(solution)/shard_map/ppermute | solution.py:262
  91.2 20.5 %collective-permute-start.10 = (bf16[8,64,128]{2,1,0:T(8,128)(2,1)}, bf16[8,64,128]{2,1,0:T(8,128)(2,1)S(1)}, u32[]{:S(2)}, u32[]{:S(2)}) collective-permute-start(bf16[8,64,128]{2,1,0:T(8,128)(2,1)} %get-tuple-element.18), channel_id=1, source_target_pairs={{0,8},{1,25},{4,12},{5,29},{8,16},{9,1},{12,20},{13,5},{16,24},{17... | collective-permute-start | bytes 393224 | tf_op jit(solution)/shard_map/ppermute | solution.py:262
  94.6 17.1 %collective-permute-start.11 = (bf16[8,64,128]{2,1,0:T(8,128)(2,1)}, bf16[8,64,128]{2,1,0:T(8,128)(2,1)S(1)}, u32[]{:S(2)}, u32[]{:S(2)}) collective-permute-start(bf16[8,64,128]{2,1,0:T(8,128)(2,1)} %get-tuple-element.19), channel_id=1, source_target_pairs={{0,24},{1,9},{4,28},{5,13},{8,0},{9,17},{12,4},{13,21},{16,8},{17,... | collective-permute-start | bytes 393224 | tf_op jit(solution)/shard_map/ppermute | solution.py:262
  94.6 18.8 %collective-permute-start.12 = (bf16[8,64,128]{2,1,0:T(8,128)(2,1)}, bf16[8,64,128]{2,1,0:T(8,128)(2,1)S(1)}, u32[]{:S(2)}, u32[]{:S(2)}) collective-permute-start(bf16[8,64,128]{2,1,0:T(8,128)(2,1)} %get-tuple-element.20), channel_id=1, source_target_pairs={{0,4},{1,29},{4,8},{5,1},{8,12},{9,5},{12,16},{13,9},{16,20},{17,1... | collective-permute-start | bytes 393224 | tf_op jit(solution)/shard_map/ppermute | solution.py:262
  106.2 7.3 %collective-permute-start.13 = (bf16[8,64,128]{2,1,0:T(8,128)(2,1)}, bf16[8,64,128]{2,1,0:T(8,128)(2,1)S(1)}, u32[]{:S(2)}, u32[]{:S(2)}) collective-permute-start(bf16[8,64,128]{2,1,0:T(8,128)(2,1)} %get-tuple-element.21), channel_id=1, source_target_pairs={{0,28},{1,5},{4,0},{5,9},{8,4},{9,13},{12,8},{13,17},{16,12},{17,2... | collective-permute-start | bytes 393224 | tf_op jit(solution)/shard_map/ppermute | solution.py:262
  129.7 21.1 %all-to-all-start.3 = ((bf16[32,128,128]{2,1,0:T(8,128)(2,1)}), bf16[32,128,128]{2,1,0:T(8,128)(2,1)S(1)}, u32[]{:S(2)}, u32[]{:S(2)}) async-start(bf16[32,128,128]{2,1,0:T(8,128)(2,1)} %get-tuple-element.22), calls=%async_computation.3 | async-start | bytes 2097152 | tf_op jit(solution)/shard_map/all_to_all | solution.py:266

commit v8 on v5

--- a/solution.py
+++ b/solution.py
@@ -148,7 +148,7 @@
     return total.reshape(NZ, PART, DH)
 
 
-def grads(count, first, last, tab, *refs):
+def grads(count, first, last, added, tab, *refs):
     parts = refs[:NZ]
     tiles = refs[NZ : 2 * NZ]
     kv_ref = refs[2 * NZ]
@@ -156,6 +156,8 @@
     if not first:
         dk_in, dv_in = rest[:2]
         rest = rest[2:]
+    arrived = rest[:count] if added else ()
+    rest = rest[len(arrived) :]
     dq_refs = rest[:count]
     dk_ref, dv_ref = rest[-2:]
     step = pl.program_id(0)
@@ -169,9 +171,13 @@
     for n, dq_ref in enumerate(dq_refs):
 
         @pl.when(step == n)
-        def _(dq_ref=dq_ref):
+        def _(n=n, dq_ref=dq_ref):
             for j in range(NZ):
-                dq_ref[tab[count + j]] = total[j].astype(dq_ref.dtype)
+                at = tab[count + j]
+                part = total[j]
+                if added:
+                    part = part + arrived[n][at].astype(F32)
+                dq_ref[at] = part.astype(dq_ref.dtype)
 
     if last:
         out_ref = rest[count]
@@ -187,14 +193,15 @@
 OUT_ROWS = 2 * KROWS + QROWS
 
 
-def grads_call(count, first, last, tab, parts, kv, sums=()):
+def grads_call(count, first, last, tab, parts, kv, sums=(), arrived=()):
     pairs = count * QB * KLEN
     whole = pl.BlockSpec((KLEN, DH), lambda i, t: (0, 0))
     part = pl.BlockSpec((PART // SHARE, WIDE, DH), lambda i, t: (t[i], 0, 0))
     tile = pl.BlockSpec((1, 8, DH), lambda i, t: (NSP, t[i] // 2, 0))
     in_specs = [part] * NZ + [tile] * NZ
     in_specs.append(pl.BlockSpec((NSP, 2 * KROWS, DH), lambda i, t: (0, 0, 0)))
-    out_specs = [pl.BlockSpec((NZ, PART, DH), lambda i, t: (0, 0, 0))] * count
+    dq = pl.BlockSpec((NZ, PART, DH), lambda i, t: (0, 0, 0))
+    out_specs = [dq] * count
     out_shape = [jax.ShapeDtypeStruct((NZ, PART, DH), F32 if last else BF16)] * count
     scratch = []
     if last:
@@ -205,11 +212,11 @@
         out_specs += [whole] * 2
         out_shape += [jax.ShapeDtypeStruct((KLEN, DH), F32)] * 2
     return pl.pallas_call(
-        functools.partial(grads, count, first, last),
+        functools.partial(grads, count, first, last, bool(arrived)),
         grid_spec=pltpu.PrefetchScalarGridSpec(
             num_scalar_prefetch=1,
             grid=(count,),
-            in_specs=in_specs + [whole] * len(sums),
+            in_specs=in_specs + [whole] * len(sums) + [dq] * len(arrived),
             out_specs=out_specs,
             scratch_shapes=scratch,
         ),
@@ -217,7 +224,7 @@
         compiler_params=pltpu.CompilerParams(vmem_limit_bytes=26 << 20),
         cost_estimate=cost(pairs * 10 * DH, 4 << 20, pairs),
         name="grads",
-    )(tab, *parts, *parts, kv, *sums)
+    )(tab, *parts, *parts, kv, *sums, *arrived)
 
 
 def unpack(x_ref, *refs):
@@ -285,21 +292,20 @@
     sign = 1 - 2 * lax.axis_index("c")
     where = (z + sign * jnp.arange(-half, half, dtype=jnp.int32)) % NZ
 
-    sent = []
-    sums = ()
-    groups = ((4, 3, -3), (2, -2), (1, -1), (0,))
-    for n, group in enumerate(groups):
+    def call(group, sums, arrived=()):
         tab = jnp.concatenate([(z + sign * jnp.array(group, jnp.int32)) % NZ, where])
-        first, last = n == 0, n == len(groups) - 1
         out = grads_call(
-            len(group), first, last, tab.astype(jnp.int32), parts, kv, sums
+            len(group), not sums, 0 in group, tab.astype(jnp.int32), parts, kv, sums, arrived
         )
-        sums = out[len(group) :]
-        for by, dq in zip(group, out):
-            if by:
-                sent.append(turn(dq, by))
-            else:
-                mine = dq
+        return out[: len(group)], out[len(group) :]
+
+    (four, back3), sums = call((4, -3), ())
+    arrived = (turn(four, 1), turn(back3, -1))
+    (two, one, back1), sums = call((2, 1, -1), sums)
+    sent = [turn(two, 2), turn(one, 1), turn(back1, -1)]
+    (three, back2), sums = call((3, -2), sums, arrived)
+    sent += [turn(three, 3), turn(back2, -2)]
+    (mine,), sums = call((0,), sums)
     mine = mine + sum(x.astype(F32) for x in sent)
     mine = (mine * (ROOT * SCALE)).reshape(NKV, NXC, QROWS, DH)
     mine = jnp.swapaxes(mine, 0, 1).reshape(NSP, QROWS, DH).astype(BF16)

time: 133 us -> 130 us (0.977)
  waiting for transfers between devices: 18.8 us -> 23.2 us
  blocking collectives: 48 us -> 43.9 us
  starting transfers between devices: 32.1 us -> 28.3 us
    ppermute x14, waiting for transfers between devices: 14.1 us -> 18.6 us  [turn(): return lax.ppermute(x, ('z', 'c'), pairs)]
    all_to_all x2, blocking collectives: 48 us -> 43.9 us  [regroup(): return lax.all_to_all(x, PLANE, split_axis=0, concat_axis=0, tiled=True)]
    ppermute x14, starting transfers between devices: 28.2 us -> 24.4 us  [turn(): return lax.ppermute(x, ('z', 'c'), pairs)]
  transfers between devices with their start and end apart: 15 -> 15, of which waited for: 6 -> 7; matrix products, arithmetic and copies ran while one was open for 0% -> 0% of each run, Pallas kernels for 15% -> 17%
where the time goes in v8:
time: 130 us; the launch traced here: 129 us
  blocking collectives  43.9 us (34%)
  Pallas kernels  32.7 us (25%)
  starting transfers between devices  28.3 us (22%)
  waiting for transfers between devices  23.2 us (18%)
    all_to_all x2, blocking collectives, regroup(): return lax.all_to_all(x, PLANE, split_axis=0, concat_axis=0, tiled=True)  43.9 us
    pallas_call x4, Pallas kernels, grads_call(): pl.pallas_call(functools.partial(grads, count, first, last, bool(arrived)...  26.7 us
    ppermute x14, starting transfers between devices, turn(): return lax.ppermute(x, ('z', 'c'), pairs)  24.4 us
    ppermute x14, waiting for transfers between devices, turn(): return lax.ppermute(x, ('z', 'c'), pairs)  18.6 us
    all_to_all x1, waiting for transfers between devices, regroup(): return lax.all_to_all(x, PLANE, split_axis=0, concat_axis=0, tiled=True)  4.61 us
    all_to_all x1, starting transfers between devices, regroup(): return lax.all_to_all(x, PLANE, split_axis=0, concat_axis=0, tiled=True)  3.85 us
  transfers between devices with their start and end apart: 15, of which 7 were waited for; matrix products, arithmetic and copies ran while one was open for 0% of the time, Pallas kernels for 17%

profile of v8, /device:TPU:1, one launch (start us, length us, event | category | flops | bytes accessed | tf_op | source)
XLA Modules:
  0.0 129.5 jit_solution(8379184564896556700)
XLA Ops:
  0.6 2.1 %pack_queries.1 = bf16[32,40,128]{2,1,0:T(8,128)(2,1)} custom-call(s32[1]{0:T(128)} %bitcast.1.b_ref, bf16[128,4096]{1,0:T(8,128)(2,1)} %q_ref.1, bf16[128,4096]{1,0:T(8,128)(2,1)} %g_ref.1, bf16[128,4096]{1,0:T(8,128)(2,1)} %o_ref.1, f32[32,128]{1,0:T(8,128)} %bitcast.9), custom_call_target="tpu_custom_call" | custom-call | flops 1000000 | bytes 1000000 | tf_op jit(solution)/shard_map/pack_queries/pallas_call | solution.py:75
  2.8 18.3 %all_to_all.15.x_ref = bf16[32,40,128]{2,1,0:T(8,128)(2,1)S(1)} all-to-all(bf16[32,40,128]{2,1,0:T(8,128)(2,1)} %pack_queries.1), channel_id=1, replica_groups=mesh['y'=4,'xh'=2,'z'=8,'xl'=2,'c'=2] {'xl','c','y','xh'}, dimensions={0} | all-to-all | bytes 655360 | tf_op jit(solution)/shard_map/all_to_all | solution.py:273
  21.1 5.7 %collective-permute-start = (bf16[33,32,128]{2,1,0:T(8,128)(2,1)S(1)}, bf16[33,32,128]{2,1,0:T(8,128)(2,1)S(1)}, u32[]{:S(2)}, u32[]{:S(2)}) collective-permute-start(bf16[33,32,128]{2,1,0:T(8,128)(2,1)S(1)} %gather_stats.1.refs_4_.refs_12_), channel_id=1, source_target_pairs={{0,4},{1,29},{4,8},{5,1},{8,12},{9,5},{12,16},{13,9},{16,20},{17,1... | collective-permute-start | bytes 811016 | tf_op jit(solution)/shard_map/ppermute | solution.py:269
  26.8 0.0 collective-permute-start.4
  26.8 6.0 %collective-permute-done.refs_3_.refs_11_ = bf16[33,32,128]{2,1,0:T(8,128)(2,1)S(1)} collective-permute-done((bf16[33,32,128]{2,1,0:T(8,128)(2,1)S(1)}, bf16[33,32,128]{2,1,0:T(8,128)(2,1)S(1)}, u32[]{:S(2)}, u32[]{:S(2)}) %collective-permute-start) | collective-permute-done | bytes 270368 | tf_op jit(solution)/shard_map/ppermute | solution.py:269
  32.7 3.4 %collective-permute-start.1 = (bf16[33,32,128]{2,1,0:T(8,128)(2,1)S(1)}, bf16[33,32,128]{2,1,0:T(8,128)(2,1)S(1)}, u32[]{:S(2)}, u32[]{:S(2)}) collective-permute-start(bf16[33,32,128]{2,1,0:T(8,128)(2,1)S(1)} %collective-permute-done.refs_3_.refs_11_), channel_id=1, source_target_pairs={{0,4},{1,29},{4,8},{5,1},{8,12},{9,5},{12,16},{13,9},{16,20},{17,1... | collective-permute-start | bytes 811016 | tf_op jit(solution)/shard_map/ppermute | solution.py:269
  36.1 2.4 %pack_keys.1 = bf16[32,128,128]{2,1,0:T(8,128)(2,1)} custom-call(bf16[64,4096]{1,0:T(8,128)(2,1)} %k_ref.1, bf16[64,4096]{1,0:T(8,128)(2,1)} %v_ref.1), custom_call_target="tpu_custom_call" | custom-call | flops 1000000 | bytes 2000000 | tf_op jit(solution)/shard_map/pack_keys/pallas_call | solution.py:113
  38.5 0.0 copy-start.2
  38.5 0.0 copy-start
  38.5 0.0 copy-start.1
  38.5 3.8 %all-to-all-start.1 = ((bf16[32,128,128]{2,1,0:T(8,128)(2,1)}), bf16[32,128,128]{2,1,0:T(8,128)(2,1)S(1)}, u32[]{:S(2)}, u32[]{:S(2)}) async-start(bf16[32,128,128]{2,1,0:T(8,128)(2,1)} %pack_keys.1), calls=%async_computation.1 | async-start | bytes 2097152 | tf_op jit(solution)/shard_map/all_to_all | solution.py:273
  42.4 0.0 collective-permute-done.4.refs_5_.refs_13_
  42.4 0.1 collective-permute-start.5
  42.5 0.0 collective-permute-done.1.refs_2_.refs_10_
  42.5 2.7 %collective-permute-start.2 = (bf16[33,32,128]{2,1,0:T(8,128)(2,1)S(1)}, bf16[33,32,128]{2,1,0:T(8,128)(2,1)S(1)}, u32[]{:S(2)}, u32[]{:S(2)}) collective-permute-start(bf16[33,32,128]{2,1,0:T(8,128)(2,1)S(1)} %collective-permute-done.1.refs_2_.refs_10_), channel_id=1, source_target_pairs={{0,4},{1,29},{4,8},{5,1},{8,12},{9,5},{12,16},{13,9},{16,20},{17,1... | collective-permute-start | bytes 811016 | tf_op jit(solution)/shard_map/ppermute | solution.py:269
  45.1 0.0 copy-done.2
  45.1 0.0 copy-done
  45.2 0.0 copy-done.1
  45.2 5.8 %collective-permute-done.5.refs_6_.refs_14_ = bf16[33,32,128]{2,1,0:T(8,128)(2,1)S(1)} collective-permute-done((bf16[33,32,128]{2,1,0:T(8,128)(2,1)S(1)}, bf16[33,32,128]{2,1,0:T(8,128)(2,1)S(1)}, u32[]{:S(2)}, u32[]{:S(2)}) %collective-permute-start.5) | collective-permute-done | bytes 270368 | tf_op jit(solution)/shard_map/ppermute | solution.py:269
  51.0 0.0 collective-permute-start.6
  51.0 0.0 collective-permute-done.2.refs_1_.refs_9_
  51.0 2.7 %collective-permute-start.3 = (bf16[33,32,128]{2,1,0:T(8,128)(2,1)S(1)}, bf16[33,32,128]{2,1,0:T(8,128)(2,1)S(1)}, u32[]{:S(2)}, u32[]{:S(2)}) collective-permute-start(bf16[33,32,128]{2,1,0:T(8,128)(2,1)S(1)} %collective-permute-done.2.refs_1_.refs_9_), channel_id=1, source_target_pairs={{0,4},{1,29},{4,8},{5,1},{8,12},{9,5},{12,16},{13,9},{16,20},{17,1... | collective-permute-start | bytes 811016 | tf_op jit(solution)/shard_map/ppermute | solution.py:269
  53.7 0.1 pad_add_fusion.2.tab
  53.7 0.1 pad_add_fusion.3
  53.8 4.6 %all-to-all-done.1.refs_16_ = bf16[32,128,128]{2,1,0:T(8,128)(2,1)S(1)} async-done(((bf16[32,128,128]{2,1,0:T(8,128)(2,1)}), bf16[32,128,128]{2,1,0:T(8,128)(2,1)S(1)}, u32[]{:S(2)}, u32[]{:S(2)}) %all-to-all-start.1) | async-done | bytes 1048608 | tf_op jit(solution)/shard_map/all_to_all | solution.py:273
  58.4 0.2 collective-permute-done.6.refs_7_.refs_15_
  58.6 0.7 collective-permute-done.3.refs_0_.refs_8_
  59.4 6.7 %grads.4 = (bf16[8,64,128]{2,1,0:T(8,128)(2,1)S(1)}, bf16[8,64,128]{2,1,0:T(8,128)(2,1)S(1)}, f32[2048,128]{1,0:T(8,128)S(1)}, f32[2048,128]{1,0:T(8,128)S(1)}) custom-call(s32[10]{0:T(128)S(1)} %get-tuple-element.33.tab, bf16[33,32,128]{2,1,0:T(8,128)(2,1)S(1)} %collective-permute-done.3.refs_0_.refs_8_, ...), custom_call_target="tpu_custom_call" | custom-call | flops 2684354560 | bytes 4194304 | tf_op jit(solution)/shard_map/grads/pallas_call | solution.py:214
  66.1 2.3 %collective-permute-start.7 = (bf16[8,64,128]{2,1,0:T(8,128)(2,1)S(1)}, bf16[8,64,128]{2,1,0:T(8,128)(2,1)S(1)}, u32[]{:S(2)}, u32[]{:S(2)}) collective-permute-start(bf16[8,64,128]{2,1,0:T(8,128)(2,1)S(1)} %get-tuple-element.22), channel_id=1, source_target_pairs={{0,4},{1,29},{4,8},{5,1},{8,12},{9,5},{12,16},{13,9},{16,20},{17,1... | collective-permute-start | bytes 393224 | tf_op jit(solution)/shard_map/ppermute | solution.py:269
  68.4 0.0 collective-permute-start.8
  68.4 9.8 %grads.5 = (bf16[8,64,128]{2,1,0:T(8,128)(2,1)S(1)}, bf16[8,64,128]{2,1,0:T(8,128)(2,1)S(1)}, bf16[8,64,128]{2,1,0:T(8,128)(2,1)S(1)}, f32[2048,128]{1,0:T(8,128)S(1)}, f32[2048,128]{1,0:T(8,128)S(1)}) custom-call(s32[11]{0:T(128)S(1)} %pad_add_fusion.2.tab, bf16[33,32,128]{2,1,0:T(8,128)(2,1)S(1)} %collective-permute-done.3.refs_0_.refs_8_, ...), custom_call_target="tpu_custom_call" | custom-call | flops 4026531840 | bytes 4194304 | tf_op jit(solution)/shard_map/grads/pallas_call | solution.py:214
  78.2 1.5 %collective-permute-start.9 = (bf16[8,64,128]{2,1,0:T(8,128)(2,1)S(1)}, bf16[8,64,128]{2,1,0:T(8,128)(2,1)S(1)}, u32[]{:S(2)}, u32[]{:S(2)}) collective-permute-start(bf16[8,64,128]{2,1,0:T(8,128)(2,1)S(1)} %get-tuple-element.28), channel_id=1, source_target_pairs={{0,8},{1,25},{4,12},{5,29},{8,16},{9,1},{12,20},{13,5},{16,24},{17... | collective-permute-start | bytes 393224 | tf_op jit(solution)/shard_map/ppermute | solution.py:269
  79.7 1.3 %collective-permute-start.10 = (bf16[8,64,128]{2,1,0:T(8,128)(2,1)S(1)}, bf16[8,64,128]{2,1,0:T(8,128)(2,1)S(1)}, u32[]{:S(2)}, u32[]{:S(2)}) collective-permute-start(bf16[8,64,128]{2,1,0:T(8,128)(2,1)S(1)} %get-tuple-element.29), channel_id=1, source_target_pairs={{0,4},{1,29},{4,8},{5,1},{8,12},{9,5},{12,16},{13,9},{16,20},{17,1... | collective-permute-start | bytes 393224 | tf_op jit(solution)/shard_map/ppermute | solution.py:269
  81.0 1.1 collective-permute-start.11
  82.1 0.0 collective-permute-done.7.refs_19_
  82.1 0.0 collective-permute-done.8.refs_20_
  82.1 6.8 %grads.6 = (bf16[8,64,128]{2,1,0:T(8,128)(2,1)S(1)}, bf16[8,64,128]{2,1,0:T(8,128)(2,1)S(1)}, f32[2048,128]{1,0:T(8,128)S(1)}, f32[2048,128]{1,0:T(8,128)S(1)}) custom-call(s32[10]{0:T(128)S(1)} %get-tuple-element.34.tab, bf16[33,32,128]{2,1,0:T(8,128)(2,1)S(1)} %collective-permute-done.3.refs_0_.refs_8_, ...), custom_call_target="tpu_custom_call" | custom-call | flops 2684354560 | bytes 4194304 | tf_op jit(solution)/shard_map/grads/pallas_call | solution.py:214
  88.9 3.6 %collective-permute-start.12 = (bf16[8,64,128]{2,1,0:T(8,128)(2,1)S(1)}, bf16[8,64,128]{2,1,0:T(8,128)(2,1)S(1)}, u32[]{:S(2)}, u32[]{:S(2)}) collective-permute-start(bf16[8,64,128]{2,1,0:T(8,128)(2,1)S(1)} %get-tuple-element.31), channel_id=1, source_target_pairs={{0,12},{1,21},{4,16},{5,25},{8,20},{9,29},{12,24},{13,1},{16,28},{... | collective-permute-start | bytes 393224 | tf_op jit(solution)/shard_map/ppermute | solution.py:269
  92.5 0.2 collective-permute-start.13
  92.6 0.1 pad_add_fusion.tab
  92.7 3.5 %grads.7 = (f32[8,64,128]{2,1,0:T(8,128)S(1)}, bf16[32,144,128]{2,1,0:T(8,128)(2,1)S(1)}) custom-call(s32[9]{0:T(128)S(1)} %pad_add_fusion.tab, bf16[33,32,128]{2,1,0:T(8,128)(2,1)S(1)} %collective-permute-done.3.refs_0_.refs_8_, bf16[33,32,128]{2,1,0:T(8,128)(2,1)S(1)} %collective-permute-done.2.refs_1_.refs_9_, ...), custom_call_target="tpu_custom_call" | custom-call | flops 1342177280 | bytes 4194304 | tf_op jit(solution)/shard_map/grads/pallas_call | solution.py:214
  96.2 0.0 collective-permute-done.9
  96.2 0.0 collective-permute-done.10
  96.2 0.0 collective-permute-done.11
  96.2 1.0 collective-permute-done.12
  97.2 4.9 %collective-permute-done.13 = bf16[8,64,128]{2,1,0:T(8,128)(2,1)S(1)} collective-permute-done((bf16[8,64,128]{2,1,0:T(8,128)(2,1)S(1)}, bf16[8,64,128]{2,1,0:T(8,128)(2,1)S(1)}, u32[]{:S(2)}, u32[]{:S(2)}) %collective-permute-start.13) | collective-permute-done | bytes 131104 | tf_op jit(solution)/shard_map/ppermute | solution.py:269
  102.0 0.1 multiply_convert_fusion
  102.2 25.6 %all_to_all.16.x_ref = bf16[32,144,128]{2,1,0:T(8,128)(2,1)S(1)} all-to-all(bf16[32,144,128]{2,1,0:T(8,128)(2,1)S(1)} %constant_dynamic-update-slice_fusion), channel_id=1, replica_groups=mesh['y'=4,'xh'=2,'z'=8,'xl'=2,'c'=2] {'xl','c','y','xh'}, dimensions={0} | all-to-all | bytes 2359296 | tf_op jit(solution)/shard_map/all_to_all | solution.py:273
  127.9 1.5 %unpack.1 = (f32[16,4096]{1,0:T(8,128)}, f32[64,4096]{1,0:T(8,128)}, f32[64,4096]{1,0:T(8,128)}) custom-call(bf16[32,144,128]{2,1,0:T(8,128)(2,1)S(1)} %all_to_all.16.x_ref), custom_call_target="tpu_custom_call" | custom-call | flops 1000000 | bytes 3000000 | tf_op jit(solution)/shard_map/unpack/pallas_call | solution.py:251
  (6 shorter events, 0.1 us)
Async XLA Ops:
  21.1 11.6 %collective-permute-start = (bf16[33,32,128]{2,1,0:T(8,128)(2,1)S(1)}, bf16[33,32,128]{2,1,0:T(8,128)(2,1)S(1)}, u32[]{:S(2)}, u32[]{:S(2)}) collective-permute-start(bf16[33,32,128]{2,1,0:T(8,128)(2,1)S(1)} %gather_stats.1.refs_4_.refs_12_), channel_id=1, source_target_pairs={{0,4},{1,29},{4,8},{5,1},{8,12},{9,5},{12,16},{13,9},{16,20},{17,1... | collective-permute-start | bytes 811016 | tf_op jit(solution)/shard_map/ppermute | solution.py:269
  26.8 15.6 %collective-permute-start.4 = (bf16[33,32,128]{2,1,0:T(8,128)(2,1)S(1)}, bf16[33,32,128]{2,1,0:T(8,128)(2,1)S(1)}, u32[]{:S(2)}, u32[]{:S(2)}) collective-permute-start(bf16[33,32,128]{2,1,0:T(8,128)(2,1)S(1)} %gather_stats.1.refs_4_.refs_12_), channel_id=1, source_target_pairs={{0,28},{1,5},{4,0},{5,9},{8,4},{9,13},{12,8},{13,17},{16,12},{17,2... | collective-permute-start | bytes 811016 | tf_op jit(solution)/shard_map/ppermute | solution.py:269
  32.7 9.7 %collective-permute-start.1 = (bf16[33,32,128]{2,1,0:T(8,128)(2,1)S(1)}, bf16[33,32,128]{2,1,0:T(8,128)(2,1)S(1)}, u32[]{:S(2)}, u32[]{:S(2)}) collective-permute-start(bf16[33,32,128]{2,1,0:T(8,128)(2,1)S(1)} %collective-permute-done.refs_3_.refs_11_), channel_id=1, source_target_pairs={{0,4},{1,29},{4,8},{5,1},{8,12},{9,5},{12,16},{13,9},{16,20},{17,1... | collective-permute-start | bytes 811016 | tf_op jit(solution)/shard_map/ppermute | solution.py:269
  38.5 6.6 %copy-start.2 = (s32[3]{0:T(128)S(1)}, s32[3]{0:T(128)}, u32[]{:S(2)}) copy-start(s32[3]{0:T(128)} %constant.90.clone) | copy-start | bytes 40
  38.5 6.7 %copy-start = (s32[2]{0:T(128)S(1)}, s32[2]{0:T(128)}, u32[]{:S(2)}) copy-start(s32[2]{0:T(128)} %constant.91.clone) | copy-start | bytes 28
  38.5 6.7 %copy-start.1 = (s32[2]{0:T(128)S(1)}, s32[2]{0:T(128)}, u32[]{:S(2)}) copy-start(s32[2]{0:T(128)} %constant.89.clone) | copy-start | bytes 28
  38.5 19.9 %all-to-all-start.1 = ((bf16[32,128,128]{2,1,0:T(8,128)(2,1)}), bf16[32,128,128]{2,1,0:T(8,128)(2,1)S(1)}, u32[]{:S(2)}, u32[]{:S(2)}) async-start(bf16[32,128,128]{2,1,0:T(8,128)(2,1)} %pack_keys.1), calls=%async_computation.1 | async-start | bytes 2097152 | tf_op jit(solution)/shard_map/all_to_all | solution.py:273
  42.4 8.6 %collective-permute-start.5 = (bf16[33,32,128]{2,1,0:T(8,128)(2,1)S(1)}, bf16[33,32,128]{2,1,0:T(8,128)(2,1)S(1)}, u32[]{:S(2)}, u32[]{:S(2)}) collective-permute-start(bf16[33,32,128]{2,1,0:T(8,128)(2,1)S(1)} %collective-permute-done.4.refs_5_.refs_13_), channel_id=1, source_target_pairs={{0,28},{1,5},{4,0},{5,9},{8,4},{9,13},{12,8},{13,17},{16,12},{17,2... | collective-permute-start | bytes 811016 | tf_op jit(solution)/shard_map/ppermute | solution.py:269
  42.5 8.5 %collective-permute-start.2 = (bf16[33,32,128]{2,1,0:T(8,128)(2,1)S(1)}, bf16[33,32,128]{2,1,0:T(8,128)(2,1)S(1)}, u32[]{:S(2)}, u32[]{:S(2)}) collective-permute-start(bf16[33,32,128]{2,1,0:T(8,128)(2,1)S(1)} %collective-permute-done.1.refs_2_.refs_10_), channel_id=1, source_target_pairs={{0,4},{1,29},{4,8},{5,1},{8,12},{9,5},{12,16},{13,9},{16,20},{17,1... | collective-permute-start | bytes 811016 | tf_op jit(solution)/shard_map/ppermute | solution.py:269
  51.0 7.7 %collective-permute-start.6 = (bf16[33,32,128]{2,1,0:T(8,128)(2,1)S(1)}, bf16[33,32,128]{2,1,0:T(8,128)(2,1)S(1)}, u32[]{:S(2)}, u32[]{:S(2)}) collective-permute-start(bf16[33,32,128]{2,1,0:T(8,128)(2,1)S(1)} %collective-permute-done.5.refs_6_.refs_14_), channel_id=1, source_target_pairs={{0,28},{1,5},{4,0},{5,9},{8,4},{9,13},{12,8},{13,17},{16,12},{17,2... | collective-permute-start | bytes 811016 | tf_op jit(solution)/shard_map/ppermute | solution.py:269
  51.0 8.4 %collective-permute-start.3 = (bf16[33,32,128]{2,1,0:T(8,128)(2,1)S(1)}, bf16[33,32,128]{2,1,0:T(8,128)(2,1)S(1)}, u32[]{:S(2)}, u32[]{:S(2)}) collective-permute-start(bf16[33,32,128]{2,1,0:T(8,128)(2,1)S(1)} %collective-permute-done.2.refs_1_.refs_9_), channel_id=1, source_target_pairs={{0,4},{1,29},{4,8},{5,1},{8,12},{9,5},{12,16},{13,9},{16,20},{17,1... | collective-permute-start | bytes 811016 | tf_op jit(solution)/shard_map/ppermute | solution.py:269
  66.1 16.0 %collective-permute-start.7 = (bf16[8,64,128]{2,1,0:T(8,128)(2,1)S(1)}, bf16[8,64,128]{2,1,0:T(8,128)(2,1)S(1)}, u32[]{:S(2)}, u32[]{:S(2)}) collective-permute-start(bf16[8,64,128]{2,1,0:T(8,128)(2,1)S(1)} %get-tuple-element.22), channel_id=1, source_target_pairs={{0,4},{1,29},{4,8},{5,1},{8,12},{9,5},{12,16},{13,9},{16,20},{17,1... | collective-permute-start | bytes 393224 | tf_op jit(solution)/shard_map/ppermute | solution.py:269
  68.4 13.7 %collective-permute-start.8 = (bf16[8,64,128]{2,1,0:T(8,128)(2,1)S(1)}, bf16[8,64,128]{2,1,0:T(8,128)(2,1)S(1)}, u32[]{:S(2)}, u32[]{:S(2)}) collective-permute-start(bf16[8,64,128]{2,1,0:T(8,128)(2,1)S(1)} %get-tuple-element.23), channel_id=1, source_target_pairs={{0,28},{1,5},{4,0},{5,9},{8,4},{9,13},{12,8},{13,17},{16,12},{17,2... | collective-permute-start | bytes 393224 | tf_op jit(solution)/shard_map/ppermute | solution.py:269
  78.2 18.0 %collective-permute-start.9 = (bf16[8,64,128]{2,1,0:T(8,128)(2,1)S(1)}, bf16[8,64,128]{2,1,0:T(8,128)(2,1)S(1)}, u32[]{:S(2)}, u32[]{:S(2)}) collective-permute-start(bf16[8,64,128]{2,1,0:T(8,128)(2,1)S(1)} %get-tuple-element.28), channel_id=1, source_target_pairs={{0,8},{1,25},{4,12},{5,29},{8,16},{9,1},{12,20},{13,5},{16,24},{17... | collective-permute-start | bytes 393224 | tf_op jit(solution)/shard_map/ppermute | solution.py:269
  79.7 16.5 %collective-permute-start.10 = (bf16[8,64,128]{2,1,0:T(8,128)(2,1)S(1)}, bf16[8,64,128]{2,1,0:T(8,128)(2,1)S(1)}, u32[]{:S(2)}, u32[]{:S(2)}) collective-permute-start(bf16[8,64,128]{2,1,0:T(8,128)(2,1)S(1)} %get-tuple-element.29), channel_id=1, source_target_pairs={{0,4},{1,29},{4,8},{5,1},{8,12},{9,5},{12,16},{13,9},{16,20},{17,1... | collective-permute-start | bytes 393224 | tf_op jit(solution)/shard_map/ppermute | solution.py:269
  81.0 15.2 %collective-permute-start.11 = (bf16[8,64,128]{2,1,0:T(8,128)(2,1)S(1)}, bf16[8,64,128]{2,1,0:T(8,128)(2,1)S(1)}, u32[]{:S(2)}, u32[]{:S(2)}) collective-permute-start(bf16[8,64,128]{2,1,0:T(8,128)(2,1)S(1)} %get-tuple-element.30), channel_id=1, source_target_pairs={{0,28},{1,5},{4,0},{5,9},{8,4},{9,13},{12,8},{13,17},{16,12},{17,2... | collective-permute-start | bytes 393224 | tf_op jit(solution)/shard_map/ppermute | solution.py:269
  88.9 8.3 %collective-permute-start.12 = (bf16[8,64,128]{2,1,0:T(8,128)(2,1)S(1)}, bf16[8,64,128]{2,1,0:T(8,128)(2,1)S(1)}, u32[]{:S(2)}, u32[]{:S(2)}) collective-permute-start(bf16[8,64,128]{2,1,0:T(8,128)(2,1)S(1)} %get-tuple-element.31), channel_id=1, source_target_pairs={{0,12},{1,21},{4,16},{5,25},{8,20},{9,29},{12,24},{13,1},{16,28},{... | collective-permute-start | bytes 393224 | tf_op jit(solution)/shard_map/ppermute | solution.py:269
  92.5 9.6 %collective-permute-start.13 = (bf16[8,64,128]{2,1,0:T(8,128)(2,1)S(1)}, bf16[8,64,128]{2,1,0:T(8,128)(2,1)S(1)}, u32[]{:S(2)}, u32[]{:S(2)}) collective-permute-start(bf16[8,64,128]{2,1,0:T(8,128)(2,1)S(1)} %get-tuple-element.32), channel_id=1, source_target_pairs={{0,24},{1,9},{4,28},{5,13},{8,0},{9,17},{12,4},{13,21},{16,8},{17,... | collective-permute-start | bytes 393224 | tf_op jit(solution)/shard_map/ppermute | solution.py:269

commit v9 on v8

--- a/solution.py
+++ b/solution.py
@@ -174,10 +174,10 @@
         def _(n=n, dq_ref=dq_ref):
             for j in range(NZ):
                 at = tab[count + j]
-                part = total[j]
+                part = total[j].reshape(NXC, QROWS, DH)
                 if added:
-                    part = part + arrived[n][at].astype(F32)
-                dq_ref[at] = part.astype(dq_ref.dtype)
+                    part = part + arrived[n][:, at].astype(F32)
+                dq_ref[:, at] = part.astype(dq_ref.dtype)
 
     if last:
         out_ref = rest[count]
@@ -200,9 +200,9 @@
     tile = pl.BlockSpec((1, 8, DH), lambda i, t: (NSP, t[i] // 2, 0))
     in_specs = [part] * NZ + [tile] * NZ
     in_specs.append(pl.BlockSpec((NSP, 2 * KROWS, DH), lambda i, t: (0, 0, 0)))
-    dq = pl.BlockSpec((NZ, PART, DH), lambda i, t: (0, 0, 0))
+    dq = pl.BlockSpec((NXC, NZ, QROWS, DH), lambda i, t: (0, 0, 0, 0))
     out_specs = [dq] * count
-    out_shape = [jax.ShapeDtypeStruct((NZ, PART, DH), F32 if last else BF16)] * count
+    out_shape = [jax.ShapeDtypeStruct((NXC, NZ, QROWS, DH), F32 if last else BF16)] * count
     scratch = []
     if last:
         out_specs.append(pl.BlockSpec((NSP, OUT_ROWS, DH), lambda i, t: (0, 0, 0)))
@@ -307,8 +307,7 @@
     sent += [turn(three, 3), turn(back2, -2)]
     (mine,), sums = call((0,), sums)
     mine = mine + sum(x.astype(F32) for x in sent)
-    mine = (mine * (ROOT * SCALE)).reshape(NKV, NXC, QROWS, DH)
-    mine = jnp.swapaxes(mine, 0, 1).reshape(NSP, QROWS, DH).astype(BF16)
+    mine = (mine * (ROOT * SCALE)).astype(BF16).reshape(NSP, QROWS, DH)
     packed = lax.dynamic_update_slice(sums[0], mine, (0, 2 * KROWS, 0))
     packed = regroup(packed)
     return unpacked(packed)

time: 130 us -> 130 us (level)
  no operation moved by 1% of the time
where the time goes in v9:
time: 130 us; the launch traced here: 129 us
  blocking collectives  43.9 us (34%)
  Pallas kernels  32.7 us (25%)
  starting transfers between devices  28.3 us (22%)
  waiting for transfers between devices  23.2 us (18%)
    all_to_all x2, blocking collectives, regroup(): return lax.all_to_all(x, PLANE, split_axis=0, concat_axis=0, tiled=True)  43.9 us
    pallas_call x4, Pallas kernels, grads_call(): pl.pallas_call(functools.partial(grads, count, first, last, bool(arrived)...  26.7 us
    ppermute x14, starting transfers between devices, turn(): return lax.ppermute(x, ('z', 'c'), pairs)  24.4 us
    ppermute x14, waiting for transfers between devices, turn(): return lax.ppermute(x, ('z', 'c'), pairs)  18.6 us
    all_to_all x1, waiting for transfers between devices, regroup(): return lax.all_to_all(x, PLANE, split_axis=0, concat_axis=0, tiled=True)  4.61 us
    all_to_all x1, starting transfers between devices, regroup(): return lax.all_to_all(x, PLANE, split_axis=0, concat_axis=0, tiled=True)  3.85 us
  transfers between devices with their start and end apart: 15, of which 7 were waited for; matrix products, arithmetic and copies ran while one was open for 0% of the time, Pallas kernels for 17%

profile of v9, /device:TPU:1, one launch (start us, length us, event | category | flops | bytes accessed | tf_op | source)
XLA Modules:
  0.0 129.5 jit_solution(7684178062391409727)
XLA Ops:
  0.6 2.1 %pack_queries.1 = bf16[32,40,128]{2,1,0:T(8,128)(2,1)} custom-call(s32[1]{0:T(128)} %bitcast.1.b_ref, bf16[128,4096]{1,0:T(8,128)(2,1)} %q_ref.1, bf16[128,4096]{1,0:T(8,128)(2,1)} %g_ref.1, bf16[128,4096]{1,0:T(8,128)(2,1)} %o_ref.1, f32[32,128]{1,0:T(8,128)} %bitcast.5), custom_call_target="tpu_custom_call" | custom-call | flops 1000000 | bytes 1000000 | tf_op jit(solution)/shard_map/pack_queries/pallas_call | solution.py:75
  2.8 18.3 %all_to_all.15.x_ref = bf16[32,40,128]{2,1,0:T(8,128)(2,1)S(1)} all-to-all(bf16[32,40,128]{2,1,0:T(8,128)(2,1)} %pack_queries.1), channel_id=1, replica_groups=mesh['y'=4,'xh'=2,'z'=8,'xl'=2,'c'=2] {'xl','c','y','xh'}, dimensions={0} | all-to-all | bytes 655360 | tf_op jit(solution)/shard_map/all_to_all | solution.py:273
  21.1 5.7 %collective-permute-start = (bf16[33,32,128]{2,1,0:T(8,128)(2,1)S(1)}, bf16[33,32,128]{2,1,0:T(8,128)(2,1)S(1)}, u32[]{:S(2)}, u32[]{:S(2)}) collective-permute-start(bf16[33,32,128]{2,1,0:T(8,128)(2,1)S(1)} %gather_stats.1.refs_4_.refs_12_), channel_id=1, source_target_pairs={{0,4},{1,29},{4,8},{5,1},{8,12},{9,5},{12,16},{13,9},{16,20},{17,1... | collective-permute-start | bytes 811016 | tf_op jit(solution)/shard_map/ppermute | solution.py:269
  26.8 0.0 collective-permute-start.4
  26.8 6.0 %collective-permute-done.refs_3_.refs_11_ = bf16[33,32,128]{2,1,0:T(8,128)(2,1)S(1)} collective-permute-done((bf16[33,32,128]{2,1,0:T(8,128)(2,1)S(1)}, bf16[33,32,128]{2,1,0:T(8,128)(2,1)S(1)}, u32[]{:S(2)}, u32[]{:S(2)}) %collective-permute-start) | collective-permute-done | bytes 270368 | tf_op jit(solution)/shard_map/ppermute | solution.py:269
  32.7 3.4 %collective-permute-start.1 = (bf16[33,32,128]{2,1,0:T(8,128)(2,1)S(1)}, bf16[33,32,128]{2,1,0:T(8,128)(2,1)S(1)}, u32[]{:S(2)}, u32[]{:S(2)}) collective-permute-start(bf16[33,32,128]{2,1,0:T(8,128)(2,1)S(1)} %collective-permute-done.refs_3_.refs_11_), channel_id=1, source_target_pairs={{0,4},{1,29},{4,8},{5,1},{8,12},{9,5},{12,16},{13,9},{16,20},{17,1... | collective-permute-start | bytes 811016 | tf_op jit(solution)/shard_map/ppermute | solution.py:269
  36.1 2.4 %pack_keys.1 = bf16[32,128,128]{2,1,0:T(8,128)(2,1)} custom-call(bf16[64,4096]{1,0:T(8,128)(2,1)} %k_ref.1, bf16[64,4096]{1,0:T(8,128)(2,1)} %v_ref.1), custom_call_target="tpu_custom_call" | custom-call | flops 1000000 | bytes 2000000 | tf_op jit(solution)/shard_map/pack_keys/pallas_call | solution.py:113
  38.5 0.0 copy-start.2
  38.5 0.0 copy-start
  38.5 0.0 copy-start.1
  38.5 3.8 %all-to-all-start.1 = ((bf16[32,128,128]{2,1,0:T(8,128)(2,1)}), bf16[32,128,128]{2,1,0:T(8,128)(2,1)S(1)}, u32[]{:S(2)}, u32[]{:S(2)}) async-start(bf16[32,128,128]{2,1,0:T(8,128)(2,1)} %pack_keys.1), calls=%async_computation.1 | async-start | bytes 2097152 | tf_op jit(solution)/shard_map/all_to_all | solution.py:273
  42.4 0.0 collective-permute-done.4.refs_5_.refs_13_
  42.4 0.1 collective-permute-start.5
  42.5 0.0 collective-permute-done.1.refs_2_.refs_10_
  42.5 2.7 %collective-permute-start.2 = (bf16[33,32,128]{2,1,0:T(8,128)(2,1)S(1)}, bf16[33,32,128]{2,1,0:T(8,128)(2,1)S(1)}, u32[]{:S(2)}, u32[]{:S(2)}) collective-permute-start(bf16[33,32,128]{2,1,0:T(8,128)(2,1)S(1)} %collective-permute-done.1.refs_2_.refs_10_), channel_id=1, source_target_pairs={{0,4},{1,29},{4,8},{5,1},{8,12},{9,5},{12,16},{13,9},{16,20},{17,1... | collective-permute-start | bytes 811016 | tf_op jit(solution)/shard_map/ppermute | solution.py:269
  45.1 0.0 copy-done.2
  45.1 0.0 copy-done
  45.2 0.0 copy-done.1
  45.2 5.8 %collective-permute-done.5.refs_6_.refs_14_ = bf16[33,32,128]{2,1,0:T(8,128)(2,1)S(1)} collective-permute-done((bf16[33,32,128]{2,1,0:T(8,128)(2,1)S(1)}, bf16[33,32,128]{2,1,0:T(8,128)(2,1)S(1)}, u32[]{:S(2)}, u32[]{:S(2)}) %collective-permute-start.5) | collective-permute-done | bytes 270368 | tf_op jit(solution)/shard_map/ppermute | solution.py:269
  51.0 0.0 collective-permute-start.6
  51.0 0.0 collective-permute-done.2.refs_1_.refs_9_
  51.0 2.7 %collective-permute-start.3 = (bf16[33,32,128]{2,1,0:T(8,128)(2,1)S(1)}, bf16[33,32,128]{2,1,0:T(8,128)(2,1)S(1)}, u32[]{:S(2)}, u32[]{:S(2)}) collective-permute-start(bf16[33,32,128]{2,1,0:T(8,128)(2,1)S(1)} %collective-permute-done.2.refs_1_.refs_9_), channel_id=1, source_target_pairs={{0,4},{1,29},{4,8},{5,1},{8,12},{9,5},{12,16},{13,9},{16,20},{17,1... | collective-permute-start | bytes 811016 | tf_op jit(solution)/shard_map/ppermute | solution.py:269
  53.7 0.1 pad_add_fusion.2.tab
  53.7 0.1 pad_add_fusion.3
  53.8 4.6 %all-to-all-done.1.refs_16_ = bf16[32,128,128]{2,1,0:T(8,128)(2,1)S(1)} async-done(((bf16[32,128,128]{2,1,0:T(8,128)(2,1)}), bf16[32,128,128]{2,1,0:T(8,128)(2,1)S(1)}, u32[]{:S(2)}, u32[]{:S(2)}) %all-to-all-start.1) | async-done | bytes 1048608 | tf_op jit(solution)/shard_map/all_to_all | solution.py:273
  58.4 0.2 collective-permute-done.6.refs_7_.refs_15_
  58.6 0.7 collective-permute-done.3.refs_0_.refs_8_
  59.4 6.7 %grads.4 = (bf16[4,8,16,128]{3,2,1,0:T(8,128)(2,1)S(1)}, bf16[4,8,16,128]{3,2,1,0:T(8,128)(2,1)S(1)}, f32[2048,128]{1,0:T(8,128)S(1)}, f32[2048,128]{1,0:T(8,128)S(1)}) custom-call(s32[10]{0:T(128)S(1)} %get-tuple-element.33.tab, bf16[33,32,128]{2,1,0:T(8,128)(2,1)S(1)} %collective-permute-done.3.refs_0_.refs_8_, ...), custom_call_target="tpu_custom_call" | custom-call | flops 2684354560 | bytes 4194304 | tf_op jit(solution)/shard_map/grads/pallas_call | solution.py:214
  66.1 2.3 %collective-permute-start.7 = (bf16[4,8,16,128]{3,2,1,0:T(8,128)(2,1)S(1)}, bf16[4,8,16,128]{3,2,1,0:T(8,128)(2,1)S(1)}, u32[]{:S(2)}, u32[]{:S(2)}) collective-permute-start(bf16[4,8,16,128]{3,2,1,0:T(8,128)(2,1)S(1)} %get-tuple-element.22), channel_id=1, source_target_pairs={{0,4},{1,29},{4,8},{5,1},{8,12},{9,5},{12,16},{13,9},{16,20},{17,1... | collective-permute-start | bytes 393224 | tf_op jit(solution)/shard_map/ppermute | solution.py:269
  68.4 0.0 collective-permute-start.8
  68.4 9.8 %grads.5 = (bf16[4,8,16,128]{3,2,1,0:T(8,128)(2,1)S(1)}, bf16[4,8,16,128]{3,2,1,0:T(8,128)(2,1)S(1)}, bf16[4,8,16,128]{3,2,1,0:T(8,128)(2,1)S(1)}, f32[2048,128]{1,0:T(8,128)S(1)}, f32[2048,128]{1,0:T(8,128)S(1)}) custom-call(s32[11]{0:T(128)S(1)} %pad_add_fusion.2.tab, bf16[33,32,128]{2,1,0:T(8,128)(2,1)S(1)} %collective-permute-done.3.refs_0_.refs_8_, ...), custom_call_target="tpu_custom_call" | custom-call | flops 4026531840 | bytes 4194304 | tf_op jit(solution)/shard_map/grads/pallas_call | solution.py:214
  78.2 1.5 %collective-permute-start.9 = (bf16[4,8,16,128]{3,2,1,0:T(8,128)(2,1)S(1)}, bf16[4,8,16,128]{3,2,1,0:T(8,128)(2,1)S(1)}, u32[]{:S(2)}, u32[]{:S(2)}) collective-permute-start(bf16[4,8,16,128]{3,2,1,0:T(8,128)(2,1)S(1)} %get-tuple-element.28), channel_id=1, source_target_pairs={{0,8},{1,25},{4,12},{5,29},{8,16},{9,1},{12,20},{13,5},{16,24},{17... | collective-permute-start | bytes 393224 | tf_op jit(solution)/shard_map/ppermute | solution.py:269
  79.7 1.3 %collective-permute-start.10 = (bf16[4,8,16,128]{3,2,1,0:T(8,128)(2,1)S(1)}, bf16[4,8,16,128]{3,2,1,0:T(8,128)(2,1)S(1)}, u32[]{:S(2)}, u32[]{:S(2)}) collective-permute-start(bf16[4,8,16,128]{3,2,1,0:T(8,128)(2,1)S(1)} %get-tuple-element.29), channel_id=1, source_target_pairs={{0,4},{1,29},{4,8},{5,1},{8,12},{9,5},{12,16},{13,9},{16,20},{17,1... | collective-permute-start | bytes 393224 | tf_op jit(solution)/shard_map/ppermute | solution.py:269
  81.0 1.1 collective-permute-start.11
  82.1 0.0 collective-permute-done.7.refs_19_
  82.1 0.0 collective-permute-done.8.refs_20_
  82.1 6.8 %grads.6 = (bf16[4,8,16,128]{3,2,1,0:T(8,128)(2,1)S(1)}, bf16[4,8,16,128]{3,2,1,0:T(8,128)(2,1)S(1)}, f32[2048,128]{1,0:T(8,128)S(1)}, f32[2048,128]{1,0:T(8,128)S(1)}) custom-call(s32[10]{0:T(128)S(1)} %get-tuple-element.34.tab, bf16[33,32,128]{2,1,0:T(8,128)(2,1)S(1)} %collective-permute-done.3.refs_0_.refs_8_, ...), custom_call_target="tpu_custom_call" | custom-call | flops 2684354560 | bytes 4194304 | tf_op jit(solution)/shard_map/grads/pallas_call | solution.py:214
  88.9 3.6 %collective-permute-start.12 = (bf16[4,8,16,128]{3,2,1,0:T(8,128)(2,1)S(1)}, bf16[4,8,16,128]{3,2,1,0:T(8,128)(2,1)S(1)}, u32[]{:S(2)}, u32[]{:S(2)}) collective-permute-start(bf16[4,8,16,128]{3,2,1,0:T(8,128)(2,1)S(1)} %get-tuple-element.31), channel_id=1, source_target_pairs={{0,12},{1,21},{4,16},{5,25},{8,20},{9,29},{12,24},{13,1},{16,28},{... | collective-permute-start | bytes 393224 | tf_op jit(solution)/shard_map/ppermute | solution.py:269
  92.5 0.2 collective-permute-start.13
  92.6 0.1 pad_add_fusion.tab
  92.7 3.5 %grads.7 = (f32[4,8,16,128]{3,2,1,0:T(8,128)S(1)}, bf16[32,144,128]{2,1,0:T(8,128)(2,1)S(1)}) custom-call(s32[9]{0:T(128)S(1)} %pad_add_fusion.tab, bf16[33,32,128]{2,1,0:T(8,128)(2,1)S(1)} %collective-permute-done.3.refs_0_.refs_8_, bf16[33,32,128]{2,1,0:T(8,128)(2,1)S(1)} %collective-permute-done.2.refs_1_.refs_9_, ...), custom_call_target="tpu_custom_call" | custom-call | flops 1342177280 | bytes 4194304 | tf_op jit(solution)/shard_map/grads/pallas_call | solution.py:214
  96.2 0.0 collective-permute-done.9
  96.2 0.0 collective-permute-done.10
  96.2 0.0 collective-permute-done.11
  96.2 1.0 collective-permute-done.12
  97.2 4.9 %collective-permute-done.13 = bf16[4,8,16,128]{3,2,1,0:T(8,128)(2,1)S(1)} collective-permute-done((bf16[4,8,16,128]{3,2,1,0:T(8,128)(2,1)S(1)}, bf16[4,8,16,128]{3,2,1,0:T(8,128)(2,1)S(1)}, u32[]{:S(2)}, u32[]{:S(2)}) %collective-permute-start.13) | collective-permute-done | bytes 131104 | tf_op jit(solution)/shard_map/ppermute | solution.py:269
  102.0 0.1 multiply_convert_fusion
  102.2 25.6 %all_to_all.16.x_ref = bf16[32,144,128]{2,1,0:T(8,128)(2,1)S(1)} all-to-all(bf16[32,144,128]{2,1,0:T(8,128)(2,1)S(1)} %constant_dynamic-update-slice_fusion), channel_id=1, replica_groups=mesh['y'=4,'xh'=2,'z'=8,'xl'=2,'c'=2] {'xl','c','y','xh'}, dimensions={0} | all-to-all | bytes 2359296 | tf_op jit(solution)/shard_map/all_to_all | solution.py:273
  127.8 1.5 %unpack.1 = (f32[16,4096]{1,0:T(8,128)}, f32[64,4096]{1,0:T(8,128)}, f32[64,4096]{1,0:T(8,128)}) custom-call(bf16[32,144,128]{2,1,0:T(8,128)(2,1)S(1)} %all_to_all.16.x_ref), custom_call_target="tpu_custom_call" | custom-call | flops 1000000 | bytes 3000000 | tf_op jit(solution)/shard_map/unpack/pallas_call | solution.py:251
  (5 shorter events, 0.1 us)
Async XLA Ops:
  21.1 11.6 %collective-permute-start = (bf16[33,32,128]{2,1,0:T(8,128)(2,1)S(1)}, bf16[33,32,128]{2,1,0:T(8,128)(2,1)S(1)}, u32[]{:S(2)}, u32[]{:S(2)}) collective-permute-start(bf16[33,32,128]{2,1,0:T(8,128)(2,1)S(1)} %gather_stats.1.refs_4_.refs_12_), channel_id=1, source_target_pairs={{0,4},{1,29},{4,8},{5,1},{8,12},{9,5},{12,16},{13,9},{16,20},{17,1... | collective-permute-start | bytes 811016 | tf_op jit(solution)/shard_map/ppermute | solution.py:269
  26.8 15.6 %collective-permute-start.4 = (bf16[33,32,128]{2,1,0:T(8,128)(2,1)S(1)}, bf16[33,32,128]{2,1,0:T(8,128)(2,1)S(1)}, u32[]{:S(2)}, u32[]{:S(2)}) collective-permute-start(bf16[33,32,128]{2,1,0:T(8,128)(2,1)S(1)} %gather_stats.1.refs_4_.refs_12_), channel_id=1, source_target_pairs={{0,28},{1,5},{4,0},{5,9},{8,4},{9,13},{12,8},{13,17},{16,12},{17,2... | collective-permute-start | bytes 811016 | tf_op jit(solution)/shard_map/ppermute | solution.py:269
  32.7 9.7 %collective-permute-start.1 = (bf16[33,32,128]{2,1,0:T(8,128)(2,1)S(1)}, bf16[33,32,128]{2,1,0:T(8,128)(2,1)S(1)}, u32[]{:S(2)}, u32[]{:S(2)}) collective-permute-start(bf16[33,32,128]{2,1,0:T(8,128)(2,1)S(1)} %collective-permute-done.refs_3_.refs_11_), channel_id=1, source_target_pairs={{0,4},{1,29},{4,8},{5,1},{8,12},{9,5},{12,16},{13,9},{16,20},{17,1... | collective-permute-start | bytes 811016 | tf_op jit(solution)/shard_map/ppermute | solution.py:269
  38.5 6.6 %copy-start.2 = (s32[3]{0:T(128)S(1)}, s32[3]{0:T(128)}, u32[]{:S(2)}) copy-start(s32[3]{0:T(128)} %constant.90.clone) | copy-start | bytes 40
  38.5 6.7 %copy-start = (s32[2]{0:T(128)S(1)}, s32[2]{0:T(128)}, u32[]{:S(2)}) copy-start(s32[2]{0:T(128)} %constant.91.clone) | copy-start | bytes 28
  38.5 6.7 %copy-start.1 = (s32[2]{0:T(128)S(1)}, s32[2]{0:T(128)}, u32[]{:S(2)}) copy-start(s32[2]{0:T(128)} %constant.89.clone) | copy-start | bytes 28
  38.5 19.9 %all-to-all-start.1 = ((bf16[32,128,128]{2,1,0:T(8,128)(2,1)}), bf16[32,128,128]{2,1,0:T(8,128)(2,1)S(1)}, u32[]{:S(2)}, u32[]{:S(2)}) async-start(bf16[32,128,128]{2,1,0:T(8,128)(2,1)} %pack_keys.1), calls=%async_computation.1 | async-start | bytes 2097152 | tf_op jit(solution)/shard_map/all_to_all | solution.py:273
  42.4 8.6 %collective-permute-start.5 = (bf16[33,32,128]{2,1,0:T(8,128)(2,1)S(1)}, bf16[33,32,128]{2,1,0:T(8,128)(2,1)S(1)}, u32[]{:S(2)}, u32[]{:S(2)}) collective-permute-start(bf16[33,32,128]{2,1,0:T(8,128)(2,1)S(1)} %collective-permute-done.4.refs_5_.refs_13_), channel_id=1, source_target_pairs={{0,28},{1,5},{4,0},{5,9},{8,4},{9,13},{12,8},{13,17},{16,12},{17,2... | collective-permute-start | bytes 811016 | tf_op jit(solution)/shard_map/ppermute | solution.py:269
  42.5 8.5 %collective-permute-start.2 = (bf16[33,32,128]{2,1,0:T(8,128)(2,1)S(1)}, bf16[33,32,128]{2,1,0:T(8,128)(2,1)S(1)}, u32[]{:S(2)}, u32[]{:S(2)}) collective-permute-start(bf16[33,32,128]{2,1,0:T(8,128)(2,1)S(1)} %collective-permute-done.1.refs_2_.refs_10_), channel_id=1, source_target_pairs={{0,4},{1,29},{4,8},{5,1},{8,12},{9,5},{12,16},{13,9},{16,20},{17,1... | collective-permute-start | bytes 811016 | tf_op jit(solution)/shard_map/ppermute | solution.py:269
  51.0 7.7 %collective-permute-start.6 = (bf16[33,32,128]{2,1,0:T(8,128)(2,1)S(1)}, bf16[33,32,128]{2,1,0:T(8,128)(2,1)S(1)}, u32[]{:S(2)}, u32[]{:S(2)}) collective-permute-start(bf16[33,32,128]{2,1,0:T(8,128)(2,1)S(1)} %collective-permute-done.5.refs_6_.refs_14_), channel_id=1, source_target_pairs={{0,28},{1,5},{4,0},{5,9},{8,4},{9,13},{12,8},{13,17},{16,12},{17,2... | collective-permute-start | bytes 811016 | tf_op jit(solution)/shard_map/ppermute | solution.py:269
  51.0 8.4 %collective-permute-start.3 = (bf16[33,32,128]{2,1,0:T(8,128)(2,1)S(1)}, bf16[33,32,128]{2,1,0:T(8,128)(2,1)S(1)}, u32[]{:S(2)}, u32[]{:S(2)}) collective-permute-start(bf16[33,32,128]{2,1,0:T(8,128)(2,1)S(1)} %collective-permute-done.2.refs_1_.refs_9_), channel_id=1, source_target_pairs={{0,4},{1,29},{4,8},{5,1},{8,12},{9,5},{12,16},{13,9},{16,20},{17,1... | collective-permute-start | bytes 811016 | tf_op jit(solution)/shard_map/ppermute | solution.py:269
  66.1 16.0 %collective-permute-start.7 = (bf16[4,8,16,128]{3,2,1,0:T(8,128)(2,1)S(1)}, bf16[4,8,16,128]{3,2,1,0:T(8,128)(2,1)S(1)}, u32[]{:S(2)}, u32[]{:S(2)}) collective-permute-start(bf16[4,8,16,128]{3,2,1,0:T(8,128)(2,1)S(1)} %get-tuple-element.22), channel_id=1, source_target_pairs={{0,4},{1,29},{4,8},{5,1},{8,12},{9,5},{12,16},{13,9},{16,20},{17,1... | collective-permute-start | bytes 393224 | tf_op jit(solution)/shard_map/ppermute | solution.py:269
  68.4 13.7 %collective-permute-start.8 = (bf16[4,8,16,128]{3,2,1,0:T(8,128)(2,1)S(1)}, bf16[4,8,16,128]{3,2,1,0:T(8,128)(2,1)S(1)}, u32[]{:S(2)}, u32[]{:S(2)}) collective-permute-start(bf16[4,8,16,128]{3,2,1,0:T(8,128)(2,1)S(1)} %get-tuple-element.23), channel_id=1, source_target_pairs={{0,28},{1,5},{4,0},{5,9},{8,4},{9,13},{12,8},{13,17},{16,12},{17,2... | collective-permute-start | bytes 393224 | tf_op jit(solution)/shard_map/ppermute | solution.py:269
  78.2 18.0 %collective-permute-start.9 = (bf16[4,8,16,128]{3,2,1,0:T(8,128)(2,1)S(1)}, bf16[4,8,16,128]{3,2,1,0:T(8,128)(2,1)S(1)}, u32[]{:S(2)}, u32[]{:S(2)}) collective-permute-start(bf16[4,8,16,128]{3,2,1,0:T(8,128)(2,1)S(1)} %get-tuple-element.28), channel_id=1, source_target_pairs={{0,8},{1,25},{4,12},{5,29},{8,16},{9,1},{12,20},{13,5},{16,24},{17... | collective-permute-start | bytes 393224 | tf_op jit(solution)/shard_map/ppermute | solution.py:269
  79.7 16.5 %collective-permute-start.10 = (bf16[4,8,16,128]{3,2,1,0:T(8,128)(2,1)S(1)}, bf16[4,8,16,128]{3,2,1,0:T(8,128)(2,1)S(1)}, u32[]{:S(2)}, u32[]{:S(2)}) collective-permute-start(bf16[4,8,16,128]{3,2,1,0:T(8,128)(2,1)S(1)} %get-tuple-element.29), channel_id=1, source_target_pairs={{0,4},{1,29},{4,8},{5,1},{8,12},{9,5},{12,16},{13,9},{16,20},{17,1... | collective-permute-start | bytes 393224 | tf_op jit(solution)/shard_map/ppermute | solution.py:269
  81.0 15.2 %collective-permute-start.11 = (bf16[4,8,16,128]{3,2,1,0:T(8,128)(2,1)S(1)}, bf16[4,8,16,128]{3,2,1,0:T(8,128)(2,1)S(1)}, u32[]{:S(2)}, u32[]{:S(2)}) collective-permute-start(bf16[4,8,16,128]{3,2,1,0:T(8,128)(2,1)S(1)} %get-tuple-element.30), channel_id=1, source_target_pairs={{0,28},{1,5},{4,0},{5,9},{8,4},{9,13},{12,8},{13,17},{16,12},{17,2... | collective-permute-start | bytes 393224 | tf_op jit(solution)/shard_map/ppermute | solution.py:269
  88.9 8.3 %collective-permute-start.12 = (bf16[4,8,16,128]{3,2,1,0:T(8,128)(2,1)S(1)}, bf16[4,8,16,128]{3,2,1,0:T(8,128)(2,1)S(1)}, u32[]{:S(2)}, u32[]{:S(2)}) collective-permute-start(bf16[4,8,16,128]{3,2,1,0:T(8,128)(2,1)S(1)} %get-tuple-element.31), channel_id=1, source_target_pairs={{0,12},{1,21},{4,16},{5,25},{8,20},{9,29},{12,24},{13,1},{16,28},{... | collective-permute-start | bytes 393224 | tf_op jit(solution)/shard_map/ppermute | solution.py:269
  92.5 9.6 %collective-permute-start.13 = (bf16[4,8,16,128]{3,2,1,0:T(8,128)(2,1)S(1)}, bf16[4,8,16,128]{3,2,1,0:T(8,128)(2,1)S(1)}, u32[]{:S(2)}, u32[]{:S(2)}) collective-permute-start(bf16[4,8,16,128]{3,2,1,0:T(8,128)(2,1)S(1)} %get-tuple-element.32), channel_id=1, source_target_pairs={{0,24},{1,9},{4,28},{5,13},{8,0},{9,17},{12,4},{13,21},{16,8},{17,... | collective-permute-start | bytes 393224 | tf_op jit(solution)/shard_map/ppermute | solution.py:269
